TPU v7x, 256 devices: a whole 4x4x8 slice. The times are simulated.
256 devices in a mesh: dom: 32 (over z, x_hi, core), frame: 8 (over x_lo, y).
Axes of the slice: x: 4 (x_hi: 2, x_lo: 2; x = x_hi * 2 + x_lo), y: 4, z: 8, core: 2. Of those that a mesh axis runs over, the one named last changes fastest.
Arguments:
- features: bfloat16 [4096, 512], P('dom'), may hold values from -6 to 6
- positions: bfloat16 [3, 4096], P(None, 'dom'), may hold values from 0 to 4
- neighbours: int32 [4096, 128], P('dom'), may hold values from 0 to 255, as said below
- counts: int32 [4096], P('dom'), may hold values from 1 to 128, as said below
- send_rows: int32 [32, 2, 64], P('dom'), may hold values from 0 to 127
- frames: float32 [8, 3, 3], P('frame')
- w_edge: float32 [9, 512], replicated, may hold values from -2 to 2
- b_edge: float32 [512], replicated, may hold values from -4 to 4
- w_message: bfloat16 [512, 512], replicated, may hold values from -0.25 to 0.25
- w_update: bfloat16 [512, 512], replicated, may hold values from -0.25 to 0.25
- w_readout: bfloat16 [512, 512], replicated, may hold values from -0.25 to 0.25
- w_heads: bfloat16 [512, 4], replicated, may hold values from -0.25 to 0.25
Outputs:
- predictions: float32 [4, 4096], P(None, 'dom')
Inputs may be any that keep to these rules, and one draw needn't show every extreme that they name: `counts`: each domain has its own largest count, one of 32, 64, 96 or 128, reached by one of its atoms; some domain reaches 128. `neighbours`: order a domain's table as the 64 rows from the domain below, its own 128 atoms, then the 64 rows from the domain above; every slot of an atom in aligned block b of 16 atoms of its domain names a row at positions (b * 128) // max(7, 1) to that plus 128 - 1 of this order.
All inputs are finite; a program needn't handle non-finite values.
Results may differ from a plain program's by a relative error of at most 0.0049.
Values may be sent and summed in bfloat16 or wider, within the bound.
No kernel may reach another device: no remote copies, remote signals or barrier semaphores. Data moves between devices by JAX's collectives and lax.ppermute only.
A program may use at most 64 MiB of HBM per device.

v0:
```python
import jax
import jax.numpy as jnp
from jax import lax
from jax.sharding import PartitionSpec as P

WINDOW = 128


message_scale = 0.0884
radial_step = 1.25
block_atoms = 16


def padded(cells, sides, width):
    for axis, dim in sides:
        count = lax.axis_size(axis)
        head = lax.slice_in_dim(cells, 0, width, axis=dim)
        tail = lax.slice_in_dim(cells, cells.shape[dim] - width, cells.shape[dim], axis=dim)
        cells = jnp.concatenate(
            [
                lax.ppermute(tail, axis, [(i, (i + 1) % count) for i in range(count)]),
                cells,
                lax.ppermute(head, axis, [((i + 1) % count, i) for i in range(count)]),
            ],
            axis=dim,
        )
    return cells


def from_everyone(array, axis):
    copies = jnp.broadcast_to(array, (lax.axis_size(axis), *array.shape))
    return lax.all_to_all(copies, axis, split_axis=0, concat_axis=0, tiled=True)


def taken_together(array, axis):
    everything = from_everyone(array, axis)
    return jnp.sum(everything, axis=0)


def edge_messages(rows_feat, rows_pos, centre_pos, live_mask, rotation, w_edge, b_edge):
    relative = rows_pos - centre_pos[:, None, :]
    frame_vec = jnp.einsum("bkc,ac->bka", relative, rotation, precision=lax.Precision.HIGHEST)
    distance = jnp.sqrt(jnp.sum(relative * relative, axis=-1) + 0.25)
    centres = jnp.arange(w_edge.shape[0] - 3, dtype=jnp.float32) * radial_step
    radial = jnp.exp(-((distance[..., None] - centres) ** 2))
    edge_in = jnp.concatenate([radial, frame_vec], axis=-1)
    preact = jnp.einsum("bki,iw->bkw", edge_in, w_edge, precision=lax.Precision.HIGHEST) + b_edge
    edge_gate = jax.nn.silu(preact) * live_mask[..., None]
    return jnp.sum(edge_gate * rows_feat, axis=1) * message_scale


def fetch_rows(local_rows, window_feat, window_pos):
    picker = (local_rows[..., None] == lax.broadcasted_iota(jnp.int32, (1, 1, WINDOW), 2)).astype(
        jnp.bfloat16
    )
    flat_pick = picker.reshape(-1, WINDOW)
    got_feat = jnp.dot(flat_pick, window_feat, preferred_element_type=jnp.float32)
    got_pos = jnp.dot(flat_pick, window_pos, preferred_element_type=jnp.float32)
    shape_rows = local_rows.shape
    return (
        got_feat.reshape(shape_rows + (window_feat.shape[1],)),
        got_pos.reshape(shape_rows + (3,)),
    )


def local(
    features,
    positions,
    neighbours,
    counts,
    send_rows,
    frames,
    w_edge,
    b_edge,
    w_message,
    w_update,
    w_readout,
    w_heads,
):
    local_atoms = features.shape[0]
    feature_width = features.shape[1]
    slot_total = neighbours.shape[1]
    frame_count = lax.axis_size("frame")
    cap_rows = send_rows.shape[2]
    rows_pos = positions.T
    chosen = send_rows[0]
    chosen = chosen.reshape(-1)
    padded_feat, padded_pos = (
        padded(features[chosen], (("dom", 0),), cap_rows),
        padded(rows_pos[chosen], (("dom", 0),), cap_rows),
    )
    ghost_feat = jnp.concatenate([padded_feat[:cap_rows], padded_feat[-cap_rows:]], axis=0)
    ghost_pos = jnp.concatenate([padded_pos[:cap_rows], padded_pos[-cap_rows:]], axis=0)
    ordered_feat = jnp.concatenate([ghost_feat[:cap_rows], features, ghost_feat[cap_rows:]], axis=0)
    ordered_pos = jnp.concatenate([ghost_pos[:cap_rows], rows_pos, ghost_pos[cap_rows:]], axis=0)
    table_rows = ordered_feat.shape[0]
    block_total = local_atoms // block_atoms
    span_rows = table_rows - WINDOW
    denom = max(block_total - 1, 1)
    placed = jnp.where(
        neighbours < local_atoms,
        neighbours + cap_rows,
        jnp.where(neighbours < local_atoms + cap_rows, neighbours - local_atoms, neighbours),
    )
    block_ids = jnp.arange(block_total, dtype=jnp.int32)
    block_starts = block_ids * span_rows // denom
    rotation = frames[0]
    coords = rows_pos.astype(jnp.float32)
    block_inputs = (
        placed.reshape(-1, block_atoms, slot_total),
        counts.reshape(-1, block_atoms),
        coords.reshape(-1, block_atoms, 3),
        block_starts,
    )

    def one_block(block_in):
        block_idx, block_count, block_centre, block_start = block_in
        window_feat = lax.dynamic_slice_in_dim(ordered_feat, block_start, WINDOW, 0)
        window_pos = lax.dynamic_slice_in_dim(ordered_pos, block_start, WINDOW, 0)
        local_rows = block_idx - block_start
        slot_place = lax.broadcasted_iota(jnp.int32, block_idx.shape, 1)
        live_mask = (slot_place < block_count[:, None]).astype(jnp.float32)
        got_feat, got_pos = fetch_rows(local_rows, window_feat, window_pos)
        return edge_messages(got_feat, got_pos, block_centre, live_mask, rotation, w_edge, b_edge)

    message = (
        lax.map(one_block, block_inputs).reshape(local_atoms, feature_width).astype(jnp.bfloat16)
    )
    hidden = jax.nn.silu(jnp.dot(message, w_message, preferred_element_type=jnp.float32)).astype(
        jnp.bfloat16
    )
    updated = (
        features.astype(jnp.float32) + jnp.dot(hidden, w_update, preferred_element_type=jnp.float32)
    ).astype(jnp.bfloat16)
    readout = jax.nn.silu(jnp.dot(updated, w_readout, preferred_element_type=jnp.float32)).astype(
        jnp.bfloat16
    )
    heads = jnp.dot(readout, w_heads, preferred_element_type=jnp.float32)
    force_can = jnp.einsum("na,ac->cn", heads[:, :3], rotation, precision=lax.Precision.HIGHEST)
    frame_term = jnp.concatenate([force_can, heads[:, 3][None, :]], axis=0)
    return taken_together(frame_term, "frame") / frame_count


def solution(mesh):
    placed = (
        P("dom", None),
        P(None, "dom"),
        P("dom", None),
        P("dom"),
        P("dom", None, None),
        P("frame", None, None),
        P(),
        P(),
        P(),
        P(),
        P(),
        P(),
    )
    return jax.shard_map(
        local, mesh=mesh, in_specs=placed, out_specs=P(None, "dom"), check_vma=False
    )
```

profile of v0, /device:TPU:2, one launch (start us, length us, event | category | flops | bytes accessed | tf_op | source)
XLA Modules:
  0.0 135.5 jit_solution(346088870993158607)
XLA Ops:
  0.0 0.9 copy.30
  0.9 0.8 reshape_squeeze.3
  1.6 0.7 gather_fusion
  2.5 6.9 %collective-permute-start.1 = (bf16[64,3]{1,0:T(8,128)(2,1)S(1)}, bf16[64,3]{1,0:T(8,128)(2,1)S(1)}, u32[]{:S(2)}, u32[]{:S(2)}) collective-permute-start(bf16[64,3]{1,0:T(8,128)(2,1)S(1)} %get-tuple-element.134), channel_id=1, source_target_pairs={{8,0},{16,8},{24,16},{32,24},{40,32},{48,40},{56,48},{64,56},{72,6... | collective-permute-start | bytes 1160 | tf_op jit(solution)/shard_map/ppermute | solution.py:23
  9.4 1.8 %gather_fusion.1 = bf16[128,512]{1,0:T(8,128)(2,1)S(1)} fusion(bf16[128,512]{1,0:T(8,128)(2,1)} %param.14, s32[1024]{0:T(1024)S(1)} %pad_clamp_fusion), kind=kCustom, calls=%fused_computation.1 | custom fusion | bytes 262656 | tf_op jit(solution)/shard_map/gather | solution.py:89
  11.3 5.3 %collective-permute-start.3 = (bf16[64,512]{1,0:T(8,128)(2,1)S(1)}, bf16[64,512]{1,0:T(8,128)(2,1)S(1)}, u32[]{:S(2)}, u32[]{:S(2)}) collective-permute-start(bf16[64,512]{1,0:T(8,128)(2,1)S(1)} %get-tuple-element.132), channel_id=1, source_target_pairs={{8,0},{16,8},{24,16},{32,24},{40,32},{48,40},{56,48},{64,56},{72,6... | collective-permute-start | bytes 196616 | tf_op jit(solution)/shard_map/ppermute | solution.py:23
  16.8 0.9 fusion.22
  17.7 0.7 reshape.119
  18.5 0.7 copy.40
  19.4 0.9 pad_maximum_fusion
  20.4 102.8 %while.10 = (s32[]{:T(128)}, bf16[8,16,512]{2,1,0:T(8,128)(2,1)S(1)}, s32[8,16,128]{2,1,0:T(8,128)S(1)}, s32[8]{0:T(128)S(1)}, bf16[256,3]{0,1:T(4,128)(2,1)S(1)...) while((s32[]{:T(128)}, ...), condition=%wide.region_3.4_spmd, body=%wide.region_0.3_spmd.sunk | while | flops 392468480 | bytes 9009435 | solution.py:127
  20.4 0.6 dynamic_slice.48
  22.7 0.6 subtract_bitcast_fusion.2
  23.3 2.5 %fusion.52 = f32[16,128,512]{2,1,0:T(8,128)} fusion(s32[16,128]{1,0:T(8,128)S(1)} %subtract_bitcast_fusion.2, bf16[256,512]{1,0:T(8,128)(2,1)S(1)} %get-tuple-element.244, s32[]{:T(128)S(6)} %select_n.40), kind=kOutput, calls=%fused_computation.5.clone.1 | convolution fusion | flops 268697600 | bytes 4333572 | tf_op jit(solution)/shard_map/while/body/eval_jaxpr/dot_general | solution.py:57
  25.9 0.5 multiply_reduce_fusion.4
  26.8 6.5 %multiply_reduce_fusion.5 = f32[16,512]{1,0:T(8,128)S(1)} fusion(f32[16,128,512]{2,1,0:T(8,128)} %fusion.52, f32[16,128]{1,0:T(8,128)S(1)} %fusion.54, f32[512]{0:T(512)S(1)} %copy-done.7, f32[16,128,3]{1,2,0:T(4,128)S(1)} %fusion.55, f32[16,128,6]{1,2,0:T(8,128)S(1)} %negate_exponential_fusion.2, f32[9,512]{1,0:T(8,128)S(1)} %copy-done.6), kind=kOutput, calls=%fused_computation.2.clone.1 | convolution fusion | flops 121645056 | bytes 4329472 | tf_op jit(solution)/shard_map/while/body/eval_jaxpr/bki,iw->bkw/dot_general | solution.py:47
  33.3 0.6 dynamic_slice.48
  35.6 0.6 subtract_bitcast_fusion.2
  36.1 2.5 %fusion.52 = f32[16,128,512]{2,1,0:T(8,128)} fusion(s32[16,128]{1,0:T(8,128)S(1)} %subtract_bitcast_fusion.2, bf16[256,512]{1,0:T(8,128)(2,1)S(1)} %get-tuple-element.244, s32[]{:T(128)S(6)} %select_n.40), kind=kOutput, calls=%fused_computation.5.clone.1 | convolution fusion | flops 268697600 | bytes 4333572 | tf_op jit(solution)/shard_map/while/body/eval_jaxpr/dot_general | solution.py:57
  39.6 6.5 %multiply_reduce_fusion.5 = f32[16,512]{1,0:T(8,128)S(1)} fusion(f32[16,128,512]{2,1,0:T(8,128)} %fusion.52, f32[16,128]{1,0:T(8,128)S(1)} %fusion.54, f32[512]{0:T(512)S(1)} %copy-done.7, f32[16,128,3]{1,2,0:T(4,128)S(1)} %fusion.55, f32[16,128,6]{1,2,0:T(8,128)S(1)} %negate_exponential_fusion.2, f32[9,512]{1,0:T(8,128)S(1)} %copy-done.6), kind=kOutput, calls=%fused_computation.2.clone.1 | convolution fusion | flops 121645056 | bytes 4329472 | tf_op jit(solution)/shard_map/while/body/eval_jaxpr/bki,iw->bkw/dot_general | solution.py:47
  46.1 0.6 dynamic_slice.48
  48.4 0.6 subtract_bitcast_fusion.2
  49.0 2.5 %fusion.52 = f32[16,128,512]{2,1,0:T(8,128)} fusion(s32[16,128]{1,0:T(8,128)S(1)} %subtract_bitcast_fusion.2, bf16[256,512]{1,0:T(8,128)(2,1)S(1)} %get-tuple-element.244, s32[]{:T(128)S(6)} %select_n.40), kind=kOutput, calls=%fused_computation.5.clone.1 | convolution fusion | flops 268697600 | bytes 4333572 | tf_op jit(solution)/shard_map/while/body/eval_jaxpr/dot_general | solution.py:57
  52.4 6.5 %multiply_reduce_fusion.5 = f32[16,512]{1,0:T(8,128)S(1)} fusion(f32[16,128,512]{2,1,0:T(8,128)} %fusion.52, f32[16,128]{1,0:T(8,128)S(1)} %fusion.54, f32[512]{0:T(512)S(1)} %copy-done.7, f32[16,128,3]{1,2,0:T(4,128)S(1)} %fusion.55, f32[16,128,6]{1,2,0:T(8,128)S(1)} %negate_exponential_fusion.2, f32[9,512]{1,0:T(8,128)S(1)} %copy-done.6), kind=kOutput, calls=%fused_computation.2.clone.1 | convolution fusion | flops 121645056 | bytes 4329472 | tf_op jit(solution)/shard_map/while/body/eval_jaxpr/bki,iw->bkw/dot_general | solution.py:47
  59.0 0.6 dynamic_slice.48
  61.2 0.6 subtract_bitcast_fusion.2
  61.8 2.5 %fusion.52 = f32[16,128,512]{2,1,0:T(8,128)} fusion(s32[16,128]{1,0:T(8,128)S(1)} %subtract_bitcast_fusion.2, bf16[256,512]{1,0:T(8,128)(2,1)S(1)} %get-tuple-element.244, s32[]{:T(128)S(6)} %select_n.40), kind=kOutput, calls=%fused_computation.5.clone.1 | convolution fusion | flops 268697600 | bytes 4333572 | tf_op jit(solution)/shard_map/while/body/eval_jaxpr/dot_general | solution.py:57
  64.4 0.5 multiply_reduce_fusion.4
  65.3 6.5 %multiply_reduce_fusion.5 = f32[16,512]{1,0:T(8,128)S(1)} fusion(f32[16,128,512]{2,1,0:T(8,128)} %fusion.52, f32[16,128]{1,0:T(8,128)S(1)} %fusion.54, f32[512]{0:T(512)S(1)} %copy-done.7, f32[16,128,3]{1,2,0:T(4,128)S(1)} %fusion.55, f32[16,128,6]{1,2,0:T(8,128)S(1)} %negate_exponential_fusion.2, f32[9,512]{1,0:T(8,128)S(1)} %copy-done.6), kind=kOutput, calls=%fused_computation.2.clone.1 | convolution fusion | flops 121645056 | bytes 4329472 | tf_op jit(solution)/shard_map/while/body/eval_jaxpr/bki,iw->bkw/dot_general | solution.py:47
  71.8 0.6 dynamic_slice.48
  74.1 0.6 subtract_bitcast_fusion.2
  74.7 2.5 %fusion.52 = f32[16,128,512]{2,1,0:T(8,128)} fusion(s32[16,128]{1,0:T(8,128)S(1)} %subtract_bitcast_fusion.2, bf16[256,512]{1,0:T(8,128)(2,1)S(1)} %get-tuple-element.244, s32[]{:T(128)S(6)} %select_n.40), kind=kOutput, calls=%fused_computation.5.clone.1 | convolution fusion | flops 268697600 | bytes 4333572 | tf_op jit(solution)/shard_map/while/body/eval_jaxpr/dot_general | solution.py:57
  77.2 0.5 multiply_reduce_fusion.4
  78.1 6.5 %multiply_reduce_fusion.5 = f32[16,512]{1,0:T(8,128)S(1)} fusion(f32[16,128,512]{2,1,0:T(8,128)} %fusion.52, f32[16,128]{1,0:T(8,128)S(1)} %fusion.54, f32[512]{0:T(512)S(1)} %copy-done.7, f32[16,128,3]{1,2,0:T(4,128)S(1)} %fusion.55, f32[16,128,6]{1,2,0:T(8,128)S(1)} %negate_exponential_fusion.2, f32[9,512]{1,0:T(8,128)S(1)} %copy-done.6), kind=kOutput, calls=%fused_computation.2.clone.1 | convolution fusion | flops 121645056 | bytes 4329472 | tf_op jit(solution)/shard_map/while/body/eval_jaxpr/bki,iw->bkw/dot_general | solution.py:47
  84.7 0.6 dynamic_slice.48
  86.9 0.6 subtract_bitcast_fusion.2
  87.5 2.5 %fusion.52 = f32[16,128,512]{2,1,0:T(8,128)} fusion(s32[16,128]{1,0:T(8,128)S(1)} %subtract_bitcast_fusion.2, bf16[256,512]{1,0:T(8,128)(2,1)S(1)} %get-tuple-element.244, s32[]{:T(128)S(6)} %select_n.40), kind=kOutput, calls=%fused_computation.5.clone.1 | convolution fusion | flops 268697600 | bytes 4333572 | tf_op jit(solution)/shard_map/while/body/eval_jaxpr/dot_general | solution.py:57
  91.0 6.5 %multiply_reduce_fusion.5 = f32[16,512]{1,0:T(8,128)S(1)} fusion(f32[16,128,512]{2,1,0:T(8,128)} %fusion.52, f32[16,128]{1,0:T(8,128)S(1)} %fusion.54, f32[512]{0:T(512)S(1)} %copy-done.7, f32[16,128,3]{1,2,0:T(4,128)S(1)} %fusion.55, f32[16,128,6]{1,2,0:T(8,128)S(1)} %negate_exponential_fusion.2, f32[9,512]{1,0:T(8,128)S(1)} %copy-done.6), kind=kOutput, calls=%fused_computation.2.clone.1 | convolution fusion | flops 121645056 | bytes 4329472 | tf_op jit(solution)/shard_map/while/body/eval_jaxpr/bki,iw->bkw/dot_general | solution.py:47
  97.5 0.6 dynamic_slice.48
  99.8 0.6 subtract_bitcast_fusion.2
  100.4 2.5 %fusion.52 = f32[16,128,512]{2,1,0:T(8,128)} fusion(s32[16,128]{1,0:T(8,128)S(1)} %subtract_bitcast_fusion.2, bf16[256,512]{1,0:T(8,128)(2,1)S(1)} %get-tuple-element.244, s32[]{:T(128)S(6)} %select_n.40), kind=kOutput, calls=%fused_computation.5.clone.1 | convolution fusion | flops 268697600 | bytes 4333572 | tf_op jit(solution)/shard_map/while/body/eval_jaxpr/dot_general | solution.py:57
  103.8 6.5 %multiply_reduce_fusion.5 = f32[16,512]{1,0:T(8,128)S(1)} fusion(f32[16,128,512]{2,1,0:T(8,128)} %fusion.52, f32[16,128]{1,0:T(8,128)S(1)} %fusion.54, f32[512]{0:T(512)S(1)} %copy-done.7, f32[16,128,3]{1,2,0:T(4,128)S(1)} %fusion.55, f32[16,128,6]{1,2,0:T(8,128)S(1)} %negate_exponential_fusion.2, f32[9,512]{1,0:T(8,128)S(1)} %copy-done.6), kind=kOutput, calls=%fused_computation.2.clone.1 | convolution fusion | flops 121645056 | bytes 4329472 | tf_op jit(solution)/shard_map/while/body/eval_jaxpr/bki,iw->bkw/dot_general | solution.py:47
  110.4 0.6 dynamic_slice.48
  112.6 0.6 subtract_bitcast_fusion.2
  113.2 2.5 %fusion.52 = f32[16,128,512]{2,1,0:T(8,128)} fusion(s32[16,128]{1,0:T(8,128)S(1)} %subtract_bitcast_fusion.2, bf16[256,512]{1,0:T(8,128)(2,1)S(1)} %get-tuple-element.244, s32[]{:T(128)S(6)} %select_n.40), kind=kOutput, calls=%fused_computation.5.clone.1 | convolution fusion | flops 268697600 | bytes 4333572 | tf_op jit(solution)/shard_map/while/body/eval_jaxpr/dot_general | solution.py:57
  116.7 6.5 %multiply_reduce_fusion.5 = f32[16,512]{1,0:T(8,128)S(1)} fusion(f32[16,128,512]{2,1,0:T(8,128)} %fusion.52, f32[16,128]{1,0:T(8,128)S(1)} %fusion.54, f32[512]{0:T(512)S(1)} %copy-done.7, f32[16,128,3]{1,2,0:T(4,128)S(1)} %fusion.55, f32[16,128,6]{1,2,0:T(8,128)S(1)} %negate_exponential_fusion.2, f32[9,512]{1,0:T(8,128)S(1)} %copy-done.6), kind=kOutput, calls=%fused_computation.2.clone.1 | convolution fusion | flops 121645056 | bytes 4329472 | tf_op jit(solution)/shard_map/while/body/eval_jaxpr/bki,iw->bkw/dot_general | solution.py:47
  124.3 10.5 %all_to_all.5 = f32[8,4,128]{2,1,0:T(4,128)S(1)} all-to-all(f32[8,4,128]{2,1,0:T(4,128)S(1)} %broadcast_in_dim.6), channel_id=1, replica_groups=mesh['dom'=32,'frame'=8] {'frame'}, dimensions={0} | all-to-all | bytes 32768 | tf_op jit(solution)/shard_map/all_to_all | solution.py:32
  134.9 0.6 broadcast_multiply_fusion
  (146 shorter events, 8.0 us)
Async XLA Ops:
  0.0 123.2 %copy-start = (bf16[512,512]{1,0:T(8,128)(2,1)S(1)}, bf16[512,512]{1,0:T(8,128)(2,1)}, u32[]{:S(2)}) copy-start(bf16[512,512]{1,0:T(8,128)(2,1)} %param.22) | copy-start | bytes 1572868
  2.4 16.8 %collective-permute-start = (bf16[64,3]{1,0:T(8,128)(2,1)S(1)}, bf16[64,3]{1,0:T(8,128)(2,1)S(1)}, u32[]{:S(2)}, u32[]{:S(2)}) collective-permute-start(bf16[64,3]{1,0:T(8,128)(2,1)S(1)} %get-tuple-element.133), channel_id=1, source_target_pairs={{0,8},{8,16},{16,24},{24,32},{32,40},{40,48},{48,56},{56,64},{64,7... | collective-permute-start | bytes 1160 | tf_op jit(solution)/shard_map/ppermute | solution.py:21
  2.5 16.8 %collective-permute-start.1 = (bf16[64,3]{1,0:T(8,128)(2,1)S(1)}, bf16[64,3]{1,0:T(8,128)(2,1)S(1)}, u32[]{:S(2)}, u32[]{:S(2)}) collective-permute-start(bf16[64,3]{1,0:T(8,128)(2,1)S(1)} %get-tuple-element.134), channel_id=1, source_target_pairs={{8,0},{16,8},{24,16},{32,24},{40,32},{48,40},{56,48},{64,56},{72,6... | collective-permute-start | bytes 1160 | tf_op jit(solution)/shard_map/ppermute | solution.py:23
  11.2 8.2 %collective-permute-start.2 = (bf16[64,512]{1,0:T(8,128)(2,1)S(1)}, bf16[64,512]{1,0:T(8,128)(2,1)S(1)}, u32[]{:S(2)}, u32[]{:S(2)}) collective-permute-start(bf16[64,512]{1,0:T(8,128)(2,1)S(1)} %get-tuple-element.131), channel_id=1, source_target_pairs={{0,8},{8,16},{16,24},{24,32},{32,40},{40,48},{48,56},{56,64},{64,7... | collective-permute-start | bytes 196616 | tf_op jit(solution)/shard_map/ppermute | solution.py:21
  11.3 8.1 %collective-permute-start.3 = (bf16[64,512]{1,0:T(8,128)(2,1)S(1)}, bf16[64,512]{1,0:T(8,128)(2,1)S(1)}, u32[]{:S(2)}, u32[]{:S(2)}) collective-permute-start(bf16[64,512]{1,0:T(8,128)(2,1)S(1)} %get-tuple-element.132), channel_id=1, source_target_pairs={{8,0},{16,8},{24,16},{32,24},{40,32},{48,40},{56,48},{64,56},{72,6... | collective-permute-start | bytes 196616 | tf_op jit(solution)/shard_map/ppermute | solution.py:23
  20.4 103.1 %copy-start.1 = (bf16[128,512]{1,0:T(8,128)(2,1)S(1)}, bf16[128,512]{1,0:T(8,128)(2,1)}, u32[]{:S(2)}) copy-start(bf16[128,512]{1,0:T(8,128)(2,1)} %param.14) | copy-start | bytes 393220
  20.4 103.1 %copy-start.4 = (bf16[512,512]{1,0:T(8,128)(2,1)S(1)}, bf16[512,512]{1,0:T(8,128)(2,1)}, u32[]{:S(2)}) copy-start(bf16[512,512]{1,0:T(8,128)(2,1)} %param.24) | copy-start | bytes 1572868
  20.4 103.1 %copy-start.5 = (bf16[512,512]{1,0:T(8,128)(2,1)S(1)}, bf16[512,512]{1,0:T(8,128)(2,1)}, u32[]{:S(2)}) copy-start(bf16[512,512]{1,0:T(8,128)(2,1)} %param.23) | copy-start | bytes 1572868
  20.4 6.3 %copy-start.6 = (f32[9,512]{1,0:T(8,128)S(1)}, f32[9,512]{1,0:T(8,128)}, u32[]{:S(2)}) copy-start(f32[9,512]{1,0:T(8,128)} %get-tuple-element.241) | copy-start | bytes 55300 | tf_op jit(solution)/shard_map/while
  20.4 6.3 %copy-start.7 = (f32[512]{0:T(512)S(1)}, f32[512]{0:T(512)}, u32[]{:S(2)}) copy-start(f32[512]{0:T(512)} %get-tuple-element.242) | copy-start | bytes 6148 | tf_op jit(solution)/shard_map/while
  33.3 6.3 %copy-start.6 = (f32[9,512]{1,0:T(8,128)S(1)}, f32[9,512]{1,0:T(8,128)}, u32[]{:S(2)}) copy-start(f32[9,512]{1,0:T(8,128)} %get-tuple-element.241) | copy-start | bytes 55300 | tf_op jit(solution)/shard_map/while
  33.3 6.3 %copy-start.7 = (f32[512]{0:T(512)S(1)}, f32[512]{0:T(512)}, u32[]{:S(2)}) copy-start(f32[512]{0:T(512)} %get-tuple-element.242) | copy-start | bytes 6148 | tf_op jit(solution)/shard_map/while
  46.1 6.3 %copy-start.6 = (f32[9,512]{1,0:T(8,128)S(1)}, f32[9,512]{1,0:T(8,128)}, u32[]{:S(2)}) copy-start(f32[9,512]{1,0:T(8,128)} %get-tuple-element.241) | copy-start | bytes 55300 | tf_op jit(solution)/shard_map/while
  46.1 6.3 %copy-start.7 = (f32[512]{0:T(512)S(1)}, f32[512]{0:T(512)}, u32[]{:S(2)}) copy-start(f32[512]{0:T(512)} %get-tuple-element.242) | copy-start | bytes 6148 | tf_op jit(solution)/shard_map/while
  59.0 6.3 %copy-start.6 = (f32[9,512]{1,0:T(8,128)S(1)}, f32[9,512]{1,0:T(8,128)}, u32[]{:S(2)}) copy-start(f32[9,512]{1,0:T(8,128)} %get-tuple-element.241) | copy-start | bytes 55300 | tf_op jit(solution)/shard_map/while
  59.0 6.3 %copy-start.7 = (f32[512]{0:T(512)S(1)}, f32[512]{0:T(512)}, u32[]{:S(2)}) copy-start(f32[512]{0:T(512)} %get-tuple-element.242) | copy-start | bytes 6148 | tf_op jit(solution)/shard_map/while
  71.8 6.3 %copy-start.6 = (f32[9,512]{1,0:T(8,128)S(1)}, f32[9,512]{1,0:T(8,128)}, u32[]{:S(2)}) copy-start(f32[9,512]{1,0:T(8,128)} %get-tuple-element.241) | copy-start | bytes 55300 | tf_op jit(solution)/shard_map/while
  71.8 6.3 %copy-start.7 = (f32[512]{0:T(512)S(1)}, f32[512]{0:T(512)}, u32[]{:S(2)}) copy-start(f32[512]{0:T(512)} %get-tuple-element.242) | copy-start | bytes 6148 | tf_op jit(solution)/shard_map/while
  84.7 6.3 %copy-start.6 = (f32[9,512]{1,0:T(8,128)S(1)}, f32[9,512]{1,0:T(8,128)}, u32[]{:S(2)}) copy-start(f32[9,512]{1,0:T(8,128)} %get-tuple-element.241) | copy-start | bytes 55300 | tf_op jit(solution)/shard_map/while
  84.7 6.3 %copy-start.7 = (f32[512]{0:T(512)S(1)}, f32[512]{0:T(512)}, u32[]{:S(2)}) copy-start(f32[512]{0:T(512)} %get-tuple-element.242) | copy-start | bytes 6148 | tf_op jit(solution)/shard_map/while
  97.5 6.3 %copy-start.6 = (f32[9,512]{1,0:T(8,128)S(1)}, f32[9,512]{1,0:T(8,128)}, u32[]{:S(2)}) copy-start(f32[9,512]{1,0:T(8,128)} %get-tuple-element.241) | copy-start | bytes 55300 | tf_op jit(solution)/shard_map/while
  97.5 6.3 %copy-start.7 = (f32[512]{0:T(512)S(1)}, f32[512]{0:T(512)}, u32[]{:S(2)}) copy-start(f32[512]{0:T(512)} %get-tuple-element.242) | copy-start | bytes 6148 | tf_op jit(solution)/shard_map/while
  110.3 6.3 %copy-start.6 = (f32[9,512]{1,0:T(8,128)S(1)}, f32[9,512]{1,0:T(8,128)}, u32[]{:S(2)}) copy-start(f32[9,512]{1,0:T(8,128)} %get-tuple-element.241) | copy-start | bytes 55300 | tf_op jit(solution)/shard_map/while
  110.3 6.3 %copy-start.7 = (f32[512]{0:T(512)S(1)}, f32[512]{0:T(512)}, u32[]{:S(2)}) copy-start(f32[512]{0:T(512)} %get-tuple-element.242) | copy-start | bytes 6148 | tf_op jit(solution)/shard_map/while
  123.2 0.8 copy-start.2
  123.2 0.9 copy-start.3
where the time goes:
time: 137 us; the launch traced here: 135 us
  matrix products  78 us (57%)
  loops' own time  14.2 us (10%)
  starting transfers between devices  12.4 us (9%)
  local copies, waits for them, and re-layouts  11.5 us (8%)
  blocking collectives  10.5 us (8%)
  other arithmetic  8.53 us (6%)
    dot_general x8, matrix products, edge_messages(): jnp.einsum('bki,iw->bkw', edge_in, w_edge, precision=lax.Precision.HIGHEST)  51.8 us
    dot_general x8, matrix products, fetch_rows(): jnp.dot(flat_pick, window_feat, preferred_element_type=jnp.float32)  19.9 us
    another operation x1, loops' own time, local(): lax.map(one_block, block_inputs).reshape(local_atoms, feature_width)  14.2 us
    ppermute x2, starting transfers between devices, padded(): lax.ppermute(head, axis, [((i + 1) % count, i) for i in range(count)])  12.3 us
    all_to_all x1, blocking collectives, from_everyone(): return lax.all_to_all(copies, axis, split_axis=0, concat_axis=0, tiled=True)  10.5 us
    dynamic_slice x8, local copies, waits for them, and re-layouts, local(): lax.map(one_block, block_inputs).reshape(local_atoms, feature_width)  4.66 us
    sub x8, other arithmetic, one_block(): local_rows = block_idx - block_start  4.53 us
    dot_general x8, matrix products, fetch_rows(): got_pos = jnp.dot(flat_pick, window_pos, preferred_element_type=jnp.float32)  3.73 us
  transfers between devices with their start and end apart: 4, of which 0 were waited for; matrix products, arithmetic and copies ran while one was open for 3% of the time, Pallas kernels for 0%

commit v1 on v0

v1 whole, which is shorter than its diff:
```python
import jax
import jax.numpy as jnp
from jax import lax
from jax.experimental import pallas as pl
from jax.experimental.pallas import tpu as pltpu
from jax.sharding import PartitionSpec as P

BF = jnp.bfloat16
F32 = jnp.float32
I32 = jnp.int32
message_scale = 0.0884
radial_step = 1.25

ATOMS = 128
HALF = 64
CAP = 64
TABLE = CAP + ATOMS
WIDTH = 512
SLOTS = 128
FEATS = 16
GROUP = 8
GROUPS = HALF // GROUP
EXTRA = 128
PAY = WIDTH + EXTRA
RADIAL = 6
WINDOWS = ((0, 128), (16, 160), (32, 176), (48, 192))


def iota(shape, dim):
    return lax.broadcasted_iota(I32, shape, dim)


def dot(a, b):
    return jnp.dot(a, b, preferred_element_type=F32)


def dot_t(a, b):
    return lax.dot_general(a, b, (((1,), (1,)), ((), ())), preferred_element_type=F32)


def mask(cond):
    return jnp.where(cond, 1.0, 0.0).astype(F32)


def pick(cond):
    return mask(cond).astype(BF)


def pack_kernel(feat_ref, pos_ref, rows_ref, frame_ref, out_ref):
    odd = lax.axis_index("frame") % 2
    wanted = jnp.where(odd == 1, rows_ref[0, 1:2, :], rows_ref[0, 0:1, :])
    row = iota((CAP, CAP), 0)
    source = jnp.where(odd == 1, row, CAP - 1 - row)
    column = jnp.sum(
        jnp.where(iota((CAP, CAP), 1) == source, wanted, 0).astype(F32), axis=1, keepdims=True
    ).astype(I32)
    chosen = pick(iota((CAP, ATOMS), 1) == column)
    out_ref[:, :WIDTH] = dot(chosen, feat_ref[...]).astype(BF)
    lane = iota((CAP, EXTRA), 1)
    rest = jnp.zeros((CAP, EXTRA), F32)
    for c in range(3):
        line = chosen.astype(F32) * pos_ref[c : c + 1, :].astype(F32)
        rest = jnp.where(lane == c, jnp.sum(line, axis=1, keepdims=True), rest)
    turn = jnp.zeros((CAP, EXTRA), F32)
    for a in range(3):
        for c in range(3):
            k = 8 + 3 * a + c
            turn = jnp.where((lane == k) | (lane == k + 16) | (lane == k + 32), frame_ref[a, :, c : c + 1], turn)
    high = turn.astype(BF).astype(F32)
    mid = (turn - high).astype(BF).astype(F32)
    low = (turn - high - mid).astype(BF).astype(F32)
    turn = jnp.where(lane < 24, high, jnp.where(lane < 40, mid, low))
    out_ref[:, WIDTH:] = (rest + turn).astype(BF)


def main_kernel(
    pay_ref,
    feat_ref,
    pos_ref,
    nbr_ref,
    cnt_ref,
    frame_ref,
    we_ref,
    be_ref,
    wm_ref,
    wu_ref,
    wr_ref,
    wh_ref,
    out_ref,
    table,
    edges,
    rhs,
    times,
    message,
):
    odd = lax.axis_index("frame") % 2

    def local(n):
        return jnp.where(odd == 1, ATOMS - 1 - n, n)

    own = pick(iota((ATOMS, ATOMS), 1) == local(iota((ATOMS, ATOMS), 0)))
    table[:CAP, :] = pay_ref[:, :WIDTH]
    table[CAP:, :] = dot(own, feat_ref[...]).astype(BF)

    raw = nbr_ref[...]
    order = jnp.where(raw < ATOMS, raw + CAP, jnp.where(raw < ATOMS + CAP, raw - ATOMS, raw))
    order = jnp.where(odd == 1, 2 * CAP + ATOMS - 1 - order, order)
    by_slot = order.astype(F32).T.astype(BF)
    atom = local(iota((ATOMS, ATOMS), 0))
    lane = iota((ATOMS, ATOMS), 1)
    to_low = pick(atom == lane)
    to_low = jnp.where(lane < HALF, to_low, jnp.zeros_like(to_low))
    to_high = pick(atom + HALF == lane)
    folded = dot(by_slot[: SLOTS // 2], to_low) + dot(by_slot[SLOTS // 2 :], to_high)
    cnt = jnp.broadcast_to(cnt_ref[...].astype(F32), (8, ATOMS)).astype(BF)
    live = (dot(cnt, to_low) + dot(cnt, to_high))[0:1, :]
    slot = iota((SLOTS // 2, ATOMS), 0) + jnp.where(iota((SLOTS // 2, ATOMS), 1) < HALF, 0, SLOTS // 2)
    folded = jnp.where(slot.astype(F32) < live, folded, -1.0).astype(BF)
    place = iota((TABLE, ATOMS), 0).astype(F32).astype(BF)
    total = jnp.zeros((TABLE, ATOMS), BF)
    one = jnp.ones((TABLE, ATOMS), BF)
    for k in range(SLOTS // 2):
        total = jnp.where(place == folded[k : k + 1, :], total + one, total)
    for a in range(GROUP):
        spread = pick(iota((ATOMS, ATOMS), 0) % HALF == iota((ATOMS, ATOMS), 1) * GROUP + a)
        times[a, :, :] = dot(total, spread)

    lane8 = iota((8, ATOMS), 1)
    atom8 = local(lane8)
    in_group = mask(atom8 // GROUP == iota((8, ATOMS), 0))
    spread = pick(local(iota((ATOMS, ATOMS), 0)) % GROUP == lane // FEATS)
    centre = []
    reach = []
    ones = jnp.ones((ATOMS, ATOMS), BF)
    extra = pay_ref[:, WIDTH:]
    for c in range(3):
        line = pos_ref[c : c + 1, :].astype(F32)
        centre.append(dot((in_group * line).astype(BF), spread))
        mine = dot((own.astype(F32) * line).astype(BF), ones)
        ghost = dot(extra, pick(iota((EXTRA, EXTRA), 0) == c))
        reach.append(jnp.concatenate([ghost, mine], axis=0))
    kind = iota((1, ATOMS), 1) % FEATS
    shift = kind.astype(F32) * radial_step
    for g in range(GROUPS):
        lo, hi = WINDOWS[g // 2]
        rel = [reach[c][lo:hi] - centre[c][g : g + 1, :] for c in range(3)]
        dist = jnp.sqrt(rel[0] * rel[0] + rel[1] * rel[1] + rel[2] * rel[2] + 0.25) - shift
        value = jnp.exp(-(dist * dist))
        axis = jnp.where(kind % 3 == 0, rel[0], jnp.where(kind % 3 == 1, rel[1], rel[2]))
        axis_high = axis.astype(BF).astype(F32)
        axis = jnp.where((kind >= 9) & (kind < 12), axis - axis_high, axis_high)
        value = jnp.where(kind < RADIAL, value, jnp.where(kind < 15, axis, 1.0))
        edges[g, lo:hi, :] = value.astype(BF)

    turns = []
    for a in range(3):
        turns.append([(frame_ref[a, :, c : c + 1]) for c in range(3)])
    head = extra[0:1, :].astype(F32)
    other = []
    for a in range(3):
        other.append([])
        for c in range(3):
            k = 8 + 3 * a + c
            other[a].append(head[:, k : k + 1] + head[:, k + 16 : k + 17] + head[:, k + 32 : k + 33])
    block = iota((ATOMS, WIDTH), 0) // FEATS
    for f, rot in enumerate((turns, other)):
        vec = [
            0.5 * (rot[0][c] * we_ref[6:7, :] + rot[1][c] * we_ref[7:8, :] + rot[2][c] * we_ref[8:9, :])
            for c in range(3)
        ]
        vec = jnp.concatenate(vec, axis=0)
        vec_high = vec.astype(BF).astype(F32)
        rows = jnp.concatenate(
            [0.5 * we_ref[0:RADIAL, :], vec_high, vec_high, vec - vec_high, 0.5 * be_ref[...]], axis=0
        )
        rows = jnp.concatenate([rows] * GROUP, axis=0).astype(BF)
        for a in range(GROUP):
            rhs[a, :, f * WIDTH : (f + 1) * WIDTH] = jnp.where(block == a, rows, jnp.zeros_like(rows))

    tile = 256

    def step(a, carry):
        share = times[a].astype(BF)
        for w in range(WIDTH // tile):
            span = slice(w * tile, (w + 1) * tile)
            for g in range(GROUPS):
                lo, hi = WINDOWS[g // 2]
                weighted = table[lo:hi, span] * share[lo:hi, g : g + 1]
                for f in range(2):
                    pre = dot(edges[g, lo:hi, :], rhs[a, :, f * WIDTH + w * tile : f * WIDTH + (w + 1) * tile])
                    half = pre.astype(BF)
                    gate = half * jnp.tanh(half) + half
                    prod = gate * weighted
                    parts = [prod[r : r + 16] for r in range(0, hi - lo, 16)]
                    quads = [
                        (parts[q] + parts[q + 1]) + (parts[q + 2] + parts[q + 3])
                        for q in range(0, len(parts) - 3, 4)
                    ] + parts[len(parts) // 4 * 4 :]
                    total = quads[0].astype(F32)
                    for q in quads[1:]:
                        total = total + q.astype(F32)
                    message[a, f * GROUPS + g : f * GROUPS + g + 1, span] = jnp.sum(
                        total, axis=0, keepdims=True
                    )
        return carry

    lax.fori_loop(0, GROUP, step, 0)

    msg = (message[...].reshape(ATOMS, WIDTH) * message_scale).astype(BF)
    row = iota((ATOMS, ATOMS), 0)
    row_atom = (row % GROUPS) * GROUP + row // 16
    mine = dot(pick(lane == local(row_atom)), feat_ref[...])

    def silu(x):
        h = 0.5 * x
        return h * jnp.tanh(h) + h

    hidden = silu(dot(msg, wm_ref[...])).astype(BF)
    updated = (mine + dot(hidden, wu_ref[...])).astype(BF)
    readout = silu(dot(updated, wr_ref[...])).astype(BF)
    lane_atom = (lane % GROUPS) * GROUP + lane // 16
    total = jnp.zeros((4, ATOMS), F32)
    for f, rot in enumerate((turns, other)):
        back = pick((local(row) == lane_atom) & ((lane // GROUPS) % 2 == f))
        placed = dot(back, readout).astype(BF)
        heads = dot_t(wh_ref[...], placed)
        force = [
            rot[0][c] * heads[0:1] + rot[1][c] * heads[1:2] + rot[2][c] * heads[2:3] for c in range(3)
        ]
        total = total + jnp.concatenate(force + [heads[3:4]], axis=0)
    out_ref[...] = total


def local_step(
    features,
    positions,
    neighbours,
    counts,
    send_rows,
    frames,
    w_edge,
    b_edge,
    w_message,
    w_update,
    w_readout,
    w_heads,
):
    dom_count = lax.axis_size("dom")
    frame_count = lax.axis_size("frame")
    frame = jnp.transpose(frames, (1, 0, 2))
    payload = pl.pallas_call(
        pack_kernel,
        out_shape=jax.ShapeDtypeStruct((CAP, PAY), BF),
    )(features, positions, send_rows, frame)
    pairs = []
    for d in range(dom_count):
        for f in range(frame_count):
            to = (d + 1) % dom_count if f % 2 else (d - 1) % dom_count
            pairs.append((d * frame_count + f, to * frame_count + (f ^ 1)))
    ghosts = lax.ppermute(payload, ("dom", "frame"), pairs)
    part = pl.pallas_call(
        main_kernel,
        out_shape=jax.ShapeDtypeStruct((4, ATOMS), F32),
        scratch_shapes=[
            pltpu.VMEM((TABLE, WIDTH), BF),
            pltpu.VMEM((GROUPS, TABLE, ATOMS), BF),
            pltpu.VMEM((GROUP, ATOMS, 2 * WIDTH), BF),
            pltpu.VMEM((GROUP, TABLE, ATOMS), F32),
            pltpu.VMEM((GROUP, 2 * GROUPS, WIDTH), F32),
        ],
        compiler_params=pltpu.CompilerParams(vmem_limit_bytes=32 << 20),
    )(
        ghosts,
        features,
        positions,
        neighbours,
        counts.reshape(1, ATOMS),
        frame,
        w_edge,
        b_edge.reshape(1, WIDTH),
        w_message,
        w_update,
        w_readout,
        w_heads.T,
    )
    copies = jnp.broadcast_to(part, (frame_count, *part.shape))
    everything = lax.all_to_all(copies, "frame", split_axis=0, concat_axis=0, tiled=True)
    return jnp.sum(everything, axis=0) / frame_count


def solution(mesh):
    placed = (
        P("dom", None),
        P(None, "dom"),
        P("dom", None),
        P("dom"),
        P("dom", None, None),
        P("frame", None, None),
        P(),
        P(),
        P(),
        P(),
        P(),
        P(),
    )
    return jax.shard_map(
        local_step, mesh=mesh, in_specs=placed, out_specs=P(None, "dom"), check_vma=False
    )
```

time: 137 us -> 39.1 us (0.29)
  matrix products: 78 us -> 0 us
  loops' own time: 14.2 us -> 0 us
  Pallas kernels: 0 us -> 13.1 us
  other arithmetic: 8.53 us -> 0.6 us
  local copies, waits for them, and re-layouts: 11.5 us -> 4.55 us
  starting transfers between devices: 12.4 us -> 7.87 us
  waiting for transfers between devices: 0.02 us -> 2.38 us
    dot_general x36 -> x0, matrix products: 78 us -> none  [the longest x8 51.8 us: edge_messages(): jnp.einsum('bki,iw->bkw', edge_in, w_edge, precision=lax.Precision.HIGHEST)]
    another operation x1 -> x0, loops' own time: 14.2 us -> none  [local(): lax.map(one_block, block_inputs).reshape(local_atoms, feature_width)]
    pallas_call x0 -> x2, Pallas kernels: none -> 13.1 us  [the longest x1 11.3 us: local_step(): pl.pallas_call(main_kernel, out_shape=jax.ShapeDtypeStruct((4, ATOMS), F3...]
    dynamic_slice x8 -> x0, local copies, waits for them, and re-layouts: 4.66 us -> none  [local(): lax.map(one_block, block_inputs).reshape(local_atoms, feature_width)]
    ppermute x4 -> x1, starting transfers between devices: 12.4 us -> 7.87 us  [local_step(): ghosts = lax.ppermute(payload, ('dom', 'frame'), pairs)]
    sub x8 -> x0, other arithmetic: 4.53 us -> none  [one_block(): local_rows = block_idx - block_start]
    unnamed x14 -> x22, local copies, waits for them, and re-layouts: 1.59 us -> 4.54 us
    gather x2 -> x0, local copies, waits for them, and re-layouts: 2.5 us -> none  [the longest x1 1.79 us: local(): features[chosen]]
  transfers between devices with their start and end apart: 4 -> 1, of which waited for: 0 -> 1; matrix products, arithmetic and copies ran while one was open for 3% -> 0% of each run, Pallas kernels for 0% -> 0%
where the time goes in v1:
time: 39.1 us; the launch traced here: 38.8 us
  Pallas kernels  13.1 us (34%)
  blocking collectives  10.2 us (26%)
  starting transfers between devices  7.87 us (20%)
  local copies, waits for them, and re-layouts  4.55 us (12%)
  waiting for transfers between devices  2.38 us (6%)
  other arithmetic  0.6 us (2%)
    pallas_call x1, Pallas kernels, local_step(): pl.pallas_call(main_kernel, out_shape=jax.ShapeDtypeStruct((4, ATOMS), F3...  11.3 us
    all_to_all x1, blocking collectives, local_step(): lax.all_to_all(copies, 'frame', split_axis=0, concat_axis=0, tiled=True)  10.2 us
    ppermute x1, starting transfers between devices, local_step(): ghosts = lax.ppermute(payload, ('dom', 'frame'), pairs)  7.87 us
    unnamed x22, local copies, waits for them, and re-layouts  4.54 us
    ppermute x1, waiting for transfers between devices, local_step(): ghosts = lax.ppermute(payload, ('dom', 'frame'), pairs)  2.38 us
    pallas_call x1, Pallas kernels, local_step(): pl.pallas_call(pack_kernel, out_shape=jax.ShapeDtypeStruct((CAP, PAY), BF))  1.83 us
  transfers between devices with their start and end apart: 1, of which 1 were waited for; matrix products, arithmetic and copies ran while one was open for 0% of the time, Pallas kernels for 0%

profile of v1, /device:TPU:2, one launch (start us, length us, event | category | flops | bytes accessed | tf_op | source)
XLA Modules:
  0.0 38.8 jit_solution(4063976962657111949)
XLA Ops:
  0.0 0.0 copy-start
  0.0 0.0 copy-start.4
  0.0 0.0 copy-start.8
  0.0 0.0 copy-start.9
  0.0 0.0 copy-start.10
  0.0 1.8 %shard_map.118 = bf16[64,640]{1,0:T(8,128)(2,1)} custom-call(bf16[128,512]{1,0:T(8,128)(2,1)} %feat_ref.3, bf16[3,128]{1,0:T(4,128)(2,1)} %pos_ref.3, s32[1,2,64]{2,1,0:T(2,128)} %rows_ref.1, f32[3,1,3]{2,1,0:T(1,128)} %bitcast.4), custom_call_target="tpu_custom_call" | custom-call | tf_op jit(solution)/shard_map/pallas_call | solution.py:251
  1.9 0.0 copy-start.7
  1.9 7.9 %collective-permute-start = (bf16[64,640]{1,0:T(8,128)(2,1)}, bf16[64,640]{1,0:T(8,128)(2,1)S(1)}, u32[]{:S(2)}, u32[]{:S(2)}) collective-permute-start(bf16[64,640]{1,0:T(8,128)(2,1)} %shard_map.118), channel_id=1, source_target_pairs={{0,249},{1,8},{2,251},{3,10},{4,253},{5,12},{6,255},{7,14},{8,1},{... | collective-permute-start | bytes 245768 | tf_op jit(solution)/shard_map/ppermute | solution.py:260
  9.7 2.4 %collective-permute-done.pay_ref = bf16[64,640]{1,0:T(8,128)(2,1)S(1)} collective-permute-done((bf16[64,640]{1,0:T(8,128)(2,1)}, bf16[64,640]{1,0:T(8,128)(2,1)S(1)}, u32[]{:S(2)}, u32[]{:S(2)}) %collective-permute-start) | collective-permute-done | bytes 81952 | tf_op jit(solution)/shard_map/ppermute | solution.py:260
  12.1 0.0 copy-start.6
  12.1 0.0 copy-done
  12.1 0.0 copy-done.4
  12.1 0.0 copy-done.8
  12.1 0.0 copy-done.9
  12.1 0.0 copy-done.10
  12.1 0.0 copy-done.7
  12.2 0.6 %copy-done.6 = f32[1,3,3]{2,0,1:T(1,128)S(1)} copy-done((f32[1,3,3]{2,0,1:T(1,128)S(1)}, f32[1,3,3]{2,0,1:T(1,128)}, u32[]{:S(2)}) %copy-start.6) | copy-done | bytes 60
  12.8 0.0 copy-start.1
  12.8 1.0 %copy-done.1 = bf16[512,512]{1,0:T(8,128)(2,1)S(1)} copy-done((bf16[512,512]{1,0:T(8,128)(2,1)S(1)}, bf16[512,512]{1,0:T(8,128)(2,1)}, u32[]{:S(2)}) %copy-start.1) | copy-done | bytes 524312
  13.8 0.0 copy-start.2
  13.8 1.0 %copy-done.2 = bf16[512,512]{1,0:T(8,128)(2,1)S(1)} copy-done((bf16[512,512]{1,0:T(8,128)(2,1)S(1)}, bf16[512,512]{1,0:T(8,128)(2,1)}, u32[]{:S(2)}) %copy-start.2) | copy-done | bytes 524312
  14.9 0.0 copy-start.3
  14.9 1.0 %copy-done.3 = bf16[512,512]{1,0:T(8,128)(2,1)S(1)} copy-done((bf16[512,512]{1,0:T(8,128)(2,1)S(1)}, bf16[512,512]{1,0:T(8,128)(2,1)}, u32[]{:S(2)}) %copy-start.3) | copy-done | bytes 524312
  15.9 0.0 copy-start.5
  15.9 0.8 %copy-done.5 = f32[9,512]{1,0:T(8,128)S(1)} copy-done((f32[9,512]{1,0:T(8,128)S(1)}, f32[9,512]{1,0:T(8,128)}, u32[]{:S(2)}) %copy-start.5) | copy-done | bytes 18456
  16.7 11.3 %shard_map.119 = f32[4,128]{1,0:T(4,128)S(1)} custom-call(bf16[64,640]{1,0:T(8,128)(2,1)S(1)} %collective-permute-done.pay_ref, bf16[128,512]{1,0:T(8,128)(2,1)S(1)} %copy-done, bf16[3,128]{1,0:T(4,128)(2,1)S(1)} %copy-done.8, s32[128,128]{1,0:T(8,128)S(1)} %copy-done.4, s32[1,128]{1,0:T(1,128)S(1)} %bitcast.8, f32[3,1,3]{2,1,0:T(1,128)S(1)} %bitcast.5, ...), custom_call_target="tpu_custom_call" | custom-call | tf_op jit(solution)/shard_map/pallas_call | solution.py:261
  27.9 10.2 %all_to_all.5 = f32[8,4,128]{2,1,0:T(4,128)S(1)} all-to-all(f32[8,4,128]{2,1,0:T(4,128)S(1)} %broadcast_in_dim.3), channel_id=1, replica_groups=mesh['dom'=32,'frame'=8] {'frame'}, dimensions={0} | all-to-all | bytes 32768 | tf_op jit(solution)/shard_map/all_to_all | solution.py:287
  38.2 0.6 %broadcast_multiply_fusion = f32[4,128]{1,0:T(4,128)} fusion(f32[4,128]{1,0:T(4,128)S(1)} %reduce_sum.9), kind=kLoop, calls=%fused_computation | loop fusion | flops 512 | bytes 4096 | tf_op jit(solution)/shard_map/div | solution.py:288
  (2 shorter events, 0.0 us)
Async XLA Ops:
  0.0 12.1 %copy-start = (bf16[128,512]{1,0:T(8,128)(2,1)S(1)}, bf16[128,512]{1,0:T(8,128)(2,1)}, u32[]{:S(2)}) copy-start(bf16[128,512]{1,0:T(8,128)(2,1)} %feat_ref.3) | copy-start | bytes 393220
  0.0 12.1 %copy-start.4 = (s32[128,128]{1,0:T(8,128)S(1)}, s32[128,128]{1,0:T(8,128)}, u32[]{:S(2)}) copy-start(s32[128,128]{1,0:T(8,128)} %nbr_ref.1) | copy-start | bytes 196612
  0.0 12.1 %copy-start.8 = (bf16[3,128]{1,0:T(4,128)(2,1)S(1)}, bf16[3,128]{1,0:T(4,128)(2,1)}, u32[]{:S(2)}) copy-start(bf16[3,128]{1,0:T(4,128)(2,1)} %pos_ref.3) | copy-start | bytes 2308
  0.0 12.1 %copy-start.9 = (f32[512]{0:T(512)S(1)}, f32[512]{0:T(512)}, u32[]{:S(2)}) copy-start(f32[512]{0:T(512)} %param.19) | copy-start | bytes 6148
  0.0 12.1 %copy-start.10 = (s32[128]{0:T(128)S(1)}, s32[128]{0:T(128)}, u32[]{:S(2)}) copy-start(s32[128]{0:T(128)} %param.15) | copy-start | bytes 1540
  1.9 10.3 %copy-start.7 = (bf16[512,4]{0,1:T(4,128)(2,1)S(1)}, bf16[512,4]{0,1:T(4,128)(2,1)}, u32[]{:S(2)}) copy-start(bf16[512,4]{0,1:T(4,128)(2,1)} %param.23) | copy-start | bytes 12292
  1.9 10.2 %collective-permute-start = (bf16[64,640]{1,0:T(8,128)(2,1)}, bf16[64,640]{1,0:T(8,128)(2,1)S(1)}, u32[]{:S(2)}, u32[]{:S(2)}) collective-permute-start(bf16[64,640]{1,0:T(8,128)(2,1)} %shard_map.118), channel_id=1, source_target_pairs={{0,249},{1,8},{2,251},{3,10},{4,253},{5,12},{6,255},{7,14},{8,1},{... | collective-permute-start | bytes 245768 | tf_op jit(solution)/shard_map/ppermute | solution.py:260
  12.1 0.7 %copy-start.6 = (f32[1,3,3]{2,0,1:T(1,128)S(1)}, f32[1,3,3]{2,0,1:T(1,128)}, u32[]{:S(2)}) copy-start(f32[1,3,3]{2,0,1:T(1,128)} %param.17) | copy-start | bytes 112
  12.8 1.0 %copy-start.1 = (bf16[512,512]{1,0:T(8,128)(2,1)S(1)}, bf16[512,512]{1,0:T(8,128)(2,1)}, u32[]{:S(2)}) copy-start(bf16[512,512]{1,0:T(8,128)(2,1)} %wm_ref.1) | copy-start | bytes 1572868
  13.8 1.0 %copy-start.2 = (bf16[512,512]{1,0:T(8,128)(2,1)S(1)}, bf16[512,512]{1,0:T(8,128)(2,1)}, u32[]{:S(2)}) copy-start(bf16[512,512]{1,0:T(8,128)(2,1)} %wu_ref.1) | copy-start | bytes 1572868
  14.9 1.0 %copy-start.3 = (bf16[512,512]{1,0:T(8,128)(2,1)S(1)}, bf16[512,512]{1,0:T(8,128)(2,1)}, u32[]{:S(2)}) copy-start(bf16[512,512]{1,0:T(8,128)(2,1)} %wr_ref.1) | copy-start | bytes 1572868
  15.9 0.8 %copy-start.5 = (f32[9,512]{1,0:T(8,128)S(1)}, f32[9,512]{1,0:T(8,128)}, u32[]{:S(2)}) copy-start(f32[9,512]{1,0:T(8,128)} %we_ref.1) | copy-start | bytes 55300

commit v2 on v1

v2 whole, which is shorter than its diff:
```python
import jax
import jax.numpy as jnp
from jax import lax
from jax.experimental import pallas as pl
from jax.experimental.pallas import tpu as pltpu
from jax.sharding import PartitionSpec as P

BF = jnp.bfloat16
F32 = jnp.float32
I32 = jnp.int32
message_scale = 0.0884
radial_step = 1.25

ATOMS = 128
HALF = 64
CAP = 64
TABLE = CAP + ATOMS
WIDTH = 512
SLOTS = 128
FEATS = 16
GROUP = 8
GROUPS = HALF // GROUP
EXTRA = 128
PAY = WIDTH + EXTRA
RADIAL = 6
GHOST_ROWS = ((0, 64), (16, 64), (32, 64), (48, 64))
OWN_ROWS = ((0, 64), (0, 96), (0, 112), (0, 128))
TILE = 256


def iota(shape, dim):
    return lax.broadcasted_iota(I32, shape, dim)


def dot(a, b):
    return jnp.dot(a, b, preferred_element_type=F32)


def dot_t(a, b):
    return lax.dot_general(a, b, (((1,), (1,)), ((), ())), preferred_element_type=F32)


def mask(cond):
    return jnp.where(cond, 1.0, 0.0).astype(F32)


def pick(cond):
    return mask(cond).astype(BF)


def parity():
    return lax.axis_index("frame") % 2


def local(n):
    return jnp.where(parity() == 1, ATOMS - 1 - n, n)


def entries(ref):
    return [[ref[a, :, c : c + 1] for c in range(3)] for a in range(3)]


def vectors(rot, we_ref, c):
    return 0.5 * (rot[0][c] * we_ref[6:7, :] + rot[1][c] * we_ref[7:8, :] + rot[2][c] * we_ref[8:9, :])


def split(x):
    high = x.astype(BF).astype(F32)
    return high, x - high


def centres(pos_ref):
    atom = local(iota((8, ATOMS), 1))
    in_group = mask(atom // GROUP == iota((8, ATOMS), 0))
    spread = pick(local(iota((ATOMS, ATOMS), 0)) % GROUP == iota((ATOMS, ATOMS), 1) // FEATS)
    return [dot((in_group * pos_ref[c : c + 1, :].astype(F32)).astype(BF), spread) for c in range(3)]


def placed_rows(chosen, pos_ref):
    ones = jnp.ones((ATOMS, ATOMS), BF)
    return [dot((chosen * pos_ref[c : c + 1, :].astype(F32)).astype(BF), ones) for c in range(3)]


def fill_edges(edges, reach, centre, bounds):
    kind = iota((1, ATOMS), 1) % FEATS
    shift = kind.astype(F32) * radial_step
    at = 0
    for g in range(GROUPS):
        lo, hi = bounds[g // 2]
        rel = [reach[c][lo:hi] - centre[c][g : g + 1, :] for c in range(3)]
        dist = jnp.sqrt(rel[0] * rel[0] + rel[1] * rel[1] + rel[2] * rel[2] + 0.25) - shift
        value = jnp.exp(-(dist * dist))
        axis = jnp.where(kind % 3 == 0, rel[0], jnp.where(kind % 3 == 1, rel[1], rel[2]))
        high, low = split(axis)
        axis = jnp.where((kind >= 9) & (kind < 12), low, high)
        value = jnp.where(kind < RADIAL, value, jnp.where(kind < 15, axis, 1.0))
        edges[at : at + hi - lo, :] = value.astype(BF)
        at += hi - lo


def fill_filter(rhs, rot, we_ref, be_ref):
    vec = jnp.concatenate([vectors(rot, we_ref, c) for c in range(3)], axis=0)
    high, low = split(vec)
    rows = jnp.concatenate([0.5 * we_ref[0:RADIAL, :], high, high, low, 0.5 * be_ref[...]], axis=0)
    rows = jnp.concatenate([rows] * GROUP, axis=0).astype(BF)
    block = iota((ATOMS, WIDTH), 0) // FEATS
    for a in range(GROUP):
        rhs[a, :, :] = jnp.where(block == a, rows, jnp.zeros_like(rows))


def from_middle(reach):
    lane = iota((1, ATOMS), 1)
    axis = jnp.where(lane % 3 == 0, reach[0], jnp.where(lane % 3 == 1, reach[1], reach[2])) - 2.0
    high, low = split(axis)
    axis = jnp.where((lane >= 3) & (lane < 6), low, high)
    return jnp.where(lane < 9, axis, 0.0).astype(BF)


def change_filter(rot, other, we_ref):
    vec = jnp.concatenate([vectors(other, we_ref, c) - vectors(rot, we_ref, c) for c in range(3)], axis=0)
    high, low = split(vec)
    return jnp.concatenate([high, high, low, jnp.zeros((ATOMS - 9, WIDTH), F32)], axis=0).astype(BF)


def fill_change(change, middle, pos_ref, reach, rot, other, we_ref):
    weights = change_filter(rot, other, we_ref)
    change[...] = dot(from_middle(reach), weights).astype(BF)
    row = iota((HALF, ATOMS), 0)
    chosen = mask(local(iota((HALF, ATOMS), 1)) == (row % GROUPS) * GROUP + row // GROUPS)
    middle[...] = dot(from_middle(placed_rows(chosen, pos_ref)), weights).astype(BF).astype(F32)


def fill_times(times, total):
    for a in range(GROUP):
        spread = pick(iota((ATOMS, ATOMS), 0) % HALF == iota((ATOMS, ATOMS), 1) * GROUP + a)
        times[a, :, :] = dot(total, spread)


def sum_rows(prod, rows):
    parts = [prod[r : r + 16] for r in range(0, rows, 16)]
    while len(parts) > SUMS:
        parts = [
            parts[q] + parts[q + 1] if q + 1 < len(parts) else parts[q] for q in range(0, len(parts), 2)
        ]
    total = parts[0].astype(F32)
    for part in parts[1:]:
        total = total + part.astype(F32)
    return total[:8] + total[8:]


SUMS = 2


def pair_loop(bounds, merge, table, edges, rhs, times, change, middle, partial):
    offsets = [0]
    for g in range(GROUPS):
        lo, hi = bounds[g // 2]
        offsets.append(offsets[-1] + hi - lo)

    def step(a, carry):
        share = times[a].astype(BF)
        centre = middle[pl.ds(pl.multiple_of(a * GROUPS, GROUPS), GROUPS), :]
        for w in range(WIDTH // TILE):
            span = slice(w * TILE, (w + 1) * TILE)
            for first in range(0, GROUPS, merge):
                pre = dot(edges[offsets[first] : offsets[first + merge], :], rhs[a, :, span]).astype(BF)
                for g in range(first, first + merge):
                    lo, hi = bounds[g // 2]
                    weighted = table[lo:hi, span] * share[lo:hi, g : g + 1]
                    half = pre[offsets[g] - offsets[first] : offsets[g + 1] - offsets[first]]
                    for f in range(2):
                        if f == 1:
                            half = half + (change[lo:hi, span] - centre[g : g + 1, span].astype(BF))
                        gate = half * jnp.tanh(half) + half
                        at = pl.multiple_of(a * (16 * 8) + (f * GROUPS + g) * 8, 8)
                        done = sum_rows(gate * weighted, hi - lo)
                        for t in range(TILE // 128):
                            partial[w * (TILE // 128) + t, pl.ds(at, 8), :] = done[:, t * 128 : (t + 1) * 128]
        return carry

    lax.fori_loop(0, GROUP, step, 0)
    tiles = []
    for t in range(WIDTH // 128):
        total = partial[t, pl.ds(0, ATOMS, stride=8), :]
        for r in range(1, 8):
            total = total + partial[t, pl.ds(r, ATOMS, stride=8), :]
        tiles.append(total)
    return jnp.concatenate(tiles, axis=1)


def pack_kernel(feat_ref, pos_ref, rows_ref, out_ref):
    wanted = jnp.where(parity() == 1, rows_ref[0, 1:2, :], rows_ref[0, 0:1, :])
    row = iota((CAP, CAP), 0)
    source = jnp.where(parity() == 1, row, CAP - 1 - row)
    column = jnp.sum(
        jnp.where(iota((CAP, CAP), 1) == source, wanted, 0).astype(F32), axis=1, keepdims=True
    ).astype(I32)
    chosen = pick(iota((CAP, ATOMS), 1) == column)
    out_ref[:, :WIDTH] = dot(chosen, feat_ref[...]).astype(BF)
    lane = iota((CAP, EXTRA), 1)
    rest = jnp.zeros((CAP, EXTRA), F32)
    for c in range(3):
        line = chosen.astype(F32) * pos_ref[c : c + 1, :].astype(F32)
        rest = jnp.where(lane == c, jnp.sum(line, axis=1, keepdims=True), rest)
    out_ref[:, WIDTH:] = rest.astype(BF)


def own_kernel(
    feat_ref,
    pos_ref,
    nbr_ref,
    cnt_ref,
    frame_ref,
    other_ref,
    we_ref,
    be_ref,
    sum_ref,
    ghost_ref,
    table,
    edges,
    rhs,
    times,
    change,
    middle,
    partial,
):
    own = pick(iota((ATOMS, ATOMS), 1) == local(iota((ATOMS, ATOMS), 0)))
    table[...] = dot(own, feat_ref[...]).astype(BF)

    raw = nbr_ref[...]
    order = jnp.where(raw < ATOMS, raw + CAP, jnp.where(raw < ATOMS + CAP, raw - ATOMS, raw))
    order = jnp.where(parity() == 1, 2 * CAP + ATOMS - 1 - order, order)
    by_slot = order.astype(F32).T.astype(BF)
    atom = local(iota((ATOMS, ATOMS), 0))
    lane = iota((ATOMS, ATOMS), 1)
    to_low = pick((atom == lane) & (lane < HALF))
    to_high = pick(atom + HALF == lane)
    folded = dot(by_slot[: SLOTS // 2], to_low) + dot(by_slot[SLOTS // 2 :], to_high)
    cnt = jnp.broadcast_to(cnt_ref[...].astype(F32), (8, ATOMS)).astype(BF)
    live = (dot(cnt, to_low) + dot(cnt, to_high))[0:1, :]
    slot = iota((SLOTS // 2, ATOMS), 0) + jnp.where(iota((SLOTS // 2, ATOMS), 1) < HALF, 0, SLOTS // 2)
    folded = jnp.where(slot.astype(F32) < live, folded, -1.0).astype(BF)
    place = iota((TABLE, ATOMS), 0).astype(F32).astype(BF)
    total = jnp.zeros((TABLE, ATOMS), BF)
    one = jnp.ones((TABLE, ATOMS), BF)
    for k in range(SLOTS // 2):
        total = jnp.where(place == folded[k : k + 1, :], total + one, total)
    ghost_ref[...] = total[:CAP]
    fill_times(times, total[CAP:])

    rot, other = entries(frame_ref), entries(other_ref)
    reach = placed_rows(own.astype(F32), pos_ref)
    fill_edges(edges, reach, centres(pos_ref), OWN_ROWS)
    fill_filter(rhs, rot, we_ref, be_ref)
    fill_change(change, middle, pos_ref, reach, rot, other, we_ref)
    sum_ref[...] = pair_loop(OWN_ROWS, 1, table, edges, rhs, times, change, middle, partial)


def last_kernel(
    pay_ref,
    sum_ref,
    ghost_ref,
    feat_ref,
    pos_ref,
    frame_ref,
    other_ref,
    we_ref,
    be_ref,
    wm_ref,
    wu_ref,
    wr_ref,
    wh_ref,
    out_ref,
    edges,
    rhs,
    times,
    change,
    middle,
    partial,
):
    rot, other = entries(frame_ref), entries(other_ref)
    extra = pay_ref[:, WIDTH:]
    reach = [dot(extra, pick(iota((EXTRA, EXTRA), 0) == c)) for c in range(3)]
    fill_times(times, ghost_ref[...])
    fill_edges(edges, reach, centres(pos_ref), GHOST_ROWS)
    fill_filter(rhs, rot, we_ref, be_ref)
    fill_change(change, middle, pos_ref, reach, rot, other, we_ref)
    total = pair_loop(GHOST_ROWS, GROUPS, pay_ref, edges, rhs, times, change, middle, partial)

    msg = ((total + sum_ref[...]) * message_scale).astype(BF)
    row = iota((ATOMS, ATOMS), 0)
    lane = iota((ATOMS, ATOMS), 1)
    row_atom = (row % GROUPS) * GROUP + row // 16
    mine = dot(pick(lane == local(row_atom)), feat_ref[...])

    def silu(x):
        h = 0.5 * x
        return h * jnp.tanh(h) + h

    hidden = silu(dot(msg, wm_ref[...])).astype(BF)
    updated = (mine + dot(hidden, wu_ref[...])).astype(BF)
    readout = silu(dot(updated, wr_ref[...])).astype(BF)
    lane_atom = (lane % GROUPS) * GROUP + lane // 16
    out = jnp.zeros((4, ATOMS), F32)
    for f, turn in enumerate((rot, other)):
        back = pick((local(row) == lane_atom) & ((lane // GROUPS) % 2 == f))
        heads = dot_t(wh_ref[...], dot(back, readout).astype(BF))
        force = [
            turn[0][c] * heads[0:1] + turn[1][c] * heads[1:2] + turn[2][c] * heads[2:3] for c in range(3)
        ]
        out = out + jnp.concatenate(force + [heads[3:4]], axis=0)
    out_ref[...] = out


def scratch(rows, edge_rows):
    return [
        pltpu.VMEM((edge_rows, ATOMS), BF),
        pltpu.VMEM((GROUP, ATOMS, WIDTH), BF),
        pltpu.VMEM((GROUP, rows, ATOMS), F32),
        pltpu.VMEM((rows, WIDTH), BF),
        pltpu.VMEM((HALF, WIDTH), F32),
        pltpu.VMEM((WIDTH // 128, ATOMS * 8, 128), F32),
    ]


def local_step(
    features,
    positions,
    neighbours,
    counts,
    send_rows,
    frames,
    w_edge,
    b_edge,
    w_message,
    w_update,
    w_readout,
    w_heads,
):
    dom_count = lax.axis_size("dom")
    frame_count = lax.axis_size("frame")
    frame = jnp.transpose(frames, (1, 0, 2))
    other = lax.ppermute(frame, "frame", [(f, f ^ 1) for f in range(frame_count)])
    payload = pl.pallas_call(
        pack_kernel,
        out_shape=jax.ShapeDtypeStruct((CAP, PAY), BF),
    )(features, positions, send_rows)
    pairs = []
    for d in range(dom_count):
        for f in range(frame_count):
            to = (d + 1) % dom_count if f % 2 else (d - 1) % dom_count
            pairs.append((d * frame_count + f, to * frame_count + (f ^ 1)))
    ghosts = lax.ppermute(payload, ("dom", "frame"), pairs)
    bias = b_edge.reshape(1, WIDTH)
    own_rows = 2 * sum(hi - lo for lo, hi in OWN_ROWS)
    ghost_rows = 2 * sum(hi - lo for lo, hi in GHOST_ROWS)
    own_sum, ghost_times = pl.pallas_call(
        own_kernel,
        out_shape=[
            jax.ShapeDtypeStruct((ATOMS, WIDTH), F32),
            jax.ShapeDtypeStruct((CAP, ATOMS), BF),
        ],
        scratch_shapes=[pltpu.VMEM((ATOMS, WIDTH), BF)] + scratch(ATOMS, own_rows),
        compiler_params=pltpu.CompilerParams(vmem_limit_bytes=24 << 20),
        cost_estimate=pl.CostEstimate(flops=2_000_000_000, bytes_accessed=1_000_000, transcendentals=7_000_000),
    )(features, positions, neighbours, counts.reshape(1, ATOMS), frame, other, w_edge, bias)
    part = pl.pallas_call(
        last_kernel,
        out_shape=jax.ShapeDtypeStruct((4, ATOMS), F32),
        scratch_shapes=scratch(CAP, ghost_rows),
        compiler_params=pltpu.CompilerParams(vmem_limit_bytes=24 << 20),
    )(
        ghosts,
        own_sum,
        ghost_times,
        features,
        positions,
        frame,
        other,
        w_edge,
        bias,
        w_message,
        w_update,
        w_readout,
        w_heads.T,
    )
    copies = jnp.broadcast_to(part, (frame_count, *part.shape))
    everything = lax.all_to_all(copies, "frame", split_axis=0, concat_axis=0, tiled=True)
    return jnp.sum(everything, axis=0) / frame_count


def solution(mesh):
    placed = (
        P("dom", None),
        P(None, "dom"),
        P("dom", None),
        P("dom"),
        P("dom", None, None),
        P("frame", None, None),
        P(),
        P(),
        P(),
        P(),
        P(),
        P(),
    )
    return jax.shard_map(
        local_step, mesh=mesh, in_specs=placed, out_specs=P(None, "dom"), check_vma=False
    )
```

time: 39.1 us -> 36.8 us (0.941)
  waiting for transfers between devices: 2.38 us -> 0.01 us
  local copies, waits for them, and re-layouts: 4.55 us -> 2.84 us
  Pallas kernels: 13.1 us -> 14.5 us
    ppermute x1, waiting for transfers between devices: 2.38 us -> 0.01 us  [local_step(): ghosts = lax.ppermute(payload, ('dom', 'frame'), pairs)]
    unnamed x22, local copies, waits for them, and re-layouts: 4.54 us -> 2.84 us
    ppermute x0 -> x1, starting transfers between devices: none -> 1.58 us  [local_step(): lax.ppermute(frame, 'frame', [(f, f ^ 1) for f in range(frame_count)])]
    pallas_call x1 -> x2, Pallas kernels: 11.3 us -> 12.7 us  [the longest x1 7.93 us: local_step(): pl.pallas_call(own_kernel, out_shape=[jax.ShapeDtypeStruct((ATOMS, WIDTH)...]
    ppermute x1, starting transfers between devices: 7.87 us -> 6.47 us  [local_step(): ghosts = lax.ppermute(payload, ('dom', 'frame'), pairs)]
  transfers between devices with their start and end apart: 1 -> 2, of which waited for: 1 -> 0; matrix products, arithmetic and copies ran while one was open for 0% -> 0% of each run, Pallas kernels for 0% -> 27%
where the time goes in v2:
time: 36.8 us; the launch traced here: 36.6 us
  Pallas kernels  14.5 us (39%)
  blocking collectives  10.5 us (29%)
  starting transfers between devices  8.04 us (22%)
  local copies, waits for them, and re-layouts  2.84 us (8%)
  other arithmetic  0.6 us (2%)
    all_to_all x1, blocking collectives, local_step(): lax.all_to_all(copies, 'frame', split_axis=0, concat_axis=0, tiled=True)  10.5 us
    pallas_call x1, Pallas kernels, local_step(): pl.pallas_call(own_kernel, out_shape=[jax.ShapeDtypeStruct((ATOMS, WIDTH)...  7.93 us
    ppermute x1, starting transfers between devices, local_step(): ghosts = lax.ppermute(payload, ('dom', 'frame'), pairs)  6.47 us
    pallas_call x1, Pallas kernels, local_step(): pl.pallas_call(last_kernel, out_shape=jax.ShapeDtypeStruct((4, ATOMS), F3...  4.8 us
    unnamed x22, local copies, waits for them, and re-layouts  2.84 us
    pallas_call x1, Pallas kernels, local_step(): pl.pallas_call(pack_kernel, out_shape=jax.ShapeDtypeStruct((CAP, PAY), BF))  1.79 us
    ppermute x1, starting transfers between devices, local_step(): lax.ppermute(frame, 'frame', [(f, f ^ 1) for f in range(frame_count)])  1.58 us
  transfers between devices with their start and end apart: 2, of which 0 were waited for; matrix products, arithmetic and copies ran while one was open for 0% of the time, Pallas kernels for 27%

profile of v2, /device:TPU:2, one launch (start us, length us, event | category | flops | bytes accessed | tf_op | source)
XLA Modules:
  0.0 36.6 jit_solution(5055298535269225734)
XLA Ops:
  0.0 0.0 copy-start.8
  0.0 0.0 copy-start
  0.0 0.7 %copy-done.8 = f32[1,3,3]{2,0,1:T(1,128)S(1)} copy-done((f32[1,3,3]{2,0,1:T(1,128)S(1)}, f32[1,3,3]{2,0,1:T(1,128)}, u32[]{:S(2)}) %copy-start.8) | copy-done | bytes 60
  0.7 0.0 copy-start.4
  0.7 1.6 %collective-permute-start.1 = (f32[3,1,3]{2,1,0:T(1,128)S(1)}, f32[3,1,3]{2,1,0:T(1,128)S(1)}, u32[]{:S(2)}, u32[]{:S(2)}) collective-permute-start(f32[3,1,3]{2,1,0:T(1,128)S(1)} %bitcast.7), channel_id=1, source_target_pairs={{0,1},{1,0},{2,3},{3,2},{4,5},{5,4},{6,7},{7,6},{8,9},{9,8},{10,11... | collective-permute-start | bytes 116 | tf_op jit(solution)/shard_map/ppermute | solution.py:343
  2.3 1.8 %shard_map.118 = bf16[64,640]{1,0:T(8,128)(2,1)} custom-call(bf16[128,512]{1,0:T(8,128)(2,1)} %feat_ref.5, bf16[3,128]{1,0:T(4,128)(2,1)} %pos_ref.5, s32[1,2,64]{2,1,0:T(2,128)} %rows_ref.1), custom_call_target="tpu_custom_call" | custom-call | tf_op jit(solution)/shard_map/pallas_call | solution.py:344
  4.1 0.0 copy-start.7
  4.1 6.5 %collective-permute-start = (bf16[64,640]{1,0:T(8,128)(2,1)}, bf16[64,640]{1,0:T(8,128)(2,1)S(1)}, u32[]{:S(2)}, u32[]{:S(2)}) collective-permute-start(bf16[64,640]{1,0:T(8,128)(2,1)} %shard_map.118), channel_id=1, source_target_pairs={{0,249},{1,8},{2,251},{3,10},{4,253},{5,12},{6,255},{7,14},{8,1},{... | collective-permute-start | bytes 245768 | tf_op jit(solution)/shard_map/ppermute | solution.py:353
  10.5 0.0 collective-permute-done.1.other_ref
  10.5 0.0 copy-start.6
  10.5 0.0 copy-start.10
  10.5 0.0 copy-done
  10.5 0.0 copy-done.4
  10.5 0.0 copy-done.7
  10.6 0.7 %copy-done.6 = bf16[3,128]{1,0:T(4,128)(2,1)S(1)} copy-done((bf16[3,128]{1,0:T(4,128)(2,1)S(1)}, bf16[3,128]{1,0:T(4,128)(2,1)}, u32[]{:S(2)}) %copy-start.6) | copy-done | bytes 792
  11.2 0.0 copy-done.10
  11.2 0.0 copy-start.9
  11.2 0.8 %copy-done.9 = s32[128,128]{1,0:T(8,128)S(1)} copy-done((s32[128,128]{1,0:T(8,128)S(1)}, s32[128,128]{1,0:T(8,128)}, u32[]{:S(2)}) %copy-start.9) | copy-done | bytes 65560
  12.0 0.0 copy-start.1
  12.0 0.0 copy-start.2
  12.1 0.0 copy-start.3
  12.1 7.9 %shard_map.119 = (f32[128,512]{1,0:T(8,128)S(1)}, bf16[64,128]{1,0:T(8,128)(2,1)S(1)}) custom-call(bf16[128,512]{1,0:T(8,128)(2,1)S(1)} %copy-done, bf16[3,128]{1,0:T(4,128)(2,1)S(1)} %copy-done.6, s32[128,128]{1,0:T(8,128)S(1)} %copy-done.9, s32[1,128]{1,0:T(1,128)S(1)} %bitcast.10, f32[3,1,3]{2,1,0:T(1,128)S(1)} %bitcast.8, ...), custom_call_target="tpu_custom_call" | custom-call | flops 2000000000 | bytes 1000000 | tf_op jit(solution)/shard_map/pallas_call | solution.py:357
  20.0 0.0 copy-start.5
  20.0 0.0 collective-permute-done.pay_ref
  20.0 0.0 copy-done.1
  20.0 0.0 copy-done.2
  20.0 0.0 copy-done.3
  20.0 0.6 %copy-done.5 = bf16[512,4]{0,1:T(4,128)(2,1)S(1)} copy-done((bf16[512,4]{0,1:T(4,128)(2,1)S(1)}, bf16[512,4]{0,1:T(4,128)(2,1)}, u32[]{:S(2)}) %copy-start.5) | copy-done | bytes 4120
  20.7 4.8 %shard_map.120 = f32[4,128]{1,0:T(4,128)S(1)} custom-call(bf16[64,640]{1,0:T(8,128)(2,1)S(1)} %collective-permute-done.pay_ref, f32[128,512]{1,0:T(8,128)S(1)} %get-tuple-element.7.sum_ref, bf16[64,128]{1,0:T(8,128)(2,1)S(1)} %get-tuple-element.8.ghost_ref, bf16[128,512]{1,0:T(8,128)(2,1)S(1)} %copy-done, bf16[3,128]{1,0:T(4,128)(2,1)S(1)} %copy-done.6, ...), custom_call_target="tpu_custom_call" | custom-call | tf_op jit(solution)/shard_map/pallas_call | solution.py:367
  25.5 10.5 %all_to_all.5 = f32[8,4,128]{2,1,0:T(4,128)S(1)} all-to-all(f32[8,4,128]{2,1,0:T(4,128)S(1)} %broadcast_in_dim.3), channel_id=1, replica_groups=mesh['dom'=32,'frame'=8] {'frame'}, dimensions={0} | all-to-all | bytes 32768 | tf_op jit(solution)/shard_map/all_to_all | solution.py:388
  36.0 0.6 %broadcast_multiply_fusion = f32[4,128]{1,0:T(4,128)} fusion(f32[4,128]{1,0:T(4,128)S(1)} %reduce_sum.9), kind=kLoop, calls=%fused_computation | loop fusion | flops 512 | bytes 4096 | tf_op jit(solution)/shard_map/div | solution.py:389
  (2 shorter events, 0.0 us)
Async XLA Ops:
  0.0 0.7 %copy-start.8 = (f32[1,3,3]{2,0,1:T(1,128)S(1)}, f32[1,3,3]{2,0,1:T(1,128)}, u32[]{:S(2)}) copy-start(f32[1,3,3]{2,0,1:T(1,128)} %param.17) | copy-start | bytes 112
  0.0 10.5 %copy-start = (bf16[128,512]{1,0:T(8,128)(2,1)S(1)}, bf16[128,512]{1,0:T(8,128)(2,1)}, u32[]{:S(2)}) copy-start(bf16[128,512]{1,0:T(8,128)(2,1)} %feat_ref.5) | copy-start | bytes 393220
  0.7 9.9 %copy-start.4 = (f32[9,512]{1,0:T(8,128)S(1)}, f32[9,512]{1,0:T(8,128)}, u32[]{:S(2)}) copy-start(f32[9,512]{1,0:T(8,128)} %we_ref.3) | copy-start | bytes 55300
  0.7 9.8 %collective-permute-start.1 = (f32[3,1,3]{2,1,0:T(1,128)S(1)}, f32[3,1,3]{2,1,0:T(1,128)S(1)}, u32[]{:S(2)}, u32[]{:S(2)}) collective-permute-start(f32[3,1,3]{2,1,0:T(1,128)S(1)} %bitcast.7), channel_id=1, source_target_pairs={{0,1},{1,0},{2,3},{3,2},{4,5},{5,4},{6,7},{7,6},{8,9},{9,8},{10,11... | collective-permute-start | bytes 116 | tf_op jit(solution)/shard_map/ppermute | solution.py:343
  4.1 6.5 %copy-start.7 = (f32[512]{0:T(512)S(1)}, f32[512]{0:T(512)}, u32[]{:S(2)}) copy-start(f32[512]{0:T(512)} %param.19) | copy-start | bytes 6148
  4.1 15.9 %collective-permute-start = (bf16[64,640]{1,0:T(8,128)(2,1)}, bf16[64,640]{1,0:T(8,128)(2,1)S(1)}, u32[]{:S(2)}, u32[]{:S(2)}) collective-permute-start(bf16[64,640]{1,0:T(8,128)(2,1)} %shard_map.118), channel_id=1, source_target_pairs={{0,249},{1,8},{2,251},{3,10},{4,253},{5,12},{6,255},{7,14},{8,1},{... | collective-permute-start | bytes 245768 | tf_op jit(solution)/shard_map/ppermute | solution.py:353
  10.5 0.7 %copy-start.6 = (bf16[3,128]{1,0:T(4,128)(2,1)S(1)}, bf16[3,128]{1,0:T(4,128)(2,1)}, u32[]{:S(2)}) copy-start(bf16[3,128]{1,0:T(4,128)(2,1)} %pos_ref.5) | copy-start | bytes 2308
  10.5 0.7 %copy-start.10 = (s32[128]{0:T(128)S(1)}, s32[128]{0:T(128)}, u32[]{:S(2)}) copy-start(s32[128]{0:T(128)} %param.15) | copy-start | bytes 1540
  11.2 0.8 %copy-start.9 = (s32[128,128]{1,0:T(8,128)S(1)}, s32[128,128]{1,0:T(8,128)}, u32[]{:S(2)}) copy-start(s32[128,128]{1,0:T(8,128)} %nbr_ref.1) | copy-start | bytes 196612
  12.0 8.0 %copy-start.1 = (bf16[512,512]{1,0:T(8,128)(2,1)S(1)}, bf16[512,512]{1,0:T(8,128)(2,1)}, u32[]{:S(2)}) copy-start(bf16[512,512]{1,0:T(8,128)(2,1)} %wm_ref.1) | copy-start | bytes 1572868
  12.0 8.0 %copy-start.2 = (bf16[512,512]{1,0:T(8,128)(2,1)S(1)}, bf16[512,512]{1,0:T(8,128)(2,1)}, u32[]{:S(2)}) copy-start(bf16[512,512]{1,0:T(8,128)(2,1)} %wu_ref.1) | copy-start | bytes 1572868
  12.1 8.0 %copy-start.3 = (bf16[512,512]{1,0:T(8,128)(2,1)S(1)}, bf16[512,512]{1,0:T(8,128)(2,1)}, u32[]{:S(2)}) copy-start(bf16[512,512]{1,0:T(8,128)(2,1)} %wr_ref.1) | copy-start | bytes 1572868
  20.0 0.7 %copy-start.5 = (bf16[512,4]{0,1:T(4,128)(2,1)S(1)}, bf16[512,4]{0,1:T(4,128)(2,1)}, u32[]{:S(2)}) copy-start(bf16[512,4]{0,1:T(4,128)(2,1)} %param.23) | copy-start | bytes 12292

commit v3 on v2

--- a/solution.py
+++ b/solution.py
@@ -108,28 +108,6 @@
         rhs[a, :, :] = jnp.where(block == a, rows, jnp.zeros_like(rows))
 
 
-def from_middle(reach):
-    lane = iota((1, ATOMS), 1)
-    axis = jnp.where(lane % 3 == 0, reach[0], jnp.where(lane % 3 == 1, reach[1], reach[2])) - 2.0
-    high, low = split(axis)
-    axis = jnp.where((lane >= 3) & (lane < 6), low, high)
-    return jnp.where(lane < 9, axis, 0.0).astype(BF)
-
-
-def change_filter(rot, other, we_ref):
-    vec = jnp.concatenate([vectors(other, we_ref, c) - vectors(rot, we_ref, c) for c in range(3)], axis=0)
-    high, low = split(vec)
-    return jnp.concatenate([high, high, low, jnp.zeros((ATOMS - 9, WIDTH), F32)], axis=0).astype(BF)
-
-
-def fill_change(change, middle, pos_ref, reach, rot, other, we_ref):
-    weights = change_filter(rot, other, we_ref)
-    change[...] = dot(from_middle(reach), weights).astype(BF)
-    row = iota((HALF, ATOMS), 0)
-    chosen = mask(local(iota((HALF, ATOMS), 1)) == (row % GROUPS) * GROUP + row // GROUPS)
-    middle[...] = dot(from_middle(placed_rows(chosen, pos_ref)), weights).astype(BF).astype(F32)
-
-
 def fill_times(times, total):
     for a in range(GROUP):
         spread = pick(iota((ATOMS, ATOMS), 0) % HALF == iota((ATOMS, ATOMS), 1) * GROUP + a)
@@ -151,44 +129,55 @@
 SUMS = 2
 
 
-def pair_loop(bounds, merge, table, edges, rhs, times, change, middle, partial):
+def offsets_of(bounds):
     offsets = [0]
     for g in range(GROUPS):
         lo, hi = bounds[g // 2]
         offsets.append(offsets[-1] + hi - lo)
-
-    def step(a, carry):
-        share = times[a].astype(BF)
-        centre = middle[pl.ds(pl.multiple_of(a * GROUPS, GROUPS), GROUPS), :]
-        for w in range(WIDTH // TILE):
-            span = slice(w * TILE, (w + 1) * TILE)
-            for first in range(0, GROUPS, merge):
-                pre = dot(edges[offsets[first] : offsets[first + merge], :], rhs[a, :, span]).astype(BF)
-                for g in range(first, first + merge):
-                    lo, hi = bounds[g // 2]
-                    weighted = table[lo:hi, span] * share[lo:hi, g : g + 1]
-                    half = pre[offsets[g] - offsets[first] : offsets[g + 1] - offsets[first]]
-                    for f in range(2):
-                        if f == 1:
-                            half = half + (change[lo:hi, span] - centre[g : g + 1, span].astype(BF))
-                        gate = half * jnp.tanh(half) + half
-                        at = pl.multiple_of(a * (16 * 8) + (f * GROUPS + g) * 8, 8)
-                        done = sum_rows(gate * weighted, hi - lo)
-                        for t in range(TILE // 128):
-                            partial[w * (TILE // 128) + t, pl.ds(at, 8), :] = done[:, t * 128 : (t + 1) * 128]
-        return carry
-
-    lax.fori_loop(0, GROUP, step, 0)
+    return offsets
+
+
+OWN_AT = offsets_of(OWN_ROWS)
+GHOST_AT = offsets_of(GHOST_ROWS)
+
+
+def gated(pre):
+    half = pre.astype(BF)
+    return half * jnp.tanh(half) + half
+
+
+def cut(rows):
+    return [rows[r : r + 16] for r in range(0, rows.shape[0], 16)]
+
+
+def total_of(parts):
+    while len(parts) > SUMS:
+        parts = [
+            parts[q] + parts[q + 1] if q + 1 < len(parts) else parts[q] for q in range(0, len(parts), 2)
+        ]
+    total = parts[0].astype(F32)
+    for part in parts[1:]:
+        total = total + part.astype(F32)
+    return total[:8] + total[8:]
+
+
+def keep(partial, a, k, count, w, done):
+    at = pl.multiple_of((a * count + k) * 8, 8)
+    for t in range(TILE // 128):
+        partial[w * (TILE // 128) + t, pl.ds(at, 8), :] = done[:, t * 128 : (t + 1) * 128]
+
+
+def collect(partial, rows):
     tiles = []
     for t in range(WIDTH // 128):
-        total = partial[t, pl.ds(0, ATOMS, stride=8), :]
+        total = partial[t, pl.ds(0, rows, stride=8), :]
         for r in range(1, 8):
-            total = total + partial[t, pl.ds(r, ATOMS, stride=8), :]
+            total = total + partial[t, pl.ds(r, rows, stride=8), :]
         tiles.append(total)
     return jnp.concatenate(tiles, axis=1)
 
 
-def pack_kernel(feat_ref, pos_ref, rows_ref, out_ref):
+def pack_kernel(feat_ref, pos_ref, rows_ref, frame_ref, out_ref):
     wanted = jnp.where(parity() == 1, rows_ref[0, 1:2, :], rows_ref[0, 0:1, :])
     row = iota((CAP, CAP), 0)
     source = jnp.where(parity() == 1, row, CAP - 1 - row)
@@ -202,7 +191,16 @@
     for c in range(3):
         line = chosen.astype(F32) * pos_ref[c : c + 1, :].astype(F32)
         rest = jnp.where(lane == c, jnp.sum(line, axis=1, keepdims=True), rest)
-    out_ref[:, WIDTH:] = rest.astype(BF)
+    turn = jnp.zeros((CAP, EXTRA), F32)
+    for a in range(3):
+        for c in range(3):
+            k = 8 + 3 * a + c
+            here = (lane == k) | (lane == k + 16) | (lane == k + 32)
+            turn = jnp.where(here, frame_ref[a, :, c : c + 1], turn)
+    high, rest_of = split(turn)
+    mid, low = split(rest_of)
+    turn = jnp.where(lane < 24, high, jnp.where(lane < 40, mid, low))
+    out_ref[:, WIDTH:] = (rest + turn).astype(BF)
 
 
 def own_kernel(
@@ -211,17 +209,14 @@
     nbr_ref,
     cnt_ref,
     frame_ref,
-    other_ref,
     we_ref,
     be_ref,
     sum_ref,
-    ghost_ref,
+    total_ref,
     table,
     edges,
     rhs,
     times,
-    change,
-    middle,
     partial,
 ):
     own = pick(iota((ATOMS, ATOMS), 1) == local(iota((ATOMS, ATOMS), 0)))
@@ -245,25 +240,35 @@
     one = jnp.ones((TABLE, ATOMS), BF)
     for k in range(SLOTS // 2):
         total = jnp.where(place == folded[k : k + 1, :], total + one, total)
-    ghost_ref[...] = total[:CAP]
+    total_ref[...] = total
     fill_times(times, total[CAP:])
-
-    rot, other = entries(frame_ref), entries(other_ref)
-    reach = placed_rows(own.astype(F32), pos_ref)
-    fill_edges(edges, reach, centres(pos_ref), OWN_ROWS)
-    fill_filter(rhs, rot, we_ref, be_ref)
-    fill_change(change, middle, pos_ref, reach, rot, other, we_ref)
-    sum_ref[...] = pair_loop(OWN_ROWS, 1, table, edges, rhs, times, change, middle, partial)
+    fill_edges(edges, placed_rows(own.astype(F32), pos_ref), centres(pos_ref), OWN_ROWS)
+    fill_filter(rhs, entries(frame_ref), we_ref, be_ref)
+
+    def step(a, carry):
+        share = times[a].astype(BF)
+        for w in range(WIDTH // TILE):
+            span = slice(w * TILE, (w + 1) * TILE)
+            for g in range(GROUPS):
+                lo, hi = OWN_ROWS[g // 2]
+                weighted = table[lo:hi, span] * share[lo:hi, g : g + 1]
+                gate = gated(dot(edges[OWN_AT[g] : OWN_AT[g + 1], :], rhs[a, :, span]))
+                keep(partial, a, g, GROUPS, w, total_of(cut(gate * weighted)))
+        return carry
+
+    lax.fori_loop(0, GROUP, step, 0)
+    sum_ref[...] = collect(partial, HALF)
 
 
 def last_kernel(
     pay_ref,
     sum_ref,
-    ghost_ref,
+    total_ref,
+    table,
+    edges,
     feat_ref,
     pos_ref,
     frame_ref,
-    other_ref,
     we_ref,
     be_ref,
     wm_ref,
@@ -271,23 +276,54 @@
     wr_ref,
     wh_ref,
     out_ref,
-    edges,
+    ghosts,
     rhs,
+    rhs_other,
     times,
-    change,
-    middle,
     partial,
 ):
-    rot, other = entries(frame_ref), entries(other_ref)
+    rot = entries(frame_ref)
     extra = pay_ref[:, WIDTH:]
+    head = extra[0:1, :].astype(F32)
+    other = []
+    for a in range(3):
+        other.append([])
+        for c in range(3):
+            k = 8 + 3 * a + c
+            other[a].append(head[:, k : k + 1] + head[:, k + 16 : k + 17] + head[:, k + 32 : k + 33])
     reach = [dot(extra, pick(iota((EXTRA, EXTRA), 0) == c)) for c in range(3)]
-    fill_times(times, ghost_ref[...])
-    fill_edges(edges, reach, centres(pos_ref), GHOST_ROWS)
+    fill_times(times, total_ref[...])
+    fill_edges(ghosts, reach, centres(pos_ref), GHOST_ROWS)
     fill_filter(rhs, rot, we_ref, be_ref)
-    fill_change(change, middle, pos_ref, reach, rot, other, we_ref)
-    total = pair_loop(GHOST_ROWS, GROUPS, pay_ref, edges, rhs, times, change, middle, partial)
-
-    msg = ((total + sum_ref[...]) * message_scale).astype(BF)
+    fill_filter(rhs_other, other, we_ref, be_ref)
+
+    def step(a, carry):
+        share = times[a].astype(BF)
+        for w in range(WIDTH // TILE):
+            span = slice(w * TILE, (w + 1) * TILE)
+            near = gated(dot(ghosts[...], rhs[a, :, span]))
+            far = gated(dot(ghosts[...], rhs_other[a, :, span]))
+            for g in range(GROUPS):
+                lo, hi = GHOST_ROWS[g // 2]
+                weighted = pay_ref[lo:hi, span] * share[lo:hi, g : g + 1]
+                rows = slice(GHOST_AT[g], GHOST_AT[g + 1])
+                keep(partial, a, g, 2 * GROUPS, w, total_of(cut(near[rows] * weighted)))
+                parts = cut(far[rows] * weighted)
+                lo, hi = OWN_ROWS[g // 2]
+                weighted = table[lo:hi, span] * share[CAP + lo : CAP + hi, g : g + 1]
+                gate = gated(dot(edges[OWN_AT[g] : OWN_AT[g + 1], :], rhs_other[a, :, span]))
+                parts = parts + cut(gate * weighted)
+                keep(partial, a, GROUPS + g, 2 * GROUPS, w, total_of(parts))
+        return carry
+
+    lax.fori_loop(0, GROUP, step, 0)
+    total = collect(partial, ATOMS)
+    before = [
+        piece
+        for a in range(GROUP)
+        for piece in (sum_ref[a * GROUPS : (a + 1) * GROUPS, :], jnp.zeros((GROUPS, WIDTH), F32))
+    ]
+    msg = ((total + jnp.concatenate(before, axis=0)) * message_scale).astype(BF)
     row = iota((ATOMS, ATOMS), 0)
     lane = iota((ATOMS, ATOMS), 1)
     row_atom = (row % GROUPS) * GROUP + row // 16
@@ -312,15 +348,8 @@
     out_ref[...] = out
 
 
-def scratch(rows, edge_rows):
-    return [
-        pltpu.VMEM((edge_rows, ATOMS), BF),
-        pltpu.VMEM((GROUP, ATOMS, WIDTH), BF),
-        pltpu.VMEM((GROUP, rows, ATOMS), F32),
-        pltpu.VMEM((rows, WIDTH), BF),
-        pltpu.VMEM((HALF, WIDTH), F32),
-        pltpu.VMEM((WIDTH // 128, ATOMS * 8, 128), F32),
-    ]
+def cost(microseconds):
+    return pl.CostEstimate(flops=microseconds * 10**9, bytes_accessed=microseconds * 10**6, transcendentals=0)
 
 
 def local_step(
@@ -340,11 +369,11 @@
     dom_count = lax.axis_size("dom")
     frame_count = lax.axis_size("frame")
     frame = jnp.transpose(frames, (1, 0, 2))
-    other = lax.ppermute(frame, "frame", [(f, f ^ 1) for f in range(frame_count)])
     payload = pl.pallas_call(
         pack_kernel,
         out_shape=jax.ShapeDtypeStruct((CAP, PAY), BF),
-    )(features, positions, send_rows)
+        cost_estimate=cost(2),
+    )(features, positions, send_rows, frame)
     pairs = []
     for d in range(dom_count):
         for f in range(frame_count):
@@ -352,31 +381,43 @@
             pairs.append((d * frame_count + f, to * frame_count + (f ^ 1)))
     ghosts = lax.ppermute(payload, ("dom", "frame"), pairs)
     bias = b_edge.reshape(1, WIDTH)
-    own_rows = 2 * sum(hi - lo for lo, hi in OWN_ROWS)
-    ghost_rows = 2 * sum(hi - lo for lo, hi in GHOST_ROWS)
-    own_sum, ghost_times = pl.pallas_call(
+    own_sum, total, table, edges = pl.pallas_call(
         own_kernel,
         out_shape=[
-            jax.ShapeDtypeStruct((ATOMS, WIDTH), F32),
-            jax.ShapeDtypeStruct((CAP, ATOMS), BF),
+            jax.ShapeDtypeStruct((HALF, WIDTH), F32),
+            jax.ShapeDtypeStruct((TABLE, ATOMS), BF),
+            jax.ShapeDtypeStruct((ATOMS, WIDTH), BF),
+            jax.ShapeDtypeStruct((OWN_AT[-1], ATOMS), BF),
         ],
-        scratch_shapes=[pltpu.VMEM((ATOMS, WIDTH), BF)] + scratch(ATOMS, own_rows),
+        scratch_shapes=[
+            pltpu.VMEM((GROUP, ATOMS, WIDTH), BF),
+            pltpu.VMEM((GROUP, ATOMS, ATOMS), F32),
+            pltpu.VMEM((WIDTH // 128, HALF * 8, 128), F32),
+        ],
         compiler_params=pltpu.CompilerParams(vmem_limit_bytes=24 << 20),
-        cost_estimate=pl.CostEstimate(flops=2_000_000_000, bytes_accessed=1_000_000, transcendentals=7_000_000),
-    )(features, positions, neighbours, counts.reshape(1, ATOMS), frame, other, w_edge, bias)
+        cost_estimate=cost(5),
+    )(features, positions, neighbours, counts.reshape(1, ATOMS), frame, w_edge, bias)
     part = pl.pallas_call(
         last_kernel,
         out_shape=jax.ShapeDtypeStruct((4, ATOMS), F32),
-        scratch_shapes=scratch(CAP, ghost_rows),
+        scratch_shapes=[
+            pltpu.VMEM((GHOST_AT[-1], ATOMS), BF),
+            pltpu.VMEM((GROUP, ATOMS, WIDTH), BF),
+            pltpu.VMEM((GROUP, ATOMS, WIDTH), BF),
+            pltpu.VMEM((GROUP, TABLE, ATOMS), F32),
+            pltpu.VMEM((WIDTH // 128, ATOMS * 8, 128), F32),
+        ],
         compiler_params=pltpu.CompilerParams(vmem_limit_bytes=24 << 20),
+        cost_estimate=cost(7),
     )(
         ghosts,
         own_sum,
-        ghost_times,
+        total,
+        table,
+        edges,
         features,
         positions,
         frame,
-        other,
         w_edge,
         bias,
         w_message,

time: 36.8 us -> 33.8 us (0.918)
  local copies, waits for them, and re-layouts: 2.84 us -> 0.7 us
  Pallas kernels: 14.5 us -> 14.1 us
    pallas_call x2, Pallas kernels: 9.72 us -> 7.04 us  [the longest x1 5.2 us: local_step(): pl.pallas_call(own_kernel, out_shape=[jax.ShapeDtypeStruct((HALF, WIDTH),...]
    pallas_call x1, Pallas kernels: 4.8 us -> 7.04 us  [local_step(): pl.pallas_call(last_kernel, out_shape=jax.ShapeDtypeStruct((4, ATOMS), F3...]
    unnamed x22, local copies, waits for them, and re-layouts: 2.84 us -> 0.7 us
    ppermute x1 -> x0, starting transfers between devices: 1.58 us -> none  [local_step(): lax.ppermute(frame, 'frame', [(f, f ^ 1) for f in range(frame_count)])]
    ppermute x1, starting transfers between devices: 6.47 us -> 7.87 us  [local_step(): ghosts = lax.ppermute(payload, ('dom', 'frame'), pairs)]
  transfers between devices with their start and end apart: 2 -> 1, of which waited for: 0 -> 0; matrix products, arithmetic and copies ran while one was open for 0% -> 0% of each run, Pallas kernels for 27% -> 15%
where the time goes in v3:
time: 33.8 us; the launch traced here: 33.6 us
  Pallas kernels  14.1 us (42%)
  blocking collectives  10.2 us (30%)
  starting transfers between devices  7.87 us (23%)
  local copies, waits for them, and re-layouts  0.7 us (2%)
  other arithmetic  0.6 us (2%)
    all_to_all x1, blocking collectives, local_step(): lax.all_to_all(copies, 'frame', split_axis=0, concat_axis=0, tiled=True)  10.2 us
    ppermute x1, starting transfers between devices, local_step(): ghosts = lax.ppermute(payload, ('dom', 'frame'), pairs)  7.87 us
    pallas_call x1, Pallas kernels, local_step(): pl.pallas_call(last_kernel, out_shape=jax.ShapeDtypeStruct((4, ATOMS), F3...  7.04 us
    pallas_call x1, Pallas kernels, local_step(): pl.pallas_call(own_kernel, out_shape=[jax.ShapeDtypeStruct((HALF, WIDTH),...  5.2 us
    pallas_call x1, Pallas kernels, local_step(): pl.pallas_call(pack_kernel, out_shape=jax.ShapeDtypeStruct((CAP, PAY), BF...  1.84 us
    unnamed x22, local copies, waits for them, and re-layouts  0.7 us
  transfers between devices with their start and end apart: 1, of which 0 were waited for; matrix products, arithmetic and copies ran while one was open for 0% of the time, Pallas kernels for 15%

profile of v3, /device:TPU:2, one launch (start us, length us, event | category | flops | bytes accessed | tf_op | source)
XLA Modules:
  0.0 33.6 jit_solution(12941289465385282258)
XLA Ops:
  0.0 0.0 copy-start.3
  0.0 0.0 copy-start.4
  0.0 0.0 copy-start.5
  0.0 0.0 copy-start.9
  0.0 0.0 copy-start.10
  0.0 1.8 %shard_map.118 = bf16[64,640]{1,0:T(8,128)(2,1)} custom-call(bf16[128,512]{1,0:T(8,128)(2,1)} %feat_ref.5, bf16[3,128]{1,0:T(4,128)(2,1)} %pos_ref.5, s32[1,2,64]{2,1,0:T(2,128)} %rows_ref.1, f32[3,1,3]{2,1,0:T(1,128)} %bitcast.7), custom_call_target="tpu_custom_call" | custom-call | flops 2000000000 | bytes 2000000 | tf_op jit(solution)/shard_map/pallas_call | solution.py:372
  1.9 0.0 copy-start.7
  1.9 0.0 copy-start.8
  1.9 7.9 %collective-permute-start = (bf16[64,640]{1,0:T(8,128)(2,1)}, bf16[64,640]{1,0:T(8,128)(2,1)S(1)}, u32[]{:S(2)}, u32[]{:S(2)}) collective-permute-start(bf16[64,640]{1,0:T(8,128)(2,1)} %shard_map.118), channel_id=1, source_target_pairs={{0,249},{1,8},{2,251},{3,10},{4,253},{5,12},{6,255},{7,14},{8,1},{... | collective-permute-start | bytes 245768 | tf_op jit(solution)/shard_map/ppermute | solution.py:382
  9.7 0.0 copy-done.3
  9.8 0.0 copy-done.4
  9.8 0.0 copy-done.5
  9.8 0.0 copy-done.9
  9.8 0.0 copy-done.10
  9.8 0.0 copy-done.7
  9.8 0.0 copy-done.8
  9.8 0.0 copy-start
  9.8 0.0 copy-start.1
  9.8 0.0 copy-start.2
  9.8 5.2 %shard_map.119 = (f32[64,512]{1,0:T(8,128)S(1)}, bf16[192,128]{1,0:T(8,128)(2,1)S(1)}, bf16[128,512]{1,0:T(8,128)(2,1)S(1)}, bf16[800,128]{1,0:T(8,128)(2,1)S(1)}) custom-call(bf16[128,512]{1,0:T(8,128)(2,1)S(1)} %copy-done.3, bf16[3,128]{1,0:T(4,128)(2,1)S(1)} %copy-done.9, s32[128,128]{1,0:T(8,128)S(1)} %copy-done.4, s32[1,128]{1,0:T(1,128)S(1)} %bitcast.10, ...), custom_call_target="tpu_custom_call" | custom-call | flops 5000000000 | bytes 5000000 | tf_op jit(solution)/shard_map/pallas_call | solution.py:384
  15.0 0.0 collective-permute-done.pay_ref
  15.0 0.0 copy-start.6
  15.1 0.0 copy-done
  15.1 0.0 copy-done.1
  15.1 0.0 copy-done.2
  15.1 0.6 %copy-done.6 = bf16[512,4]{0,1:T(4,128)(2,1)S(1)} copy-done((bf16[512,4]{0,1:T(4,128)(2,1)S(1)}, bf16[512,4]{0,1:T(4,128)(2,1)}, u32[]{:S(2)}) %copy-start.6) | copy-done | bytes 4120
  15.7 7.0 %shard_map.120 = f32[4,128]{1,0:T(4,128)S(1)} custom-call(bf16[64,640]{1,0:T(8,128)(2,1)S(1)} %collective-permute-done.pay_ref, f32[64,512]{1,0:T(8,128)S(1)} %get-tuple-element.9.sum_ref, bf16[192,128]{1,0:T(8,128)(2,1)S(1)} %get-tuple-element.10.total_ref, bf16[128,512]{1,0:T(8,128)(2,1)S(1)} %get-tuple-element.11.table, ...), custom_call_target="tpu_custom_call" | custom-call | flops 7000000000 | bytes 7000000 | tf_op jit(solution)/shard_map/pallas_call | solution.py:400
  22.8 10.2 %all_to_all.5 = f32[8,4,128]{2,1,0:T(4,128)S(1)} all-to-all(f32[8,4,128]{2,1,0:T(4,128)S(1)} %broadcast_in_dim.3), channel_id=1, replica_groups=mesh['dom'=32,'frame'=8] {'frame'}, dimensions={0} | all-to-all | bytes 32768 | tf_op jit(solution)/shard_map/all_to_all | solution.py:429
  33.0 0.6 %broadcast_multiply_fusion = f32[4,128]{1,0:T(4,128)} fusion(f32[4,128]{1,0:T(4,128)S(1)} %reduce_sum.9), kind=kLoop, calls=%fused_computation | loop fusion | flops 512 | bytes 4096 | tf_op jit(solution)/shard_map/div | solution.py:430
  (2 shorter events, 0.0 us)
Async XLA Ops:
  0.0 9.8 %copy-start.3 = (bf16[128,512]{1,0:T(8,128)(2,1)S(1)}, bf16[128,512]{1,0:T(8,128)(2,1)}, u32[]{:S(2)}) copy-start(bf16[128,512]{1,0:T(8,128)(2,1)} %feat_ref.5) | copy-start | bytes 393220
  0.0 9.8 %copy-start.4 = (s32[128,128]{1,0:T(8,128)S(1)}, s32[128,128]{1,0:T(8,128)}, u32[]{:S(2)}) copy-start(s32[128,128]{1,0:T(8,128)} %nbr_ref.1) | copy-start | bytes 196612
  0.0 9.8 %copy-start.5 = (f32[9,512]{1,0:T(8,128)S(1)}, f32[9,512]{1,0:T(8,128)}, u32[]{:S(2)}) copy-start(f32[9,512]{1,0:T(8,128)} %we_ref.3) | copy-start | bytes 55300
  0.0 9.7 %copy-start.9 = (bf16[3,128]{1,0:T(4,128)(2,1)S(1)}, bf16[3,128]{1,0:T(4,128)(2,1)}, u32[]{:S(2)}) copy-start(bf16[3,128]{1,0:T(4,128)(2,1)} %pos_ref.5) | copy-start | bytes 2308
  0.0 9.7 %copy-start.10 = (s32[128]{0:T(128)S(1)}, s32[128]{0:T(128)}, u32[]{:S(2)}) copy-start(s32[128]{0:T(128)} %param.15) | copy-start | bytes 1540
  1.9 7.9 %copy-start.7 = (f32[512]{0:T(512)S(1)}, f32[512]{0:T(512)}, u32[]{:S(2)}) copy-start(f32[512]{0:T(512)} %param.19) | copy-start | bytes 6148
  1.9 7.9 %copy-start.8 = (f32[1,3,3]{2,0,1:T(1,128)S(1)}, f32[1,3,3]{2,0,1:T(1,128)}, u32[]{:S(2)}) copy-start(f32[1,3,3]{2,0,1:T(1,128)} %param.17) | copy-start | bytes 112
  1.9 13.2 %collective-permute-start = (bf16[64,640]{1,0:T(8,128)(2,1)}, bf16[64,640]{1,0:T(8,128)(2,1)S(1)}, u32[]{:S(2)}, u32[]{:S(2)}) collective-permute-start(bf16[64,640]{1,0:T(8,128)(2,1)} %shard_map.118), channel_id=1, source_target_pairs={{0,249},{1,8},{2,251},{3,10},{4,253},{5,12},{6,255},{7,14},{8,1},{... | collective-permute-start | bytes 245768 | tf_op jit(solution)/shard_map/ppermute | solution.py:382
  9.8 5.3 %copy-start = (bf16[512,512]{1,0:T(8,128)(2,1)S(1)}, bf16[512,512]{1,0:T(8,128)(2,1)}, u32[]{:S(2)}) copy-start(bf16[512,512]{1,0:T(8,128)(2,1)} %wm_ref.1) | copy-start | bytes 1572868
  9.8 5.3 %copy-start.1 = (bf16[512,512]{1,0:T(8,128)(2,1)S(1)}, bf16[512,512]{1,0:T(8,128)(2,1)}, u32[]{:S(2)}) copy-start(bf16[512,512]{1,0:T(8,128)(2,1)} %wu_ref.1) | copy-start | bytes 1572868
  9.8 5.3 %copy-start.2 = (bf16[512,512]{1,0:T(8,128)(2,1)S(1)}, bf16[512,512]{1,0:T(8,128)(2,1)}, u32[]{:S(2)}) copy-start(bf16[512,512]{1,0:T(8,128)(2,1)} %wr_ref.1) | copy-start | bytes 1572868
  15.0 0.7 %copy-start.6 = (bf16[512,4]{0,1:T(4,128)(2,1)S(1)}, bf16[512,4]{0,1:T(4,128)(2,1)}, u32[]{:S(2)}) copy-start(bf16[512,4]{0,1:T(4,128)(2,1)} %param.23) | copy-start | bytes 12292

commit v4 on v3

--- a/solution.py
+++ b/solution.py
@@ -49,7 +49,7 @@
 
 
 def parity():
-    return lax.axis_index("frame") % 2
+    return lax.axis_index("frame") // (lax.axis_size("frame") // 2)
 
 
 def local(n):
@@ -211,8 +211,10 @@
     frame_ref,
     we_ref,
     be_ref,
+    wh_ref,
     sum_ref,
     total_ref,
+    wh_out,
     table,
     edges,
     rhs,
@@ -241,6 +243,7 @@
     for k in range(SLOTS // 2):
         total = jnp.where(place == folded[k : k + 1, :], total + one, total)
     total_ref[...] = total
+    wh_out[...] = wh_ref[...]
     fill_times(times, total[CAP:])
     fill_edges(edges, placed_rows(own.astype(F32), pos_ref), centres(pos_ref), OWN_ROWS)
     fill_filter(rhs, entries(frame_ref), we_ref, be_ref)
@@ -377,15 +380,16 @@
     pairs = []
     for d in range(dom_count):
         for f in range(frame_count):
-            to = (d + 1) % dom_count if f % 2 else (d - 1) % dom_count
-            pairs.append((d * frame_count + f, to * frame_count + (f ^ 1)))
+            to = (d + 1) % dom_count if f >= frame_count // 2 else (d - 1) % dom_count
+            pairs.append((d * frame_count + f, to * frame_count + (f + frame_count // 2) % frame_count))
     ghosts = lax.ppermute(payload, ("dom", "frame"), pairs)
     bias = b_edge.reshape(1, WIDTH)
-    own_sum, total, table, edges = pl.pallas_call(
+    own_sum, total, heads, table, edges = pl.pallas_call(
         own_kernel,
         out_shape=[
             jax.ShapeDtypeStruct((HALF, WIDTH), F32),
             jax.ShapeDtypeStruct((TABLE, ATOMS), BF),
+            jax.ShapeDtypeStruct((4, WIDTH), BF),
             jax.ShapeDtypeStruct((ATOMS, WIDTH), BF),
             jax.ShapeDtypeStruct((OWN_AT[-1], ATOMS), BF),
         ],
@@ -396,7 +400,7 @@
         ],
         compiler_params=pltpu.CompilerParams(vmem_limit_bytes=24 << 20),
         cost_estimate=cost(5),
-    )(features, positions, neighbours, counts.reshape(1, ATOMS), frame, w_edge, bias)
+    )(features, positions, neighbours, counts.reshape(1, ATOMS), frame, w_edge, bias, w_heads.T)
     part = pl.pallas_call(
         last_kernel,
         out_shape=jax.ShapeDtypeStruct((4, ATOMS), F32),
@@ -423,7 +427,7 @@
         w_message,
         w_update,
         w_readout,
-        w_heads.T,
+        heads,
     )
     copies = jnp.broadcast_to(part, (frame_count, *part.shape))
     everything = lax.all_to_all(copies, "frame", split_axis=0, concat_axis=0, tiled=True)

time: 33.8 us -> 32.9 us (0.973)
  starting transfers between devices: 7.87 us -> 0.01 us
  blocking collectives: 10.2 us -> 17.1 us
    ppermute x1, starting transfers between devices: 7.87 us -> 0.01 us  [local_step(): ghosts = lax.ppermute(payload, ('dom', 'frame'), pairs)]
    all_to_all x1, blocking collectives: 10.2 us -> 17.1 us  [local_step(): lax.all_to_all(copies, 'frame', split_axis=0, concat_axis=0, tiled=True)]
  transfers between devices with their start and end apart: 1 -> 1, of which waited for: 0 -> 0; matrix products, arithmetic and copies ran while one was open for 0% -> 0% of each run, Pallas kernels for 15% -> 16%
where the time goes in v4:
time: 32.9 us; the launch traced here: 32.8 us
  blocking collectives  17.1 us (52%)
  Pallas kernels  14.3 us (43%)
  local copies, waits for them, and re-layouts  0.67 us (2%)
  other arithmetic  0.6 us (2%)
    all_to_all x1, blocking collectives, local_step(): lax.all_to_all(copies, 'frame', split_axis=0, concat_axis=0, tiled=True)  17.1 us
    pallas_call x1, Pallas kernels, local_step(): pl.pallas_call(last_kernel, out_shape=jax.ShapeDtypeStruct((4, ATOMS), F3...  7.19 us
    pallas_call x1, Pallas kernels, local_step(): pl.pallas_call(own_kernel, out_shape=[jax.ShapeDtypeStruct((HALF, WIDTH),...  5.25 us
    pallas_call x1, Pallas kernels, local_step(): pl.pallas_call(pack_kernel, out_shape=jax.ShapeDtypeStruct((CAP, PAY), BF...  1.86 us
    unnamed x22, local copies, waits for them, and re-layouts  0.66 us
  transfers between devices with their start and end apart: 1, of which 0 were waited for; matrix products, arithmetic and copies ran while one was open for 0% of the time, Pallas kernels for 16%

profile of v4, /device:TPU:2, one launch (start us, length us, event | category | flops | bytes accessed | tf_op | source)
XLA Modules:
  0.0 32.8 jit_solution(8521557288178110164)
XLA Ops:
  0.0 0.0 copy-start.3
  0.0 0.0 copy-start.4
  0.0 0.0 copy-start.5
  0.0 0.0 copy-start.7
  0.0 0.0 copy-start.9
  0.0 0.0 copy-start.10
  0.0 1.9 %shard_map.118 = bf16[64,640]{1,0:T(8,128)(2,1)} custom-call(bf16[128,512]{1,0:T(8,128)(2,1)} %feat_ref.5, bf16[3,128]{1,0:T(4,128)(2,1)} %pos_ref.5, s32[1,2,64]{2,1,0:T(2,128)} %rows_ref.1, f32[3,1,3]{2,1,0:T(1,128)} %bitcast.7), custom_call_target="tpu_custom_call" | custom-call | flops 2000000000 | bytes 2000000 | tf_op jit(solution)/shard_map/pallas_call | solution.py:375
  1.9 0.0 copy-start.6
  1.9 0.0 collective-permute-start
  1.9 0.0 copy-start.8
  1.9 0.0 copy-done.3
  1.9 0.0 copy-done.4
  1.9 0.0 copy-done.5
  1.9 0.0 copy-done.7
  1.9 0.0 copy-done.9
  2.0 0.0 copy-done.10
  2.0 0.6 %copy-done.6 = bf16[512,4]{0,1:T(4,128)(2,1)S(1)} copy-done((bf16[512,4]{0,1:T(4,128)(2,1)S(1)}, bf16[512,4]{0,1:T(4,128)(2,1)}, u32[]{:S(2)}) %copy-start.6) | copy-done | bytes 4120
  2.6 0.0 copy-done.8
  2.6 0.0 copy-start
  2.6 0.0 copy-start.1
  2.6 0.0 copy-start.2
  2.6 5.3 %shard_map.119 = (f32[64,512]{1,0:T(8,128)S(1)}, bf16[192,128]{1,0:T(8,128)(2,1)S(1)}, bf16[4,512]{1,0:T(4,128)(2,1)S(1)}, bf16[128,512]{1,0:T(8,128)(2,1)S(1)}, bf16[800,128]{1,0:T(8,128)(2,1)S(1)}) custom-call(bf16[128,512]{1,0:T(8,128)(2,1)S(1)} %copy-done.3, bf16[3,128]{1,0:T(4,128)(2,1)S(1)} %copy-done.9, s32[128,128]{1,0:T(8,128)S(1)} %copy-done.4, ...), custom_call_target="tpu_custom_call" | custom-call | flops 5000000000 | bytes 5000000 | tf_op jit(solution)/shard_map/pallas_call | solution.py:387
  7.9 0.0 collective-permute-done.pay_ref
  7.9 0.0 copy-done
  7.9 0.0 copy-done.1
  7.9 0.0 copy-done.2
  7.9 7.2 %shard_map.120 = f32[4,128]{1,0:T(4,128)S(1)} custom-call(bf16[64,640]{1,0:T(8,128)(2,1)S(1)} %collective-permute-done.pay_ref, f32[64,512]{1,0:T(8,128)S(1)} %get-tuple-element.10.sum_ref, bf16[192,128]{1,0:T(8,128)(2,1)S(1)} %get-tuple-element.11.total_ref, bf16[128,512]{1,0:T(8,128)(2,1)S(1)} %get-tuple-element.12.table, ...), custom_call_target="tpu_custom_call" | custom-call | flops 7000000000 | bytes 7000000 | tf_op jit(solution)/shard_map/pallas_call | solution.py:404
  15.1 17.1 %all_to_all.5 = f32[8,4,128]{2,1,0:T(4,128)S(1)} all-to-all(f32[8,4,128]{2,1,0:T(4,128)S(1)} %broadcast_in_dim.3), channel_id=1, replica_groups=mesh['dom'=32,'frame'=8] {'frame'}, dimensions={0} | all-to-all | bytes 32768 | tf_op jit(solution)/shard_map/all_to_all | solution.py:433
  32.2 0.6 %broadcast_multiply_fusion = f32[4,128]{1,0:T(4,128)} fusion(f32[4,128]{1,0:T(4,128)S(1)} %reduce_sum.9), kind=kLoop, calls=%fused_computation | loop fusion | flops 512 | bytes 4096 | tf_op jit(solution)/shard_map/div | solution.py:434
  (2 shorter events, 0.0 us)
Async XLA Ops:
  0.0 1.9 %copy-start.3 = (bf16[128,512]{1,0:T(8,128)(2,1)S(1)}, bf16[128,512]{1,0:T(8,128)(2,1)}, u32[]{:S(2)}) copy-start(bf16[128,512]{1,0:T(8,128)(2,1)} %feat_ref.5) | copy-start | bytes 393220
  0.0 1.9 %copy-start.4 = (s32[128,128]{1,0:T(8,128)S(1)}, s32[128,128]{1,0:T(8,128)}, u32[]{:S(2)}) copy-start(s32[128,128]{1,0:T(8,128)} %nbr_ref.1) | copy-start | bytes 196612
  0.0 1.9 %copy-start.5 = (f32[9,512]{1,0:T(8,128)S(1)}, f32[9,512]{1,0:T(8,128)}, u32[]{:S(2)}) copy-start(f32[9,512]{1,0:T(8,128)} %we_ref.3) | copy-start | bytes 55300
  0.0 1.9 %copy-start.7 = (f32[512]{0:T(512)S(1)}, f32[512]{0:T(512)}, u32[]{:S(2)}) copy-start(f32[512]{0:T(512)} %param.19) | copy-start | bytes 6148
  0.0 1.9 %copy-start.9 = (bf16[3,128]{1,0:T(4,128)(2,1)S(1)}, bf16[3,128]{1,0:T(4,128)(2,1)}, u32[]{:S(2)}) copy-start(bf16[3,128]{1,0:T(4,128)(2,1)} %pos_ref.5) | copy-start | bytes 2308
  0.0 1.9 %copy-start.10 = (s32[128]{0:T(128)S(1)}, s32[128]{0:T(128)}, u32[]{:S(2)}) copy-start(s32[128]{0:T(128)} %param.15) | copy-start | bytes 1540
  1.9 0.7 %copy-start.6 = (bf16[512,4]{0,1:T(4,128)(2,1)S(1)}, bf16[512,4]{0,1:T(4,128)(2,1)}, u32[]{:S(2)}) copy-start(bf16[512,4]{0,1:T(4,128)(2,1)} %param.23) | copy-start | bytes 12292
  1.9 6.0 %collective-permute-start = (bf16[64,640]{1,0:T(8,128)(2,1)}, bf16[64,640]{1,0:T(8,128)(2,1)S(1)}, u32[]{:S(2)}, u32[]{:S(2)}) collective-permute-start(bf16[64,640]{1,0:T(8,128)(2,1)} %shard_map.118), channel_id=1, source_target_pairs={{0,252},{1,253},{2,254},{3,255},{4,8},{5,9},{6,10},{7,11},{8,4},{9... | collective-permute-start | bytes 245768 | tf_op jit(solution)/shard_map/ppermute | solution.py:385
  1.9 0.7 %copy-start.8 = (f32[1,3,3]{2,0,1:T(1,128)S(1)}, f32[1,3,3]{2,0,1:T(1,128)}, u32[]{:S(2)}) copy-start(f32[1,3,3]{2,0,1:T(1,128)} %param.17) | copy-start | bytes 112
  2.6 5.3 %copy-start = (bf16[512,512]{1,0:T(8,128)(2,1)S(1)}, bf16[512,512]{1,0:T(8,128)(2,1)}, u32[]{:S(2)}) copy-start(bf16[512,512]{1,0:T(8,128)(2,1)} %wm_ref.1) | copy-start | bytes 1572868
  2.6 5.3 %copy-start.1 = (bf16[512,512]{1,0:T(8,128)(2,1)S(1)}, bf16[512,512]{1,0:T(8,128)(2,1)}, u32[]{:S(2)}) copy-start(bf16[512,512]{1,0:T(8,128)(2,1)} %wu_ref.1) | copy-start | bytes 1572868
  2.6 5.3 %copy-start.2 = (bf16[512,512]{1,0:T(8,128)(2,1)S(1)}, bf16[512,512]{1,0:T(8,128)(2,1)}, u32[]{:S(2)}) copy-start(bf16[512,512]{1,0:T(8,128)(2,1)} %wr_ref.1) | copy-start | bytes 1572868

commit v5 on v4

--- a/solution.py
+++ b/solution.py
@@ -111,7 +111,7 @@
 def fill_times(times, total):
     for a in range(GROUP):
         spread = pick(iota((ATOMS, ATOMS), 0) % HALF == iota((ATOMS, ATOMS), 1) * GROUP + a)
-        times[a, :, :] = dot(total, spread)
+        times[a, :, :] = dot(total, spread).astype(BF)
 
 
 def sum_rows(prod, rows):
@@ -126,7 +126,7 @@
     return total[:8] + total[8:]
 
 
-SUMS = 2
+SUMS = 1
 
 
 def offsets_of(bounds):
@@ -177,7 +177,57 @@
     return jnp.concatenate(tiles, axis=1)
 
 
-def pack_kernel(feat_ref, pos_ref, rows_ref, frame_ref, out_ref):
+def early():
+    return lax.axis_index("dom") == 0
+
+
+def sum_own(table, edges, rhs, times, partial, sum_ref):
+    def step(a, carry):
+        share = times[a]
+        for w in range(WIDTH // TILE):
+            span = slice(w * TILE, (w + 1) * TILE)
+            for first in range(0, GROUPS, 2):
+                pre = dot(edges[OWN_AT[first] : OWN_AT[first + 2], :], rhs[a, :, span]).astype(BF)
+                for g in range(first, first + 2):
+                    lo, hi = OWN_ROWS[g // 2]
+                    weighted = table[lo:hi, span] * share[lo:hi, g : g + 1]
+                    gate = gated(pre[OWN_AT[g] - OWN_AT[first] : OWN_AT[g + 1] - OWN_AT[first]])
+                    keep(partial, a, g, GROUPS, w, total_of(cut(gate * weighted)))
+        return carry
+
+    lax.fori_loop(0, GROUP, step, 0)
+    sum_ref[...] = collect(partial, HALF)
+
+
+def first_kernel(
+    feat_ref,
+    pos_ref,
+    rows_ref,
+    frame_ref,
+    nbr_ref,
+    cnt_ref,
+    we_ref,
+    be_ref,
+    wh_ref,
+    pay_ref,
+    sum_ref,
+    total_ref,
+    table,
+    edges,
+    rhs,
+    times,
+    pos_out,
+    frame_out,
+    we_out,
+    be_out,
+    wh_out,
+    partial,
+):
+    pos_out[...] = pos_ref[...]
+    frame_out[...] = frame_ref[...]
+    we_out[...] = we_ref[...]
+    be_out[...] = be_ref[...]
+    wh_out[...] = wh_ref[...]
     wanted = jnp.where(parity() == 1, rows_ref[0, 1:2, :], rows_ref[0, 0:1, :])
     row = iota((CAP, CAP), 0)
     source = jnp.where(parity() == 1, row, CAP - 1 - row)
@@ -185,7 +235,7 @@
         jnp.where(iota((CAP, CAP), 1) == source, wanted, 0).astype(F32), axis=1, keepdims=True
     ).astype(I32)
     chosen = pick(iota((CAP, ATOMS), 1) == column)
-    out_ref[:, :WIDTH] = dot(chosen, feat_ref[...]).astype(BF)
+    pay_ref[:, :WIDTH] = dot(chosen, feat_ref[...]).astype(BF)
     lane = iota((CAP, EXTRA), 1)
     rest = jnp.zeros((CAP, EXTRA), F32)
     for c in range(3):
@@ -200,27 +250,8 @@
     high, rest_of = split(turn)
     mid, low = split(rest_of)
     turn = jnp.where(lane < 24, high, jnp.where(lane < 40, mid, low))
-    out_ref[:, WIDTH:] = (rest + turn).astype(BF)
-
-
-def own_kernel(
-    feat_ref,
-    pos_ref,
-    nbr_ref,
-    cnt_ref,
-    frame_ref,
-    we_ref,
-    be_ref,
-    wh_ref,
-    sum_ref,
-    total_ref,
-    wh_out,
-    table,
-    edges,
-    rhs,
-    times,
-    partial,
-):
+    pay_ref[:, WIDTH:] = (rest + turn).astype(BF)
+
     own = pick(iota((ATOMS, ATOMS), 1) == local(iota((ATOMS, ATOMS), 0)))
     table[...] = dot(own, feat_ref[...]).astype(BF)
 
@@ -243,24 +274,23 @@
     for k in range(SLOTS // 2):
         total = jnp.where(place == folded[k : k + 1, :], total + one, total)
     total_ref[...] = total
-    wh_out[...] = wh_ref[...]
     fill_times(times, total[CAP:])
     fill_edges(edges, placed_rows(own.astype(F32), pos_ref), centres(pos_ref), OWN_ROWS)
     fill_filter(rhs, entries(frame_ref), we_ref, be_ref)
 
-    def step(a, carry):
-        share = times[a].astype(BF)
-        for w in range(WIDTH // TILE):
-            span = slice(w * TILE, (w + 1) * TILE)
-            for g in range(GROUPS):
-                lo, hi = OWN_ROWS[g // 2]
-                weighted = table[lo:hi, span] * share[lo:hi, g : g + 1]
-                gate = gated(dot(edges[OWN_AT[g] : OWN_AT[g + 1], :], rhs[a, :, span]))
-                keep(partial, a, g, GROUPS, w, total_of(cut(gate * weighted)))
-        return carry
-
-    lax.fori_loop(0, GROUP, step, 0)
-    sum_ref[...] = collect(partial, HALF)
+    @pl.when(early())
+    def _():
+        sum_own(table, edges, rhs, times, partial, sum_ref)
+
+
+def own_kernel(before_ref, table, edges, rhs, times, sum_ref, partial):
+    @pl.when(early())
+    def _():
+        sum_ref[...] = before_ref[...]
+
+    @pl.when(jnp.logical_not(early()))
+    def _():
+        sum_own(table, edges, rhs, times, partial, sum_ref)
 
 
 def last_kernel(
@@ -269,7 +299,8 @@
     total_ref,
     table,
     edges,
-    feat_ref,
+    rhs,
+    own_times,
     pos_ref,
     frame_ref,
     we_ref,
@@ -280,7 +311,6 @@
     wh_ref,
     out_ref,
     ghosts,
-    rhs,
     rhs_other,
     times,
     partial,
@@ -295,28 +325,30 @@
             k = 8 + 3 * a + c
             other[a].append(head[:, k : k + 1] + head[:, k + 16 : k + 17] + head[:, k + 32 : k + 33])
     reach = [dot(extra, pick(iota((EXTRA, EXTRA), 0) == c)) for c in range(3)]
-    fill_times(times, total_ref[...])
+    fill_times(times, total_ref[:CAP, :])
     fill_edges(ghosts, reach, centres(pos_ref), GHOST_ROWS)
-    fill_filter(rhs, rot, we_ref, be_ref)
     fill_filter(rhs_other, other, we_ref, be_ref)
 
     def step(a, carry):
-        share = times[a].astype(BF)
+        share = times[a]
+        own_share = own_times[a]
         for w in range(WIDTH // TILE):
             span = slice(w * TILE, (w + 1) * TILE)
             near = gated(dot(ghosts[...], rhs[a, :, span]))
             far = gated(dot(ghosts[...], rhs_other[a, :, span]))
-            for g in range(GROUPS):
-                lo, hi = GHOST_ROWS[g // 2]
-                weighted = pay_ref[lo:hi, span] * share[lo:hi, g : g + 1]
-                rows = slice(GHOST_AT[g], GHOST_AT[g + 1])
-                keep(partial, a, g, 2 * GROUPS, w, total_of(cut(near[rows] * weighted)))
-                parts = cut(far[rows] * weighted)
-                lo, hi = OWN_ROWS[g // 2]
-                weighted = table[lo:hi, span] * share[CAP + lo : CAP + hi, g : g + 1]
-                gate = gated(dot(edges[OWN_AT[g] : OWN_AT[g + 1], :], rhs_other[a, :, span]))
-                parts = parts + cut(gate * weighted)
-                keep(partial, a, GROUPS + g, 2 * GROUPS, w, total_of(parts))
+            for first in range(0, GROUPS, 2):
+                pre = dot(edges[OWN_AT[first] : OWN_AT[first + 2], :], rhs_other[a, :, span]).astype(BF)
+                for g in range(first, first + 2):
+                    lo, hi = GHOST_ROWS[g // 2]
+                    weighted = pay_ref[lo:hi, span] * share[lo:hi, g : g + 1]
+                    rows = slice(GHOST_AT[g], GHOST_AT[g + 1])
+                    keep(partial, a, g, 2 * GROUPS, w, total_of(cut(near[rows] * weighted)))
+                    parts = cut(far[rows] * weighted)
+                    lo, hi = OWN_ROWS[g // 2]
+                    weighted = table[lo:hi, span] * own_share[lo:hi, g : g + 1]
+                    gate = gated(pre[OWN_AT[g] - OWN_AT[first] : OWN_AT[g + 1] - OWN_AT[first]])
+                    parts = parts + cut(gate * weighted)
+                    keep(partial, a, GROUPS + g, 2 * GROUPS, w, total_of(parts))
         return carry
 
     lax.fori_loop(0, GROUP, step, 0)
@@ -330,7 +362,7 @@
     row = iota((ATOMS, ATOMS), 0)
     lane = iota((ATOMS, ATOMS), 1)
     row_atom = (row % GROUPS) * GROUP + row // 16
-    mine = dot(pick(lane == local(row_atom)), feat_ref[...])
+    mine = dot(pick(lane == row_atom), table[...])
 
     def silu(x):
         h = 0.5 * x
@@ -372,43 +404,61 @@
     dom_count = lax.axis_size("dom")
     frame_count = lax.axis_size("frame")
     frame = jnp.transpose(frames, (1, 0, 2))
-    payload = pl.pallas_call(
-        pack_kernel,
-        out_shape=jax.ShapeDtypeStruct((CAP, PAY), BF),
-        cost_estimate=cost(2),
-    )(features, positions, send_rows, frame)
+    bias = b_edge.reshape(1, WIDTH)
+    direct = [
+        pltpu.with_memory_space_constraint(x, pltpu.MemorySpace.HBM)
+        for x in (
+            features,
+            positions,
+            send_rows,
+            frame,
+            neighbours,
+            counts.reshape(1, ATOMS),
+            w_edge,
+            bias,
+            w_heads.T,
+        )
+    ]
+    payload, before, total, table, edges, rhs, times, *small, heads = pl.pallas_call(
+        first_kernel,
+        out_shape=[
+            pltpu.VMEM((CAP, PAY), BF),
+            pltpu.VMEM((HALF, WIDTH), F32),
+            pltpu.VMEM((TABLE, ATOMS), BF),
+            pltpu.VMEM((ATOMS, WIDTH), BF),
+            pltpu.VMEM((OWN_AT[-1], ATOMS), BF),
+            pltpu.VMEM((GROUP, ATOMS, WIDTH), BF),
+            pltpu.VMEM((GROUP, ATOMS, ATOMS), BF),
+            pltpu.VMEM(positions.shape, BF),
+            pltpu.VMEM(frame.shape, F32),
+            pltpu.VMEM(w_edge.shape, F32),
+            pltpu.VMEM(bias.shape, F32),
+            pltpu.VMEM((4, WIDTH), BF),
+        ],
+        scratch_shapes=[pltpu.VMEM((WIDTH // 128, HALF * 8, 128), F32)],
+        compiler_params=pltpu.CompilerParams(vmem_limit_bytes=24 << 20),
+        cost_estimate=cost(3),
+    )(*direct)
     pairs = []
     for d in range(dom_count):
         for f in range(frame_count):
             to = (d + 1) % dom_count if f >= frame_count // 2 else (d - 1) % dom_count
             pairs.append((d * frame_count + f, to * frame_count + (f + frame_count // 2) % frame_count))
     ghosts = lax.ppermute(payload, ("dom", "frame"), pairs)
-    bias = b_edge.reshape(1, WIDTH)
-    own_sum, total, heads, table, edges = pl.pallas_call(
+    own_sum = pl.pallas_call(
         own_kernel,
-        out_shape=[
-            jax.ShapeDtypeStruct((HALF, WIDTH), F32),
-            jax.ShapeDtypeStruct((TABLE, ATOMS), BF),
-            jax.ShapeDtypeStruct((4, WIDTH), BF),
-            jax.ShapeDtypeStruct((ATOMS, WIDTH), BF),
-            jax.ShapeDtypeStruct((OWN_AT[-1], ATOMS), BF),
-        ],
-        scratch_shapes=[
-            pltpu.VMEM((GROUP, ATOMS, WIDTH), BF),
-            pltpu.VMEM((GROUP, ATOMS, ATOMS), F32),
-            pltpu.VMEM((WIDTH // 128, HALF * 8, 128), F32),
-        ],
+        out_shape=pltpu.VMEM((HALF, WIDTH), F32),
+        scratch_shapes=[pltpu.VMEM((WIDTH // 128, HALF * 8, 128), F32)],
         compiler_params=pltpu.CompilerParams(vmem_limit_bytes=24 << 20),
-        cost_estimate=cost(5),
-    )(features, positions, neighbours, counts.reshape(1, ATOMS), frame, w_edge, bias, w_heads.T)
+        cost_estimate=cost(4),
+    )(before, table, edges, rhs, times)
     part = pl.pallas_call(
         last_kernel,
         out_shape=jax.ShapeDtypeStruct((4, ATOMS), F32),
         scratch_shapes=[
             pltpu.VMEM((GHOST_AT[-1], ATOMS), BF),
             pltpu.VMEM((GROUP, ATOMS, WIDTH), BF),
-            pltpu.VMEM((GROUP, ATOMS, WIDTH), BF),
-            pltpu.VMEM((GROUP, TABLE, ATOMS), F32),
+            pltpu.VMEM((GROUP, CAP, ATOMS), BF),
             pltpu.VMEM((WIDTH // 128, ATOMS * 8, 128), F32),
         ],
         compiler_params=pltpu.CompilerParams(vmem_limit_bytes=24 << 20),
@@ -419,11 +469,9 @@
         total,
         table,
         edges,
-        features,
-        positions,
-        frame,
-        w_edge,
-        bias,
+        rhs,
+        times,
+        *small,
         w_message,
         w_update,
         w_readout,

time: 32.9 us -> 30.5 us (0.927)
  blocking collectives: 17.1 us -> 12.9 us
  waiting for transfers between devices: 0.01 us -> 3.78 us
  Pallas kernels: 14.3 us -> 13 us
  local copies, waits for them, and re-layouts: 0.67 us -> 0.03 us
    all_to_all x1, blocking collectives: 17.1 us -> 12.9 us  [local_step(): lax.all_to_all(copies, 'frame', split_axis=0, concat_axis=0, tiled=True)]
    ppermute x1, waiting for transfers between devices: 0.01 us -> 3.78 us  [local_step(): ghosts = lax.ppermute(payload, ('dom', 'frame'), pairs)]
    pallas_call x2, Pallas kernels: 7.11 us -> 6.11 us  [the longest x1 6.08 us: local_step(): pl.pallas_call(first_kernel, out_shape=[pltpu.VMEM((CAP, PAY), BF), pltpu...]
    unnamed x22 -> x6, local copies, waits for them, and re-layouts: 0.66 us -> 0.02 us
    pallas_call x1, Pallas kernels: 7.19 us -> 6.85 us  [local_step(): pl.pallas_call(last_kernel, out_shape=jax.ShapeDtypeStruct((4, ATOMS), F3...]
  transfers between devices with their start and end apart: 1 -> 1, of which waited for: 0 -> 1; matrix products, arithmetic and copies ran while one was open for 0% -> 0% of each run, Pallas kernels for 16% -> 0%
where the time goes in v5:
time: 30.5 us; the launch traced here: 30.4 us
  Pallas kernels  13 us (43%)
  blocking collectives  12.9 us (42%)
  waiting for transfers between devices  3.78 us (12%)
  other arithmetic  0.6 us (2%)
    all_to_all x1, blocking collectives, local_step(): lax.all_to_all(copies, 'frame', split_axis=0, concat_axis=0, tiled=True)  12.9 us
    pallas_call x1, Pallas kernels, local_step(): pl.pallas_call(last_kernel, out_shape=jax.ShapeDtypeStruct((4, ATOMS), F3...  6.85 us
    pallas_call x1, Pallas kernels, local_step(): pl.pallas_call(first_kernel, out_shape=[pltpu.VMEM((CAP, PAY), BF), pltpu...  6.08 us
    ppermute x1, waiting for transfers between devices, local_step(): ghosts = lax.ppermute(payload, ('dom', 'frame'), pairs)  3.78 us
  transfers between devices with their start and end apart: 1, of which 1 were waited for; matrix products, arithmetic and copies ran while one was open for 0% of the time, Pallas kernels for 0%

profile of v5, /device:TPU:2, one launch (start us, length us, event | category | flops | bytes accessed | tf_op | source)
XLA Modules:
  0.0 30.4 jit_solution(9067059503763207284)
XLA Ops:
  0.0 6.1 %shard_map.118 = (bf16[64,640]{1,0:T(8,128)(2,1)S(1)}, f32[64,512]{1,0:T(8,128)S(1)}, bf16[192,128]{1,0:T(8,128)(2,1)S(1)}, bf16[128,512]{1,0:T(8,128)(2,1)S(1)}...) custom-call(bf16[128,512]{1,0:T(8,128)(2,1)} %feat_ref.1, ...), custom_call_target="tpu_custom_call" | custom-call | flops 3000000000 | bytes 3000000 | tf_op jit(solution)/shard_map/pallas_call | solution.py:422
  6.1 0.1 collective-permute-start
  6.2 0.0 copy-start
  6.2 0.0 copy-start.1
  6.2 0.0 copy-start.2
  6.3 3.8 %collective-permute-done.pay_ref = bf16[64,640]{1,0:T(8,128)(2,1)S(1)} collective-permute-done((bf16[64,640]{1,0:T(8,128)(2,1)S(1)}, bf16[64,640]{1,0:T(8,128)(2,1)S(1)}, u32[]{:S(2)}, u32[]{:S(2)}) %collective-permute-start) | collective-permute-done | bytes 81952 | tf_op jit(solution)/shard_map/ppermute | solution.py:447
  10.0 0.0 copy-done
  10.0 0.0 copy-done.1
  10.0 0.0 copy-done.2
  10.0 6.9 %shard_map.120 = f32[4,128]{1,0:T(4,128)S(1)} custom-call(bf16[64,640]{1,0:T(8,128)(2,1)S(1)} %collective-permute-done.pay_ref, f32[64,512]{1,0:T(8,128)S(1)} %shard_map.119.sum_ref, bf16[192,128]{1,0:T(8,128)(2,1)S(1)} %get-tuple-element.23.total_ref, bf16[128,512]{1,0:T(8,128)(2,1)S(1)} %get-tuple-element.19.table, ...), custom_call_target="tpu_custom_call" | custom-call | flops 7000000000 | bytes 7000000 | tf_op jit(solution)/shard_map/pallas_call | solution.py:455
  16.9 12.9 %all_to_all.5 = f32[8,4,128]{2,1,0:T(4,128)S(1)} all-to-all(f32[8,4,128]{2,1,0:T(4,128)S(1)} %broadcast_in_dim.3), channel_id=1, replica_groups=mesh['dom'=32,'frame'=8] {'frame'}, dimensions={0} | all-to-all | bytes 32768 | tf_op jit(solution)/shard_map/all_to_all | solution.py:481
  29.8 0.6 %broadcast_multiply_fusion = f32[4,128]{1,0:T(4,128)} fusion(f32[4,128]{1,0:T(4,128)S(1)} %reduce_sum.9), kind=kLoop, calls=%fused_computation | loop fusion | flops 512 | bytes 4096 | tf_op jit(solution)/shard_map/div | solution.py:482
  (3 shorter events, 0.1 us)
Async XLA Ops:
  6.1 4.0 %collective-permute-start = (bf16[64,640]{1,0:T(8,128)(2,1)S(1)}, bf16[64,640]{1,0:T(8,128)(2,1)S(1)}, u32[]{:S(2)}, u32[]{:S(2)}) collective-permute-start(bf16[64,640]{1,0:T(8,128)(2,1)S(1)} %get-tuple-element.17), channel_id=1, source_target_pairs={{0,252},{1,253},{2,254},{3,255},{4,8},{5,9},{6,10},{7,11},{8,4},{9... | collective-permute-start | bytes 245768 | tf_op jit(solution)/shard_map/ppermute | solution.py:447
  6.2 3.9 %copy-start = (bf16[512,512]{1,0:T(8,128)(2,1)S(1)}, bf16[512,512]{1,0:T(8,128)(2,1)}, u32[]{:S(2)}) copy-start(bf16[512,512]{1,0:T(8,128)(2,1)} %wm_ref.1) | copy-start | bytes 1572868
  6.2 3.8 %copy-start.1 = (bf16[512,512]{1,0:T(8,128)(2,1)S(1)}, bf16[512,512]{1,0:T(8,128)(2,1)}, u32[]{:S(2)}) copy-start(bf16[512,512]{1,0:T(8,128)(2,1)} %wu_ref.1) | copy-start | bytes 1572868
  6.2 3.8 %copy-start.2 = (bf16[512,512]{1,0:T(8,128)(2,1)S(1)}, bf16[512,512]{1,0:T(8,128)(2,1)}, u32[]{:S(2)}) copy-start(bf16[512,512]{1,0:T(8,128)(2,1)} %wr_ref.1) | copy-start | bytes 1572868

commit v6 on v5

--- a/solution.py
+++ b/solution.py
@@ -178,7 +178,7 @@
 
 
 def early():
-    return lax.axis_index("dom") == 0
+    return (lax.axis_index("dom") == 0) & (parity() == 0)
 
 
 def sum_own(table, edges, rhs, times, partial, sum_ref):
@@ -199,35 +199,55 @@
     sum_ref[...] = collect(partial, HALF)
 
 
-def first_kernel(
+def prepare_and_sum(
     feat_ref,
     pos_ref,
-    rows_ref,
     frame_ref,
     nbr_ref,
     cnt_ref,
     we_ref,
     be_ref,
-    wh_ref,
-    pay_ref,
     sum_ref,
     total_ref,
     table,
     edges,
     rhs,
     times,
-    pos_out,
-    frame_out,
-    we_out,
-    be_out,
-    wh_out,
     partial,
 ):
-    pos_out[...] = pos_ref[...]
-    frame_out[...] = frame_ref[...]
-    we_out[...] = we_ref[...]
-    be_out[...] = be_ref[...]
-    wh_out[...] = wh_ref[...]
+    own = pick(iota((ATOMS, ATOMS), 1) == local(iota((ATOMS, ATOMS), 0)))
+    table[...] = dot(own, feat_ref[...]).astype(BF)
+
+    raw = nbr_ref[...]
+    order = jnp.where(raw < ATOMS, raw + CAP, jnp.where(raw < ATOMS + CAP, raw - ATOMS, raw))
+    order = jnp.where(parity() == 1, 2 * CAP + ATOMS - 1 - order, order)
+    by_slot = order.astype(F32).T.astype(BF)
+    atom = local(iota((ATOMS, ATOMS), 0))
+    lane = iota((ATOMS, ATOMS), 1)
+    to_low = pick((atom == lane) & (lane < HALF))
+    to_high = pick(atom + HALF == lane)
+    folded = dot(by_slot[: SLOTS // 2], to_low) + dot(by_slot[SLOTS // 2 :], to_high)
+    cnt = jnp.broadcast_to(cnt_ref[...].astype(F32), (8, ATOMS)).astype(BF)
+    live = (dot(cnt, to_low) + dot(cnt, to_high))[0:1, :]
+    slot = iota((SLOTS // 2, ATOMS), 0) + jnp.where(iota((SLOTS // 2, ATOMS), 1) < HALF, 0, SLOTS // 2)
+    folded = jnp.where(slot.astype(F32) < live, folded, -1.0).astype(BF)
+    place = iota((TABLE, ATOMS), 0).astype(F32).astype(BF)
+    total = jnp.zeros((TABLE, ATOMS), BF)
+    one = jnp.ones((TABLE, ATOMS), BF)
+    for k in range(SLOTS // 2):
+        total = jnp.where(place == folded[k : k + 1, :], total + one, total)
+    total_ref[...] = total
+    fill_times(times, total[CAP:])
+    fill_edges(edges, placed_rows(own.astype(F32), pos_ref), centres(pos_ref), OWN_ROWS)
+    fill_filter(rhs, entries(frame_ref), we_ref, be_ref)
+    sum_own(table, edges, rhs, times, partial, sum_ref)
+
+
+def first_kernel(rows_ref, *refs):
+    sources, (pay_ref,), results, partial = refs[:8], refs[8:9], refs[9:23], refs[23]
+    for source, result in zip(sources, results[:8]):
+        result[...] = source[...]
+    feat_ref, pos_ref, frame_ref = sources[:3]
     wanted = jnp.where(parity() == 1, rows_ref[0, 1:2, :], rows_ref[0, 0:1, :])
     row = iota((CAP, CAP), 0)
     source = jnp.where(parity() == 1, row, CAP - 1 - row)
@@ -252,45 +272,22 @@
     turn = jnp.where(lane < 24, high, jnp.where(lane < 40, mid, low))
     pay_ref[:, WIDTH:] = (rest + turn).astype(BF)
 
-    own = pick(iota((ATOMS, ATOMS), 1) == local(iota((ATOMS, ATOMS), 0)))
-    table[...] = dot(own, feat_ref[...]).astype(BF)
-
-    raw = nbr_ref[...]
-    order = jnp.where(raw < ATOMS, raw + CAP, jnp.where(raw < ATOMS + CAP, raw - ATOMS, raw))
-    order = jnp.where(parity() == 1, 2 * CAP + ATOMS - 1 - order, order)
-    by_slot = order.astype(F32).T.astype(BF)
-    atom = local(iota((ATOMS, ATOMS), 0))
-    lane = iota((ATOMS, ATOMS), 1)
-    to_low = pick((atom == lane) & (lane < HALF))
-    to_high = pick(atom + HALF == lane)
-    folded = dot(by_slot[: SLOTS // 2], to_low) + dot(by_slot[SLOTS // 2 :], to_high)
-    cnt = jnp.broadcast_to(cnt_ref[...].astype(F32), (8, ATOMS)).astype(BF)
-    live = (dot(cnt, to_low) + dot(cnt, to_high))[0:1, :]
-    slot = iota((SLOTS // 2, ATOMS), 0) + jnp.where(iota((SLOTS // 2, ATOMS), 1) < HALF, 0, SLOTS // 2)
-    folded = jnp.where(slot.astype(F32) < live, folded, -1.0).astype(BF)
-    place = iota((TABLE, ATOMS), 0).astype(F32).astype(BF)
-    total = jnp.zeros((TABLE, ATOMS), BF)
-    one = jnp.ones((TABLE, ATOMS), BF)
-    for k in range(SLOTS // 2):
-        total = jnp.where(place == folded[k : k + 1, :], total + one, total)
-    total_ref[...] = total
-    fill_times(times, total[CAP:])
-    fill_edges(edges, placed_rows(own.astype(F32), pos_ref), centres(pos_ref), OWN_ROWS)
-    fill_filter(rhs, entries(frame_ref), we_ref, be_ref)
-
     @pl.when(early())
     def _():
-        sum_own(table, edges, rhs, times, partial, sum_ref)
-
-
-def own_kernel(before_ref, table, edges, rhs, times, sum_ref, partial):
+        prepare_and_sum(*sources[:7], *results[8:], partial)
+
+
+def own_kernel(*refs):
+    sources, before, results, partial = refs[:7], refs[7:13], refs[13:19], refs[19]
+
     @pl.when(early())
     def _():
-        sum_ref[...] = before_ref[...]
+        for source, result in zip(before, results):
+            result[...] = source[...]
 
     @pl.when(jnp.logical_not(early()))
     def _():
-        sum_own(table, edges, rhs, times, partial, sum_ref)
+        prepare_and_sum(*sources, *results, partial)
 
 
 def last_kernel(
@@ -405,53 +402,36 @@
     frame_count = lax.axis_size("frame")
     frame = jnp.transpose(frames, (1, 0, 2))
     bias = b_edge.reshape(1, WIDTH)
-    direct = [
-        pltpu.with_memory_space_constraint(x, pltpu.MemorySpace.HBM)
-        for x in (
-            features,
-            positions,
-            send_rows,
-            frame,
-            neighbours,
-            counts.reshape(1, ATOMS),
-            w_edge,
-            bias,
-            w_heads.T,
-        )
+    inputs = (features, positions, frame, neighbours, counts.reshape(1, ATOMS), w_edge, bias, w_heads.T)
+    prepared = [
+        pltpu.VMEM((HALF, WIDTH), F32),
+        pltpu.VMEM((TABLE, ATOMS), BF),
+        pltpu.VMEM((ATOMS, WIDTH), BF),
+        pltpu.VMEM((OWN_AT[-1], ATOMS), BF),
+        pltpu.VMEM((GROUP, ATOMS, WIDTH), BF),
+        pltpu.VMEM((GROUP, ATOMS, ATOMS), BF),
     ]
-    payload, before, total, table, edges, rhs, times, *small, heads = pl.pallas_call(
+    payload, *first = pl.pallas_call(
         first_kernel,
-        out_shape=[
-            pltpu.VMEM((CAP, PAY), BF),
-            pltpu.VMEM((HALF, WIDTH), F32),
-            pltpu.VMEM((TABLE, ATOMS), BF),
-            pltpu.VMEM((ATOMS, WIDTH), BF),
-            pltpu.VMEM((OWN_AT[-1], ATOMS), BF),
-            pltpu.VMEM((GROUP, ATOMS, WIDTH), BF),
-            pltpu.VMEM((GROUP, ATOMS, ATOMS), BF),
-            pltpu.VMEM(positions.shape, BF),
-            pltpu.VMEM(frame.shape, F32),
-            pltpu.VMEM(w_edge.shape, F32),
-            pltpu.VMEM(bias.shape, F32),
-            pltpu.VMEM((4, WIDTH), BF),
-        ],
+        out_shape=[pltpu.VMEM((CAP, PAY), BF)] + [pltpu.VMEM(x.shape, x.dtype) for x in inputs] + prepared,
         scratch_shapes=[pltpu.VMEM((WIDTH // 128, HALF * 8, 128), F32)],
-        compiler_params=pltpu.CompilerParams(vmem_limit_bytes=24 << 20),
-        cost_estimate=cost(3),
-    )(*direct)
+        compiler_params=pltpu.CompilerParams(vmem_limit_bytes=20 << 20),
+        cost_estimate=cost(2),
+    )(*[pltpu.with_memory_space_constraint(x, pltpu.MemorySpace.HBM) for x in (send_rows, *inputs)])
+    held, before = first[:8], first[8:]
     pairs = []
     for d in range(dom_count):
         for f in range(frame_count):
             to = (d + 1) % dom_count if f >= frame_count // 2 else (d - 1) % dom_count
             pairs.append((d * frame_count + f, to * frame_count + (f + frame_count // 2) % frame_count))
     ghosts = lax.ppermute(payload, ("dom", "frame"), pairs)
-    own_sum = pl.pallas_call(
+    own = pl.pallas_call(
         own_kernel,
-        out_shape=pltpu.VMEM((HALF, WIDTH), F32),
+        out_shape=prepared,
         scratch_shapes=[pltpu.VMEM((WIDTH // 128, HALF * 8, 128), F32)],
-        compiler_params=pltpu.CompilerParams(vmem_limit_bytes=24 << 20),
-        cost_estimate=cost(4),
-    )(before, table, edges, rhs, times)
+        compiler_params=pltpu.CompilerParams(vmem_limit_bytes=20 << 20),
+        cost_estimate=cost(5),
+    )(*held[:7], *before)
     part = pl.pallas_call(
         last_kernel,
         out_shape=jax.ShapeDtypeStruct((4, ATOMS), F32),
@@ -461,21 +441,19 @@
             pltpu.VMEM((GROUP, CAP, ATOMS), BF),
             pltpu.VMEM((WIDTH // 128, ATOMS * 8, 128), F32),
         ],
-        compiler_params=pltpu.CompilerParams(vmem_limit_bytes=24 << 20),
+        compiler_params=pltpu.CompilerParams(vmem_limit_bytes=20 << 20),
         cost_estimate=cost(7),
     )(
         ghosts,
-        own_sum,
-        total,
-        table,
-        edges,
-        rhs,
-        times,
-        *small,
+        *own,
+        held[1],
+        held[2],
+        held[5],
+        held[6],
         w_message,
         w_update,
         w_readout,
-        heads,
+        held[7],
     )
     copies = jnp.broadcast_to(part, (frame_count, *part.shape))
     everything = lax.all_to_all(copies, "frame", split_axis=0, concat_axis=0, tiled=True)

time: 30.5 us -> 30.9 us (1.013)
  waiting for transfers between devices: 3.78 us -> 0.01 us
  blocking collectives: 12.9 us -> 16.6 us
    ppermute x1, waiting for transfers between devices: 3.78 us -> 0.01 us  [local_step(): ghosts = lax.ppermute(payload, ('dom', 'frame'), pairs)]
    all_to_all x1, blocking collectives: 12.9 us -> 16.6 us  [local_step(): lax.all_to_all(copies, 'frame', split_axis=0, concat_axis=0, tiled=True)]
  transfers between devices with their start and end apart: 1 -> 1, of which waited for: 1 -> 0; matrix products, arithmetic and copies ran while one was open for 0% -> 0% of each run, Pallas kernels for 0% -> 17%
where the time goes in v6:
time: 30.9 us; the launch traced here: 30.7 us
  blocking collectives  16.6 us (54%)
  Pallas kernels  13.3 us (43%)
  other arithmetic  0.6 us (2%)
    all_to_all x1, blocking collectives, local_step(): lax.all_to_all(copies, 'frame', split_axis=0, concat_axis=0, tiled=True)  16.6 us
    pallas_call x1, Pallas kernels, local_step(): pl.pallas_call(last_kernel, out_shape=jax.ShapeDtypeStruct((4, ATOMS), F3...  6.96 us
    pallas_call x1, Pallas kernels, local_step(): pl.pallas_call(own_kernel, out_shape=prepared, scratch_shapes=[pltpu.VMEM...  5.11 us
    pallas_call x1, Pallas kernels, local_step(): pl.pallas_call(first_kernel, out_shape=[pltpu.VMEM((CAP, PAY), BF)] + [pl...  1.22 us
  transfers between devices with their start and end apart: 1, of which 0 were waited for; matrix products, arithmetic and copies ran while one was open for 0% of the time, Pallas kernels for 17%

profile of v6, /device:TPU:2, one launch (start us, length us, event | category | flops | bytes accessed | tf_op | source)
XLA Modules:
  0.0 30.7 jit_solution(1767499449904512667)
XLA Ops:
  0.0 1.2 %shard_map.118 = (bf16[64,640]{1,0:T(8,128)(2,1)S(1)}, bf16[128,512]{1,0:T(8,128)(2,1)S(1)}, bf16[3,128]{1,0:T(4,128)(2,1)S(1)}, f32[3,1,3]{2,1,0:T(1,128)S(1)},...) custom-call(s32[1,2,64]{2,1,0:T(2,128)} %rows_ref.1, ...), custom_call_target="tpu_custom_call" | custom-call | flops 2000000000 | bytes 2000000 | tf_op jit(solution)/shard_map/pallas_call | solution.py:414
  1.2 0.1 collective-permute-start
  1.3 0.0 copy-start
  1.3 0.0 copy-start.1
  1.3 0.0 copy-start.2
  1.4 5.1 %shard_map.119 = (f32[64,512]{1,0:T(8,128)S(1)}, bf16[192,128]{1,0:T(8,128)(2,1)S(1)}, bf16[128,512]{1,0:T(8,128)(2,1)S(1)}, bf16[800,128]{1,0:T(8,128)(2,1)S(1)...) custom-call(bf16[128,512]{1,0:T(8,128)(2,1)S(1)} %get-tuple-element.27.refs_0_, ...), custom_call_target="tpu_custom_call" | custom-call | flops 5000000000 | bytes 5000000 | tf_op jit(solution)/shard_map/pallas_call | solution.py:428
  6.5 0.0 collective-permute-done.pay_ref
  6.5 0.0 copy-done
  6.5 0.0 copy-done.1
  6.5 0.0 copy-done.2
  6.5 7.0 %shard_map.120 = f32[4,128]{1,0:T(4,128)S(1)} custom-call(bf16[64,640]{1,0:T(8,128)(2,1)S(1)} %collective-permute-done.pay_ref, f32[64,512]{1,0:T(8,128)S(1)} %get-tuple-element.40.sum_ref, bf16[192,128]{1,0:T(8,128)(2,1)S(1)} %get-tuple-element.41.total_ref, bf16[128,512]{1,0:T(8,128)(2,1)S(1)} %get-tuple-element.42.table, ...), custom_call_target="tpu_custom_call" | custom-call | flops 7000000000 | bytes 7000000 | tf_op jit(solution)/shard_map/pallas_call | solution.py:435
  13.5 16.6 %all_to_all.5 = f32[8,4,128]{2,1,0:T(4,128)S(1)} all-to-all(f32[8,4,128]{2,1,0:T(4,128)S(1)} %broadcast_in_dim.3), channel_id=1, replica_groups=mesh['dom'=32,'frame'=8] {'frame'}, dimensions={0} | all-to-all | bytes 32768 | tf_op jit(solution)/shard_map/all_to_all | solution.py:459
  30.2 0.6 %broadcast_multiply_fusion = f32[4,128]{1,0:T(4,128)} fusion(f32[4,128]{1,0:T(4,128)S(1)} %reduce_sum.9), kind=kLoop, calls=%fused_computation | loop fusion | flops 512 | bytes 4096 | tf_op jit(solution)/shard_map/div | solution.py:460
  (2 shorter events, 0.0 us)
Async XLA Ops:
  1.2 5.3 %collective-permute-start = (bf16[64,640]{1,0:T(8,128)(2,1)S(1)}, bf16[64,640]{1,0:T(8,128)(2,1)S(1)}, u32[]{:S(2)}, u32[]{:S(2)}) collective-permute-start(bf16[64,640]{1,0:T(8,128)(2,1)S(1)} %get-tuple-element.26), channel_id=1, source_target_pairs={{0,252},{1,253},{2,254},{3,255},{4,8},{5,9},{6,10},{7,11},{8,4},{9... | collective-permute-start | bytes 245768 | tf_op jit(solution)/shard_map/ppermute | solution.py:427
  1.3 5.2 %copy-start = (bf16[512,512]{1,0:T(8,128)(2,1)S(1)}, bf16[512,512]{1,0:T(8,128)(2,1)}, u32[]{:S(2)}) copy-start(bf16[512,512]{1,0:T(8,128)(2,1)} %wm_ref.1) | copy-start | bytes 1572868
  1.3 5.2 %copy-start.1 = (bf16[512,512]{1,0:T(8,128)(2,1)S(1)}, bf16[512,512]{1,0:T(8,128)(2,1)}, u32[]{:S(2)}) copy-start(bf16[512,512]{1,0:T(8,128)(2,1)} %wu_ref.1) | copy-start | bytes 1572868
  1.3 5.2 %copy-start.2 = (bf16[512,512]{1,0:T(8,128)(2,1)S(1)}, bf16[512,512]{1,0:T(8,128)(2,1)}, u32[]{:S(2)}) copy-start(bf16[512,512]{1,0:T(8,128)(2,1)} %wr_ref.1) | copy-start | bytes 1572868

commit v7 on v6

--- a/solution.py
+++ b/solution.py
@@ -26,6 +26,7 @@
 GHOST_ROWS = ((0, 64), (16, 64), (32, 64), (48, 64))
 OWN_ROWS = ((0, 64), (0, 96), (0, 112), (0, 128))
 TILE = 256
+AHEAD = 4
 
 
 def iota(shape, dim):
@@ -167,12 +168,12 @@
         partial[w * (TILE // 128) + t, pl.ds(at, 8), :] = done[:, t * 128 : (t + 1) * 128]
 
 
-def collect(partial, rows):
+def collect(partial, begin, end):
     tiles = []
     for t in range(WIDTH // 128):
-        total = partial[t, pl.ds(0, rows, stride=8), :]
+        total = partial[t, pl.ds(begin * 8, end - begin, stride=8), :]
         for r in range(1, 8):
-            total = total + partial[t, pl.ds(r, rows, stride=8), :]
+            total = total + partial[t, pl.ds(begin * 8 + r, end - begin, stride=8), :]
         tiles.append(total)
     return jnp.concatenate(tiles, axis=1)
 
@@ -181,7 +182,7 @@
     return (lax.axis_index("dom") == 0) & (parity() == 0)
 
 
-def sum_own(table, edges, rhs, times, partial, sum_ref):
+def sum_own(begin, end, table, edges, rhs, times, partial, sum_ref):
     def step(a, carry):
         share = times[a]
         for w in range(WIDTH // TILE):
@@ -195,11 +196,12 @@
                     keep(partial, a, g, GROUPS, w, total_of(cut(gate * weighted)))
         return carry
 
-    lax.fori_loop(0, GROUP, step, 0)
-    sum_ref[...] = collect(partial, HALF)
+    lax.fori_loop(begin, end, step, 0)
+    sum_ref[begin * GROUPS : end * GROUPS, :] = collect(partial, begin * GROUPS, end * GROUPS)
 
 
 def prepare_and_sum(
+    end,
     feat_ref,
     pos_ref,
     frame_ref,
@@ -240,7 +242,7 @@
     fill_times(times, total[CAP:])
     fill_edges(edges, placed_rows(own.astype(F32), pos_ref), centres(pos_ref), OWN_ROWS)
     fill_filter(rhs, entries(frame_ref), we_ref, be_ref)
-    sum_own(table, edges, rhs, times, partial, sum_ref)
+    sum_own(0, end, table, edges, rhs, times, partial, sum_ref)
 
 
 def first_kernel(rows_ref, *refs):
@@ -274,7 +276,7 @@
 
     @pl.when(early())
     def _():
-        prepare_and_sum(*sources[:7], *results[8:], partial)
+        prepare_and_sum(AHEAD, *sources[:7], *results[8:], partial)
 
 
 def own_kernel(*refs):
@@ -284,10 +286,11 @@
     def _():
         for source, result in zip(before, results):
             result[...] = source[...]
+        sum_own(AHEAD, GROUP, *results[2:], partial, results[0])
 
     @pl.when(jnp.logical_not(early()))
     def _():
-        prepare_and_sum(*sources, *results, partial)
+        prepare_and_sum(GROUP, *sources, *results, partial)
 
 
 def last_kernel(
@@ -349,7 +352,7 @@
         return carry
 
     lax.fori_loop(0, GROUP, step, 0)
-    total = collect(partial, ATOMS)
+    total = collect(partial, 0, ATOMS)
     before = [
         piece
         for a in range(GROUP)

time: 30.9 us -> 29.1 us (0.942)
  blocking collectives: 16.6 us -> 14.8 us
    all_to_all x1, blocking collectives: 16.6 us -> 14.8 us  [local_step(): lax.all_to_all(copies, 'frame', split_axis=0, concat_axis=0, tiled=True)]
  transfers between devices with their start and end apart: 1 -> 1, of which waited for: 0 -> 0; matrix products, arithmetic and copies ran while one was open for 0% -> 0% of each run, Pallas kernels for 17% -> 18%
where the time goes in v7:
time: 29.1 us; the launch traced here: 28.9 us
  blocking collectives  14.8 us (51%)
  Pallas kernels  13.3 us (46%)
  other arithmetic  0.6 us (2%)
    all_to_all x1, blocking collectives, local_step(): lax.all_to_all(copies, 'frame', split_axis=0, concat_axis=0, tiled=True)  14.8 us
    pallas_call x1, Pallas kernels, local_step(): pl.pallas_call(last_kernel, out_shape=jax.ShapeDtypeStruct((4, ATOMS), F3...  6.96 us
    pallas_call x1, Pallas kernels, local_step(): pl.pallas_call(own_kernel, out_shape=prepared, scratch_shapes=[pltpu.VMEM...  5.11 us
    pallas_call x1, Pallas kernels, local_step(): pl.pallas_call(first_kernel, out_shape=[pltpu.VMEM((CAP, PAY), BF)] + [pl...  1.22 us
    div x1, other arithmetic, local_step(): return jnp.sum(everything, axis=0) / frame_count  0.58 us
  transfers between devices with their start and end apart: 1, of which 0 were waited for; matrix products, arithmetic and copies ran while one was open for 0% of the time, Pallas kernels for 18%

profile of v7, /device:TPU:2, one launch (start us, length us, event | category | flops | bytes accessed | tf_op | source)
XLA Modules:
  0.0 28.9 jit_solution(4452654686282270536)
XLA Ops:
  0.0 1.2 %shard_map.118 = (bf16[64,640]{1,0:T(8,128)(2,1)S(1)}, bf16[128,512]{1,0:T(8,128)(2,1)S(1)}, bf16[3,128]{1,0:T(4,128)(2,1)S(1)}, f32[3,1,3]{2,1,0:T(1,128)S(1)},...) custom-call(s32[1,2,64]{2,1,0:T(2,128)} %rows_ref.1, ...), custom_call_target="tpu_custom_call" | custom-call | flops 2000000000 | bytes 2000000 | tf_op jit(solution)/shard_map/pallas_call | solution.py:417
  1.2 0.1 collective-permute-start
  1.3 0.0 copy-start
  1.3 0.0 copy-start.1
  1.3 0.0 copy-start.2
  1.4 5.1 %shard_map.119 = (f32[64,512]{1,0:T(8,128)S(1)}, bf16[192,128]{1,0:T(8,128)(2,1)S(1)}, bf16[128,512]{1,0:T(8,128)(2,1)S(1)}, bf16[800,128]{1,0:T(8,128)(2,1)S(1)...) custom-call(bf16[128,512]{1,0:T(8,128)(2,1)S(1)} %get-tuple-element.27.refs_0_, ...), custom_call_target="tpu_custom_call" | custom-call | flops 5000000000 | bytes 5000000 | tf_op jit(solution)/shard_map/pallas_call | solution.py:431
  6.5 0.0 collective-permute-done.pay_ref
  6.5 0.0 copy-done
  6.5 0.0 copy-done.1
  6.5 0.0 copy-done.2
  6.5 7.0 %shard_map.120 = f32[4,128]{1,0:T(4,128)S(1)} custom-call(bf16[64,640]{1,0:T(8,128)(2,1)S(1)} %collective-permute-done.pay_ref, f32[64,512]{1,0:T(8,128)S(1)} %get-tuple-element.40.sum_ref, bf16[192,128]{1,0:T(8,128)(2,1)S(1)} %get-tuple-element.41.total_ref, bf16[128,512]{1,0:T(8,128)(2,1)S(1)} %get-tuple-element.42.table, ...), custom_call_target="tpu_custom_call" | custom-call | flops 7000000000 | bytes 7000000 | tf_op jit(solution)/shard_map/pallas_call | solution.py:438
  13.5 14.8 %all_to_all.5 = f32[8,4,128]{2,1,0:T(4,128)S(1)} all-to-all(f32[8,4,128]{2,1,0:T(4,128)S(1)} %broadcast_in_dim.3), channel_id=1, replica_groups=mesh['dom'=32,'frame'=8] {'frame'}, dimensions={0} | all-to-all | bytes 32768 | tf_op jit(solution)/shard_map/all_to_all | solution.py:462
  28.4 0.6 %broadcast_multiply_fusion = f32[4,128]{1,0:T(4,128)} fusion(f32[4,128]{1,0:T(4,128)S(1)} %reduce_sum.9), kind=kLoop, calls=%fused_computation | loop fusion | flops 512 | bytes 4096 | tf_op jit(solution)/shard_map/div | solution.py:463
  (2 shorter events, 0.0 us)
Async XLA Ops:
  1.2 5.3 %collective-permute-start = (bf16[64,640]{1,0:T(8,128)(2,1)S(1)}, bf16[64,640]{1,0:T(8,128)(2,1)S(1)}, u32[]{:S(2)}, u32[]{:S(2)}) collective-permute-start(bf16[64,640]{1,0:T(8,128)(2,1)S(1)} %get-tuple-element.26), channel_id=1, source_target_pairs={{0,252},{1,253},{2,254},{3,255},{4,8},{5,9},{6,10},{7,11},{8,4},{9... | collective-permute-start | bytes 245768 | tf_op jit(solution)/shard_map/ppermute | solution.py:430
  1.3 5.2 %copy-start = (bf16[512,512]{1,0:T(8,128)(2,1)S(1)}, bf16[512,512]{1,0:T(8,128)(2,1)}, u32[]{:S(2)}) copy-start(bf16[512,512]{1,0:T(8,128)(2,1)} %wm_ref.1) | copy-start | bytes 1572868
  1.3 5.2 %copy-start.1 = (bf16[512,512]{1,0:T(8,128)(2,1)S(1)}, bf16[512,512]{1,0:T(8,128)(2,1)}, u32[]{:S(2)}) copy-start(bf16[512,512]{1,0:T(8,128)(2,1)} %wu_ref.1) | copy-start | bytes 1572868
  1.3 5.2 %copy-start.2 = (bf16[512,512]{1,0:T(8,128)(2,1)S(1)}, bf16[512,512]{1,0:T(8,128)(2,1)}, u32[]{:S(2)}) copy-start(bf16[512,512]{1,0:T(8,128)(2,1)} %wr_ref.1) | copy-start | bytes 1572868

commit v8 on v7

--- a/solution.py
+++ b/solution.py
@@ -103,10 +103,15 @@
     vec = jnp.concatenate([vectors(rot, we_ref, c) for c in range(3)], axis=0)
     high, low = split(vec)
     rows = jnp.concatenate([0.5 * we_ref[0:RADIAL, :], high, high, low, 0.5 * be_ref[...]], axis=0)
-    rows = jnp.concatenate([rows] * GROUP, axis=0).astype(BF)
-    block = iota((ATOMS, WIDTH), 0) // FEATS
-    for a in range(GROUP):
-        rhs[a, :, :] = jnp.where(block == a, rows, jnp.zeros_like(rows))
+    room = ATOMS - FEATS
+    rhs[:room, :] = jnp.zeros((room, WIDTH), BF)
+    rhs[room : room + FEATS, :] = rows.astype(BF)
+    rhs[room + FEATS :, :] = jnp.zeros((room, WIDTH), BF)
+
+
+def weights_at(rhs, a, span):
+    first = (GROUP - 1 - a) * FEATS
+    return rhs[first : first + ATOMS, span]
 
 
 def fill_times(times, total):
@@ -163,9 +168,9 @@
 
 
 def keep(partial, a, k, count, w, done):
-    at = pl.multiple_of((a * count + k) * 8, 8)
+    at = (a * count + k) * 8
     for t in range(TILE // 128):
-        partial[w * (TILE // 128) + t, pl.ds(at, 8), :] = done[:, t * 128 : (t + 1) * 128]
+        partial[w * (TILE // 128) + t, at : at + 8, :] = done[:, t * 128 : (t + 1) * 128]
 
 
 def collect(partial, begin, end):
@@ -183,20 +188,20 @@
 
 
 def sum_own(begin, end, table, edges, rhs, times, partial, sum_ref):
-    def step(a, carry):
+    def step(a):
         share = times[a]
         for w in range(WIDTH // TILE):
             span = slice(w * TILE, (w + 1) * TILE)
             for first in range(0, GROUPS, 2):
-                pre = dot(edges[OWN_AT[first] : OWN_AT[first + 2], :], rhs[a, :, span]).astype(BF)
+                pre = dot(edges[OWN_AT[first] : OWN_AT[first + 2], :], weights_at(rhs, a, span)).astype(BF)
                 for g in range(first, first + 2):
                     lo, hi = OWN_ROWS[g // 2]
                     weighted = table[lo:hi, span] * share[lo:hi, g : g + 1]
                     gate = gated(pre[OWN_AT[g] - OWN_AT[first] : OWN_AT[g + 1] - OWN_AT[first]])
                     keep(partial, a, g, GROUPS, w, total_of(cut(gate * weighted)))
-        return carry
-
-    lax.fori_loop(begin, end, step, 0)
+
+    for a in range(begin, end):
+        step(a)
     sum_ref[begin * GROUPS : end * GROUPS, :] = collect(partial, begin * GROUPS, end * GROUPS)
 
 
@@ -329,15 +334,15 @@
     fill_edges(ghosts, reach, centres(pos_ref), GHOST_ROWS)
     fill_filter(rhs_other, other, we_ref, be_ref)
 
-    def step(a, carry):
+    def step(a):
         share = times[a]
         own_share = own_times[a]
         for w in range(WIDTH // TILE):
             span = slice(w * TILE, (w + 1) * TILE)
-            near = gated(dot(ghosts[...], rhs[a, :, span]))
-            far = gated(dot(ghosts[...], rhs_other[a, :, span]))
+            near = gated(dot(ghosts[...], weights_at(rhs, a, span)))
+            far = gated(dot(ghosts[...], weights_at(rhs_other, a, span)))
             for first in range(0, GROUPS, 2):
-                pre = dot(edges[OWN_AT[first] : OWN_AT[first + 2], :], rhs_other[a, :, span]).astype(BF)
+                pre = dot(edges[OWN_AT[first] : OWN_AT[first + 2], :], weights_at(rhs_other, a, span)).astype(BF)
                 for g in range(first, first + 2):
                     lo, hi = GHOST_ROWS[g // 2]
                     weighted = pay_ref[lo:hi, span] * share[lo:hi, g : g + 1]
@@ -349,9 +354,9 @@
                     gate = gated(pre[OWN_AT[g] - OWN_AT[first] : OWN_AT[g + 1] - OWN_AT[first]])
                     parts = parts + cut(gate * weighted)
                     keep(partial, a, GROUPS + g, 2 * GROUPS, w, total_of(parts))
-        return carry
-
-    lax.fori_loop(0, GROUP, step, 0)
+
+    for a in range(GROUP):
+        step(a)
     total = collect(partial, 0, ATOMS)
     before = [
         piece
@@ -411,7 +416,7 @@
         pltpu.VMEM((TABLE, ATOMS), BF),
         pltpu.VMEM((ATOMS, WIDTH), BF),
         pltpu.VMEM((OWN_AT[-1], ATOMS), BF),
-        pltpu.VMEM((GROUP, ATOMS, WIDTH), BF),
+        pltpu.VMEM((2 * ATOMS - FEATS, WIDTH), BF),
         pltpu.VMEM((GROUP, ATOMS, ATOMS), BF),
     ]
     payload, *first = pl.pallas_call(
@@ -440,7 +445,7 @@
         out_shape=jax.ShapeDtypeStruct((4, ATOMS), F32),
         scratch_shapes=[
             pltpu.VMEM((GHOST_AT[-1], ATOMS), BF),
-            pltpu.VMEM((GROUP, ATOMS, WIDTH), BF),
+            pltpu.VMEM((2 * ATOMS - FEATS, WIDTH), BF),
             pltpu.VMEM((GROUP, CAP, ATOMS), BF),
             pltpu.VMEM((WIDTH // 128, ATOMS * 8, 128), F32),
         ],

time: 29.1 us -> 27.5 us (0.945)
  Pallas kernels: 13.3 us -> 11.6 us
    pallas_call x1, Pallas kernels: 6.96 us -> 5.97 us  [local_step(): pl.pallas_call(last_kernel, out_shape=jax.ShapeDtypeStruct((4, ATOMS), F3...]
    pallas_call x1, Pallas kernels: 5.11 us -> 4.38 us  [local_step(): pl.pallas_call(own_kernel, out_shape=prepared, scratch_shapes=[pltpu.VMEM...]
  transfers between devices with their start and end apart: 1 -> 1, of which waited for: 0 -> 0; matrix products, arithmetic and copies ran while one was open for 0% -> 0% of each run, Pallas kernels for 18% -> 16%
where the time goes in v8:
time: 27.5 us; the launch traced here: 27.4 us
  blocking collectives  15 us (55%)
  Pallas kernels  11.6 us (42%)
  other arithmetic  0.6 us (2%)
    all_to_all x1, blocking collectives, local_step(): lax.all_to_all(copies, 'frame', split_axis=0, concat_axis=0, tiled=True)  15 us
    pallas_call x1, Pallas kernels, local_step(): pl.pallas_call(last_kernel, out_shape=jax.ShapeDtypeStruct((4, ATOMS), F3...  5.97 us
    pallas_call x1, Pallas kernels, local_step(): pl.pallas_call(own_kernel, out_shape=prepared, scratch_shapes=[pltpu.VMEM...  4.38 us
    pallas_call x1, Pallas kernels, local_step(): pl.pallas_call(first_kernel, out_shape=[pltpu.VMEM((CAP, PAY), BF)] + [pl...  1.22 us
    div x1, other arithmetic, local_step(): return jnp.sum(everything, axis=0) / frame_count  0.58 us
  transfers between devices with their start and end apart: 1, of which 0 were waited for; matrix products, arithmetic and copies ran while one was open for 0% of the time, Pallas kernels for 16%

profile of v8, /device:TPU:2, one launch (start us, length us, event | category | flops | bytes accessed | tf_op | source)
XLA Modules:
  0.0 27.4 jit_solution(14414526210164903506)
XLA Ops:
  0.0 1.2 %shard_map.118 = (bf16[64,640]{1,0:T(8,128)(2,1)S(1)}, bf16[128,512]{1,0:T(8,128)(2,1)S(1)}, bf16[3,128]{1,0:T(4,128)(2,1)S(1)}, f32[3,1,3]{2,1,0:T(1,128)S(1)},...) custom-call(s32[1,2,64]{2,1,0:T(2,128)} %rows_ref.1, ...), custom_call_target="tpu_custom_call" | custom-call | flops 2000000000 | bytes 2000000 | tf_op jit(solution)/shard_map/pallas_call | solution.py:422
  1.2 0.1 collective-permute-start
  1.3 0.0 copy-start
  1.3 0.0 copy-start.1
  1.3 0.0 copy-start.2
  1.4 4.4 %shard_map.119 = (f32[64,512]{1,0:T(8,128)S(1)}, bf16[192,128]{1,0:T(8,128)(2,1)S(1)}, bf16[128,512]{1,0:T(8,128)(2,1)S(1)}, bf16[800,128]{1,0:T(8,128)(2,1)S(1)...) custom-call(bf16[128,512]{1,0:T(8,128)(2,1)S(1)} %get-tuple-element.27.refs_0_, ...), custom_call_target="tpu_custom_call" | custom-call | flops 5000000000 | bytes 5000000 | tf_op jit(solution)/shard_map/pallas_call | solution.py:436
  5.8 0.0 collective-permute-done.pay_ref
  5.8 0.0 copy-done
  5.8 0.0 copy-done.1
  5.8 0.0 copy-done.2
  5.8 6.0 %shard_map.120 = f32[4,128]{1,0:T(4,128)S(1)} custom-call(bf16[64,640]{1,0:T(8,128)(2,1)S(1)} %collective-permute-done.pay_ref, f32[64,512]{1,0:T(8,128)S(1)} %get-tuple-element.40.sum_ref, bf16[192,128]{1,0:T(8,128)(2,1)S(1)} %get-tuple-element.41.total_ref, bf16[128,512]{1,0:T(8,128)(2,1)S(1)} %get-tuple-element.42.table, ...), custom_call_target="tpu_custom_call" | custom-call | flops 7000000000 | bytes 7000000 | tf_op jit(solution)/shard_map/pallas_call | solution.py:443
  11.8 15.0 %all_to_all.5 = f32[8,4,128]{2,1,0:T(4,128)S(1)} all-to-all(f32[8,4,128]{2,1,0:T(4,128)S(1)} %broadcast_in_dim.3), channel_id=1, replica_groups=mesh['dom'=32,'frame'=8] {'frame'}, dimensions={0} | all-to-all | bytes 32768 | tf_op jit(solution)/shard_map/all_to_all | solution.py:467
  26.8 0.6 %broadcast_multiply_fusion = f32[4,128]{1,0:T(4,128)} fusion(f32[4,128]{1,0:T(4,128)S(1)} %reduce_sum.9), kind=kLoop, calls=%fused_computation | loop fusion | flops 512 | bytes 4096 | tf_op jit(solution)/shard_map/div | solution.py:468
  (2 shorter events, 0.0 us)
Async XLA Ops:
  1.2 4.5 %collective-permute-start = (bf16[64,640]{1,0:T(8,128)(2,1)S(1)}, bf16[64,640]{1,0:T(8,128)(2,1)S(1)}, u32[]{:S(2)}, u32[]{:S(2)}) collective-permute-start(bf16[64,640]{1,0:T(8,128)(2,1)S(1)} %get-tuple-element.26), channel_id=1, source_target_pairs={{0,252},{1,253},{2,254},{3,255},{4,8},{5,9},{6,10},{7,11},{8,4},{9... | collective-permute-start | bytes 245768 | tf_op jit(solution)/shard_map/ppermute | solution.py:435
  1.3 4.4 %copy-start = (bf16[512,512]{1,0:T(8,128)(2,1)S(1)}, bf16[512,512]{1,0:T(8,128)(2,1)}, u32[]{:S(2)}) copy-start(bf16[512,512]{1,0:T(8,128)(2,1)} %wm_ref.1) | copy-start | bytes 1572868
  1.3 4.4 %copy-start.1 = (bf16[512,512]{1,0:T(8,128)(2,1)S(1)}, bf16[512,512]{1,0:T(8,128)(2,1)}, u32[]{:S(2)}) copy-start(bf16[512,512]{1,0:T(8,128)(2,1)} %wu_ref.1) | copy-start | bytes 1572868
  1.3 4.4 %copy-start.2 = (bf16[512,512]{1,0:T(8,128)(2,1)S(1)}, bf16[512,512]{1,0:T(8,128)(2,1)}, u32[]{:S(2)}) copy-start(bf16[512,512]{1,0:T(8,128)(2,1)} %wr_ref.1) | copy-start | bytes 1572868

commit v9 on v8

--- a/solution.py
+++ b/solution.py
@@ -26,7 +26,7 @@
 GHOST_ROWS = ((0, 64), (16, 64), (32, 64), (48, 64))
 OWN_ROWS = ((0, 64), (0, 96), (0, 112), (0, 128))
 TILE = 256
-AHEAD = 4
+AHEAD = 3
 
 
 def iota(shape, dim):
@@ -117,7 +117,7 @@
 def fill_times(times, total):
     for a in range(GROUP):
         spread = pick(iota((ATOMS, ATOMS), 0) % HALF == iota((ATOMS, ATOMS), 1) * GROUP + a)
-        times[a, :, :] = dot(total, spread).astype(BF)
+        times[a, :, :] = dot(total, spread)
 
 
 def sum_rows(prod, rows):
@@ -147,6 +147,11 @@
 GHOST_AT = offsets_of(GHOST_ROWS)
 
 
+def wide_of(column):
+    column = jnp.broadcast_to(column, (column.shape[0], 128)).astype(BF)
+    return jnp.concatenate([column] * (TILE // 128), axis=1)
+
+
 def gated(pre):
     half = pre.astype(BF)
     return half * jnp.tanh(half) + half
@@ -196,7 +201,7 @@
                 pre = dot(edges[OWN_AT[first] : OWN_AT[first + 2], :], weights_at(rhs, a, span)).astype(BF)
                 for g in range(first, first + 2):
                     lo, hi = OWN_ROWS[g // 2]
-                    weighted = table[lo:hi, span] * share[lo:hi, g : g + 1]
+                    weighted = table[lo:hi, span] * wide_of(share[lo:hi, g : g + 1])
                     gate = gated(pre[OWN_AT[g] - OWN_AT[first] : OWN_AT[g + 1] - OWN_AT[first]])
                     keep(partial, a, g, GROUPS, w, total_of(cut(gate * weighted)))
 
@@ -345,12 +350,12 @@
                 pre = dot(edges[OWN_AT[first] : OWN_AT[first + 2], :], weights_at(rhs_other, a, span)).astype(BF)
                 for g in range(first, first + 2):
                     lo, hi = GHOST_ROWS[g // 2]
-                    weighted = pay_ref[lo:hi, span] * share[lo:hi, g : g + 1]
+                    weighted = pay_ref[lo:hi, span] * wide_of(share[lo:hi, g : g + 1])
                     rows = slice(GHOST_AT[g], GHOST_AT[g + 1])
                     keep(partial, a, g, 2 * GROUPS, w, total_of(cut(near[rows] * weighted)))
                     parts = cut(far[rows] * weighted)
                     lo, hi = OWN_ROWS[g // 2]
-                    weighted = table[lo:hi, span] * own_share[lo:hi, g : g + 1]
+                    weighted = table[lo:hi, span] * wide_of(own_share[lo:hi, g : g + 1])
                     gate = gated(pre[OWN_AT[g] - OWN_AT[first] : OWN_AT[g + 1] - OWN_AT[first]])
                     parts = parts + cut(gate * weighted)
                     keep(partial, a, GROUPS + g, 2 * GROUPS, w, total_of(parts))
@@ -417,7 +422,7 @@
         pltpu.VMEM((ATOMS, WIDTH), BF),
         pltpu.VMEM((OWN_AT[-1], ATOMS), BF),
         pltpu.VMEM((2 * ATOMS - FEATS, WIDTH), BF),
-        pltpu.VMEM((GROUP, ATOMS, ATOMS), BF),
+        pltpu.VMEM((GROUP, ATOMS, ATOMS), F32),
     ]
     payload, *first = pl.pallas_call(
         first_kernel,
@@ -446,7 +451,7 @@
         scratch_shapes=[
             pltpu.VMEM((GHOST_AT[-1], ATOMS), BF),
             pltpu.VMEM((2 * ATOMS - FEATS, WIDTH), BF),
-            pltpu.VMEM((GROUP, CAP, ATOMS), BF),
+            pltpu.VMEM((GROUP, CAP, ATOMS), F32),
             pltpu.VMEM((WIDTH // 128, ATOMS * 8, 128), F32),
         ],
         compiler_params=pltpu.CompilerParams(vmem_limit_bytes=20 << 20),

time: 27.5 us -> 27 us (0.982)
  Pallas kernels: 11.6 us -> 11.1 us
    pallas_call x1, Pallas kernels: 5.97 us -> 5.68 us  [local_step(): pl.pallas_call(last_kernel, out_shape=jax.ShapeDtypeStruct((4, ATOMS), F3...]
where the time goes in v9:
time: 27 us; the launch traced here: 26.8 us
  blocking collectives  14.9 us (55%)
  Pallas kernels  11.1 us (41%)
  other arithmetic  0.6 us (2%)
    all_to_all x1, blocking collectives, local_step(): lax.all_to_all(copies, 'frame', split_axis=0, concat_axis=0, tiled=True)  14.9 us
    pallas_call x1, Pallas kernels, local_step(): pl.pallas_call(last_kernel, out_shape=jax.ShapeDtypeStruct((4, ATOMS), F3...  5.68 us
    pallas_call x1, Pallas kernels, local_step(): pl.pallas_call(own_kernel, out_shape=prepared, scratch_shapes=[pltpu.VMEM...  4.23 us
    pallas_call x1, Pallas kernels, local_step(): pl.pallas_call(first_kernel, out_shape=[pltpu.VMEM((CAP, PAY), BF)] + [pl...  1.22 us
    div x1, other arithmetic, local_step(): return jnp.sum(everything, axis=0) / frame_count  0.58 us
  transfers between devices with their start and end apart: 1, of which 0 were waited for; matrix products, arithmetic and copies ran while one was open for 0% of the time, Pallas kernels for 16%

profile of v9, /device:TPU:2, one launch (start us, length us, event | category | flops | bytes accessed | tf_op | source)
XLA Modules:
  0.0 26.8 jit_solution(13778362642175542971)
XLA Ops:
  0.0 1.2 %shard_map.118 = (bf16[64,640]{1,0:T(8,128)(2,1)S(1)}, bf16[128,512]{1,0:T(8,128)(2,1)S(1)}, bf16[3,128]{1,0:T(4,128)(2,1)S(1)}, f32[3,1,3]{2,1,0:T(1,128)S(1)},...) custom-call(s32[1,2,64]{2,1,0:T(2,128)} %rows_ref.1, ...), custom_call_target="tpu_custom_call" | custom-call | flops 2000000000 | bytes 2000000 | tf_op jit(solution)/shard_map/pallas_call | solution.py:427
  1.2 0.1 collective-permute-start
  1.3 0.0 copy-start
  1.3 0.0 copy-start.1
  1.3 0.0 copy-start.2
  1.4 4.2 %shard_map.119 = (f32[64,512]{1,0:T(8,128)S(1)}, bf16[192,128]{1,0:T(8,128)(2,1)S(1)}, bf16[128,512]{1,0:T(8,128)(2,1)S(1)}, bf16[800,128]{1,0:T(8,128)(2,1)S(1)...) custom-call(bf16[128,512]{1,0:T(8,128)(2,1)S(1)} %get-tuple-element.27.refs_0_, ...), custom_call_target="tpu_custom_call" | custom-call | flops 5000000000 | bytes 5000000 | tf_op jit(solution)/shard_map/pallas_call | solution.py:441
  5.6 0.0 collective-permute-done.pay_ref
  5.6 0.0 copy-done
  5.6 0.0 copy-done.1
  5.6 0.0 copy-done.2
  5.6 5.7 %shard_map.120 = f32[4,128]{1,0:T(4,128)S(1)} custom-call(bf16[64,640]{1,0:T(8,128)(2,1)S(1)} %collective-permute-done.pay_ref, f32[64,512]{1,0:T(8,128)S(1)} %get-tuple-element.40.sum_ref, bf16[192,128]{1,0:T(8,128)(2,1)S(1)} %get-tuple-element.41.total_ref, bf16[128,512]{1,0:T(8,128)(2,1)S(1)} %get-tuple-element.42.table, ...), custom_call_target="tpu_custom_call" | custom-call | flops 7000000000 | bytes 7000000 | tf_op jit(solution)/shard_map/pallas_call | solution.py:448
  11.4 14.9 %all_to_all.5 = f32[8,4,128]{2,1,0:T(4,128)S(1)} all-to-all(f32[8,4,128]{2,1,0:T(4,128)S(1)} %broadcast_in_dim.3), channel_id=1, replica_groups=mesh['dom'=32,'frame'=8] {'frame'}, dimensions={0} | all-to-all | bytes 32768 | tf_op jit(solution)/shard_map/all_to_all | solution.py:472
  26.3 0.6 %broadcast_multiply_fusion = f32[4,128]{1,0:T(4,128)} fusion(f32[4,128]{1,0:T(4,128)S(1)} %reduce_sum.9), kind=kLoop, calls=%fused_computation | loop fusion | flops 512 | bytes 4096 | tf_op jit(solution)/shard_map/div | solution.py:473
  (2 shorter events, 0.0 us)
Async XLA Ops:
  1.2 4.4 %collective-permute-start = (bf16[64,640]{1,0:T(8,128)(2,1)S(1)}, bf16[64,640]{1,0:T(8,128)(2,1)S(1)}, u32[]{:S(2)}, u32[]{:S(2)}) collective-permute-start(bf16[64,640]{1,0:T(8,128)(2,1)S(1)} %get-tuple-element.26), channel_id=1, source_target_pairs={{0,252},{1,253},{2,254},{3,255},{4,8},{5,9},{6,10},{7,11},{8,4},{9... | collective-permute-start | bytes 245768 | tf_op jit(solution)/shard_map/ppermute | solution.py:440
  1.3 4.3 %copy-start = (bf16[512,512]{1,0:T(8,128)(2,1)S(1)}, bf16[512,512]{1,0:T(8,128)(2,1)}, u32[]{:S(2)}) copy-start(bf16[512,512]{1,0:T(8,128)(2,1)} %wm_ref.1) | copy-start | bytes 1572868
  1.3 4.3 %copy-start.1 = (bf16[512,512]{1,0:T(8,128)(2,1)S(1)}, bf16[512,512]{1,0:T(8,128)(2,1)}, u32[]{:S(2)}) copy-start(bf16[512,512]{1,0:T(8,128)(2,1)} %wu_ref.1) | copy-start | bytes 1572868
  1.3 4.3 %copy-start.2 = (bf16[512,512]{1,0:T(8,128)(2,1)S(1)}, bf16[512,512]{1,0:T(8,128)(2,1)}, u32[]{:S(2)}) copy-start(bf16[512,512]{1,0:T(8,128)(2,1)} %wr_ref.1) | copy-start | bytes 1572868

commit v10 on v9

--- a/solution.py
+++ b/solution.py
@@ -197,9 +197,9 @@
         share = times[a]
         for w in range(WIDTH // TILE):
             span = slice(w * TILE, (w + 1) * TILE)
-            for first in range(0, GROUPS, 2):
-                pre = dot(edges[OWN_AT[first] : OWN_AT[first + 2], :], weights_at(rhs, a, span)).astype(BF)
-                for g in range(first, first + 2):
+            for first in range(0, GROUPS, 4):
+                pre = dot(edges[OWN_AT[first] : OWN_AT[first + 4], :], weights_at(rhs, a, span)).astype(BF)
+                for g in range(first, first + 4):
                     lo, hi = OWN_ROWS[g // 2]
                     weighted = table[lo:hi, span] * wide_of(share[lo:hi, g : g + 1])
                     gate = gated(pre[OWN_AT[g] - OWN_AT[first] : OWN_AT[g + 1] - OWN_AT[first]])
@@ -346,9 +346,9 @@
             span = slice(w * TILE, (w + 1) * TILE)
             near = gated(dot(ghosts[...], weights_at(rhs, a, span)))
             far = gated(dot(ghosts[...], weights_at(rhs_other, a, span)))
-            for first in range(0, GROUPS, 2):
-                pre = dot(edges[OWN_AT[first] : OWN_AT[first + 2], :], weights_at(rhs_other, a, span)).astype(BF)
-                for g in range(first, first + 2):
+            for first in range(0, GROUPS, 4):
+                pre = dot(edges[OWN_AT[first] : OWN_AT[first + 4], :], weights_at(rhs_other, a, span)).astype(BF)
+                for g in range(first, first + 4):
                     lo, hi = GHOST_ROWS[g // 2]
                     weighted = pay_ref[lo:hi, span] * wide_of(share[lo:hi, g : g + 1])
                     rows = slice(GHOST_AT[g], GHOST_AT[g + 1])

time: 27 us -> 27.1 us (level)
  Pallas kernels: 11.1 us -> 11.5 us
  transfers between devices with their start and end apart: 1 -> 1, of which waited for: 0 -> 0; matrix products, arithmetic and copies ran while one was open for 0% -> 0% of each run, Pallas kernels for 16% -> 17%
where the time goes in v10:
time: 27.1 us; the launch traced here: 26.9 us
  blocking collectives  14.7 us (54%)
  Pallas kernels  11.5 us (42%)
  other arithmetic  0.6 us (2%)
    all_to_all x1, blocking collectives, local_step(): lax.all_to_all(copies, 'frame', split_axis=0, concat_axis=0, tiled=True)  14.7 us
    pallas_call x1, Pallas kernels, local_step(): pl.pallas_call(last_kernel, out_shape=jax.ShapeDtypeStruct((4, ATOMS), F3...  5.79 us
    pallas_call x1, Pallas kernels, local_step(): pl.pallas_call(own_kernel, out_shape=prepared, scratch_shapes=[pltpu.VMEM...  4.44 us
    pallas_call x1, Pallas kernels, local_step(): pl.pallas_call(first_kernel, out_shape=[pltpu.VMEM((CAP, PAY), BF)] + [pl...  1.22 us
    div x1, other arithmetic, local_step(): return jnp.sum(everything, axis=0) / frame_count  0.58 us
  transfers between devices with their start and end apart: 1, of which 0 were waited for; matrix products, arithmetic and copies ran while one was open for 0% of the time, Pallas kernels for 17%

profile of v10, /device:TPU:2, one launch (start us, length us, event | category | flops | bytes accessed | tf_op | source)
XLA Modules:
  0.0 26.9 jit_solution(15731563908696441752)
XLA Ops:
  0.0 1.2 %shard_map.118 = (bf16[64,640]{1,0:T(8,128)(2,1)S(1)}, bf16[128,512]{1,0:T(8,128)(2,1)S(1)}, bf16[3,128]{1,0:T(4,128)(2,1)S(1)}, f32[3,1,3]{2,1,0:T(1,128)S(1)},...) custom-call(s32[1,2,64]{2,1,0:T(2,128)} %rows_ref.1, ...), custom_call_target="tpu_custom_call" | custom-call | flops 2000000000 | bytes 2000000 | tf_op jit(solution)/shard_map/pallas_call | solution.py:427
  1.2 0.1 collective-permute-start
  1.3 0.0 copy-start
  1.3 0.0 copy-start.1
  1.3 0.0 copy-start.2
  1.4 4.4 %shard_map.119 = (f32[64,512]{1,0:T(8,128)S(1)}, bf16[192,128]{1,0:T(8,128)(2,1)S(1)}, bf16[128,512]{1,0:T(8,128)(2,1)S(1)}, bf16[800,128]{1,0:T(8,128)(2,1)S(1)...) custom-call(bf16[128,512]{1,0:T(8,128)(2,1)S(1)} %get-tuple-element.27.refs_0_, ...), custom_call_target="tpu_custom_call" | custom-call | flops 5000000000 | bytes 5000000 | tf_op jit(solution)/shard_map/pallas_call | solution.py:441
  5.8 0.0 collective-permute-done.pay_ref
  5.8 0.0 copy-done
  5.8 0.0 copy-done.1
  5.8 0.0 copy-done.2
  5.9 5.8 %shard_map.120 = f32[4,128]{1,0:T(4,128)S(1)} custom-call(bf16[64,640]{1,0:T(8,128)(2,1)S(1)} %collective-permute-done.pay_ref, f32[64,512]{1,0:T(8,128)S(1)} %get-tuple-element.40.sum_ref, bf16[192,128]{1,0:T(8,128)(2,1)S(1)} %get-tuple-element.41.total_ref, bf16[128,512]{1,0:T(8,128)(2,1)S(1)} %get-tuple-element.42.table, ...), custom_call_target="tpu_custom_call" | custom-call | flops 7000000000 | bytes 7000000 | tf_op jit(solution)/shard_map/pallas_call | solution.py:448
  11.7 14.7 %all_to_all.5 = f32[8,4,128]{2,1,0:T(4,128)S(1)} all-to-all(f32[8,4,128]{2,1,0:T(4,128)S(1)} %broadcast_in_dim.3), channel_id=1, replica_groups=mesh['dom'=32,'frame'=8] {'frame'}, dimensions={0} | all-to-all | bytes 32768 | tf_op jit(solution)/shard_map/all_to_all | solution.py:472
  26.4 0.6 %broadcast_multiply_fusion = f32[4,128]{1,0:T(4,128)} fusion(f32[4,128]{1,0:T(4,128)S(1)} %reduce_sum.9), kind=kLoop, calls=%fused_computation | loop fusion | flops 512 | bytes 4096 | tf_op jit(solution)/shard_map/div | solution.py:473
  (2 shorter events, 0.0 us)
Async XLA Ops:
  1.2 4.6 %collective-permute-start = (bf16[64,640]{1,0:T(8,128)(2,1)S(1)}, bf16[64,640]{1,0:T(8,128)(2,1)S(1)}, u32[]{:S(2)}, u32[]{:S(2)}) collective-permute-start(bf16[64,640]{1,0:T(8,128)(2,1)S(1)} %get-tuple-element.26), channel_id=1, source_target_pairs={{0,252},{1,253},{2,254},{3,255},{4,8},{5,9},{6,10},{7,11},{8,4},{9... | collective-permute-start | bytes 245768 | tf_op jit(solution)/shard_map/ppermute | solution.py:440
  1.3 4.5 %copy-start = (bf16[512,512]{1,0:T(8,128)(2,1)S(1)}, bf16[512,512]{1,0:T(8,128)(2,1)}, u32[]{:S(2)}) copy-start(bf16[512,512]{1,0:T(8,128)(2,1)} %wm_ref.1) | copy-start | bytes 1572868
  1.3 4.5 %copy-start.1 = (bf16[512,512]{1,0:T(8,128)(2,1)S(1)}, bf16[512,512]{1,0:T(8,128)(2,1)}, u32[]{:S(2)}) copy-start(bf16[512,512]{1,0:T(8,128)(2,1)} %wu_ref.1) | copy-start | bytes 1572868
  1.3 4.5 %copy-start.2 = (bf16[512,512]{1,0:T(8,128)(2,1)S(1)}, bf16[512,512]{1,0:T(8,128)(2,1)}, u32[]{:S(2)}) copy-start(bf16[512,512]{1,0:T(8,128)(2,1)} %wr_ref.1) | copy-start | bytes 1572868
